TPU v7x, 32 devices: a whole 2x2x4 slice. The times are simulated.
32 devices in a mesh: dp: 16 (over z, y, core), branch: 2 (over x).
Axes of the slice: x: 2, y: 2, z: 4, core: 2. Of those that a mesh axis runs over, the one named last changes fastest.
Arguments:
- hidden: bfloat16 [24576, 768], P('dp'), may hold values from -6 to 6
- segment_ids: int32 [48, 512], P('dp'), may hold values from 0 to 3, never falling along the last dimension, each value on 1 to 256 neighbouring positions
- query_weight: bfloat16 [768, 384], replicated, may hold values from -0.21875 to 0.21875
- query_bias: bfloat16 [384], replicated, may hold values from -3 to 3
- key_weight: bfloat16 [768, 384], replicated, may hold values from -0.21875 to 0.21875
- value_weight: bfloat16 [768, 384], replicated, may hold values from -0.21875 to 0.21875
- value_bias: bfloat16 [384], replicated, may hold values from -3 to 3
- depthwise_weight: bfloat16 [9, 768], replicated, may hold values from -2 to 2
- pointwise_weight: bfloat16 [768, 384], replicated, may hold values from -0.21875 to 0.21875
- pointwise_bias: bfloat16 [384], replicated, may hold values from -3 to 3
- kernel_weight: bfloat16 [384, 54], replicated, may hold values from -0.3125 to 0.3125
- kernel_bias: bfloat16 [54], replicated, may hold values from -4 to 4
- conv_value_weight: bfloat16 [768, 384], replicated, may hold values from -0.21875 to 0.21875
- conv_value_bias: bfloat16 [384], replicated, may hold values from -3 to 3
- output_weight: bfloat16 [768, 768], replicated, may hold values from -0.75 to 0.75
- output_bias: bfloat16 [768], replicated, may hold values from -3 to 3
- norm1_gain: bfloat16 [768], replicated, may hold values from 0.25 to 1.75
- norm1_shift: bfloat16 [768], replicated, may hold values from -3 to 3
- ffn_in_weight: bfloat16 [2, 384, 1536], replicated, may hold values from -0.3125 to 0.3125
- ffn_in_bias: bfloat16 [3072], replicated, may hold values from -3 to 3
- ffn_out_weight: bfloat16 [2, 1536, 384], replicated, may hold values from -0.15625 to 0.15625
- ffn_out_bias: bfloat16 [768], replicated, may hold values from -3 to 3
- norm2_gain: bfloat16 [768], replicated, may hold values from 0.25 to 1.75
- norm2_shift: bfloat16 [768], replicated, may hold values from -3 to 3
- cotangent: bfloat16 [24576, 768], P(('dp', 'branch')), may hold values from -6 to 6
Outputs:
- layer_out: bfloat16 [24576, 768], P(('dp', 'branch'))
- input_grad: float32 [24576, 768], P(('dp', 'branch'))
- query_weight_grad: float32 [768, 384], P(('dp', 'branch'))
- query_bias_grad: float32 [384], replicated
- key_weight_grad: float32 [768, 384], P(('dp', 'branch'))
- value_weight_grad: float32 [768, 384], P(('dp', 'branch'))
- value_bias_grad: float32 [384], replicated
- depthwise_weight_grad: float32 [9, 768], P(None, ('dp', 'branch'))
- pointwise_weight_grad: float32 [768, 384], P(('dp', 'branch'))
- pointwise_bias_grad: float32 [384], replicated
- kernel_weight_grad: float32 [384, 54], replicated
- kernel_bias_grad: float32 [54], replicated
- conv_value_weight_grad: float32 [768, 384], P(('dp', 'branch'))
- conv_value_bias_grad: float32 [384], replicated
- output_weight_grad: float32 [768, 768], P(('dp', 'branch'))
- output_bias_grad: float32 [768], replicated
- norm1_gain_grad: float32 [768], replicated
- norm1_shift_grad: float32 [768], replicated
- ffn_in_weight_grad: float32 [2, 384, 1536], P(None, None, ('dp', 'branch'))
- ffn_in_bias_grad: float32 [3072], replicated
- ffn_out_weight_grad: float32 [2, 1536, 384], P(None, ('dp', 'branch'))
- ffn_out_bias_grad: float32 [768], replicated
- norm2_gain_grad: float32 [768], replicated
- norm2_shift_grad: float32 [768], replicated
Inputs may be any that keep to these rules, and one draw needn't show every extreme that they name: `segment_ids`: within a packed row the ids never fall; a document holds at most 256 tokens.
All inputs are finite; a program needn't handle non-finite values.
Results may differ from a plain program's by a relative error of at most 0.015.
Values may be sent and summed in bfloat16 or wider, within the bound.
A program may use at most 192 MiB of HBM per device.

v0:
```python
import jax
import jax.numpy as jnp
from jax import lax
from jax.sharding import PartitionSpec as P

D = 768
HEADS = 6
HEAD_DIM = 64
KERNEL = 9


norm_eps = 1e-12
lowered = jnp.bfloat16


def matmul(first_op, second_op):
    return jnp.dot(first_op, second_op, preferred_element_type=jnp.float32)


def matmul_left(first_op, second_op):
    return lax.dot_general(
        first_op, second_op, (((0,), (0,)), ((), ())), preferred_element_type=jnp.float32
    )


def matmul_right(first_op, second_op):
    return lax.dot_general(
        first_op, second_op, (((1,), (1,)), ((), ())), preferred_element_type=jnp.float32
    )


def column_sums(values):
    return jnp.sum(values.astype(jnp.float32), axis=0)


def layer_norm(values, gain, shift):
    average = jnp.mean(values, axis=-1, keepdims=True)
    centered = values - average
    variance = jnp.mean(centered * centered, axis=-1, keepdims=True)
    return centered * lax.rsqrt(variance + norm_eps) * gain + shift


def gelu_exact(values):
    return jax.nn.gelu(values, approximate=False)


def grouped_forward(values, weight):
    groups, inner_width, outer_width = weight.shape
    pieces = values.reshape(values.shape[0], groups, inner_width)
    result = jnp.einsum("ngi,gio->ngo", pieces, weight, preferred_element_type=jnp.float32)
    return result.reshape(values.shape[0], groups * outer_width)


def grouped_input_grad(grads, weight):
    groups, inner_width, outer_width = weight.shape
    pieces = grads.reshape(grads.shape[0], groups, outer_width)
    result = jnp.einsum("ngo,gio->ngi", pieces, weight, preferred_element_type=jnp.float32)
    return result.reshape(grads.shape[0], groups * inner_width)


def tap_masks(segments):
    reach = KERNEL // 2
    length = segments.shape[1]
    padded = jnp.pad(segments, ((0, 0), (reach, reach)), constant_values=-1)
    return [(padded[:, j : j + length] == segments).astype(jnp.float32) for j in range(KERNEL)]


def spread_back(terms, length):
    reach = KERNEL // 2
    pad_spec = ((0, 0), (reach, reach)) + ((0, 0),) * (terms[0].ndim - 2)
    return sum(
        (
            jnp.pad(terms[j], pad_spec)[:, 2 * reach - j : 2 * reach - j + length]
            for j in range(KERNEL)
        )
    )


def attention_inputs(hidden, head_shape, weights):
    query_weight, query_bias, key_weight, value_weight, value_bias = weights
    queries = (matmul(hidden, query_weight) + query_bias).astype(lowered).reshape(head_shape)
    keys_low = matmul(hidden, key_weight).astype(lowered).reshape(head_shape)
    values_low = (matmul(hidden, value_weight) + value_bias).astype(lowered).reshape(head_shape)
    return (queries, keys_low, values_low)


def masked_scores(query_seq, key_seq, segment_seq):
    scores = jnp.einsum(
        "qhd,khd->hqk", query_seq, key_seq, preferred_element_type=jnp.float32
    ) * HEAD_DIM ** (-0.5)
    same_segment = segment_seq[:, None] == segment_seq[None, :]
    return jnp.where(same_segment[None], scores, -1e30)


def attention_forward(hidden, segments, weights):
    row_count, length = segments.shape
    head_shape = (row_count, length, HEADS, HEAD_DIM)
    queries, keys_low, values_low = attention_inputs(hidden, head_shape, weights)

    def per_sequence(inputs):
        query_seq, key_seq, value_seq, segment_seq = inputs
        scores = masked_scores(query_seq, key_seq, segment_seq)
        row_peak = jnp.max(scores, axis=-1, keepdims=True)
        exponent = jnp.exp(scores - row_peak)
        row_sum = jnp.sum(exponent, axis=-1, keepdims=True)
        probs_low = (exponent / row_sum).astype(lowered)
        context = jnp.einsum(
            "hqk,khd->qhd", probs_low, value_seq, preferred_element_type=jnp.float32
        )
        return (context.astype(lowered), (row_peak + jnp.log(row_sum))[..., 0])

    context, log_sums = lax.map(per_sequence, (queries, keys_low, values_low, segments))
    return (context.reshape(row_count * length, HEADS * HEAD_DIM), log_sums)


def attention_backward(hidden, segments, weights, log_sums, context_grad):
    query_weight, query_bias, key_weight, value_weight, value_bias = weights
    row_count, length = segments.shape
    token_count = row_count * length
    head_shape = (row_count, length, HEADS, HEAD_DIM)
    queries, keys_low, values_low = attention_inputs(hidden, head_shape, weights)
    scale = HEAD_DIM ** (-0.5)

    def per_sequence(inputs):
        query_seq, key_seq, value_seq, segment_seq, log_seq, grad_seq = inputs
        scores = masked_scores(query_seq, key_seq, segment_seq)
        attn_probs = jnp.exp(scores - log_seq[..., None])
        probs_low = attn_probs.astype(lowered)
        value_grad = jnp.einsum(
            "hqk,qhd->khd", probs_low, grad_seq, preferred_element_type=jnp.float32
        )
        prob_grad = jnp.einsum(
            "qhd,khd->hqk", grad_seq, value_seq, preferred_element_type=jnp.float32
        )
        score_grad = attn_probs * (
            prob_grad - jnp.sum(prob_grad * attn_probs, axis=-1, keepdims=True)
        )
        score_low = score_grad.astype(lowered)
        query_grad = (
            jnp.einsum("hqk,khd->qhd", score_low, key_seq, preferred_element_type=jnp.float32)
            * scale
        )
        key_grad = (
            jnp.einsum("hqk,qhd->khd", score_low, query_seq, preferred_element_type=jnp.float32)
            * scale
        )
        return (query_grad.astype(lowered), key_grad.astype(lowered), value_grad.astype(lowered))

    grad_heads = context_grad.reshape(head_shape)
    query_low, key_low, value_low = lax.map(
        per_sequence, (queries, keys_low, values_low, segments, log_sums, grad_heads)
    )
    width = HEADS * HEAD_DIM
    query_low = query_low.reshape(token_count, width)
    key_low = key_low.reshape(token_count, width)
    value_low = value_low.reshape(token_count, width)
    input_part = (
        matmul_right(query_low, query_weight)
        + matmul_right(key_low, key_weight)
        + matmul_right(value_low, value_weight)
    )
    zero_wide = jnp.zeros((D, width), jnp.float32)
    zero_vector = jnp.zeros((width,), jnp.float32)
    big_grads = (
        matmul_left(hidden, query_low),
        matmul_left(hidden, key_low),
        matmul_left(hidden, value_low),
        jnp.zeros((D, KERNEL), jnp.float32),
        zero_wide,
        zero_wide,
    )
    small_grads = (
        column_sums(query_low),
        column_sums(value_low),
        zero_vector,
        jnp.zeros((width, HEADS * KERNEL), jnp.float32),
        jnp.zeros((HEADS * KERNEL,), jnp.float32),
        zero_vector,
    )
    return (input_part, big_grads, small_grads)


def conv_pieces(hidden, segments, weights):
    (
        query_weight,
        query_bias,
        depthwise_weight,
        pointwise_weight,
        pointwise_bias,
        kernel_weight,
        kernel_bias,
        conv_value_weight,
        conv_value_bias,
    ) = weights
    row_count, length = segments.shape
    token_count = row_count * length
    reach = KERNEL // 2
    tap_list = tap_masks(segments)
    padded_grid = jnp.pad(hidden.reshape(row_count, length, D), ((0, 0), (reach, reach), (0, 0)))
    depthwise = sum(
        (
            depthwise_weight[j].astype(jnp.float32)
            * padded_grid[:, j : j + length]
            * tap_list[j][:, :, None]
            for j in range(KERNEL)
        )
    )
    depth_low = depthwise.reshape(token_count, D).astype(lowered)
    query_pre = matmul(hidden, query_weight) + query_bias
    key_conv = matmul(depth_low, pointwise_weight) + pointwise_bias
    conv_attn = (key_conv * query_pre).astype(lowered)
    kernel_logits = matmul(conv_attn, kernel_weight) + kernel_bias
    conv_kernel = jax.nn.softmax(kernel_logits.reshape(row_count, length, HEADS, KERNEL), axis=-1)
    conv_values = (matmul(hidden, conv_value_weight) + conv_value_bias).reshape(
        row_count, length, HEADS, HEAD_DIM
    )
    value_grid = jnp.pad(conv_values, ((0, 0), (reach, reach), (0, 0), (0, 0)))
    conv_out = sum(
        (
            conv_kernel[..., j, None]
            * value_grid[:, j : j + length]
            * tap_list[j][:, :, None, None]
            for j in range(KERNEL)
        )
    )
    return (
        tap_list,
        padded_grid,
        depth_low,
        query_pre,
        key_conv,
        conv_attn,
        conv_kernel,
        value_grid,
        conv_out,
    )


def conv_forward(hidden, segments, weights):
    row_count, length = segments.shape
    conv_out = conv_pieces(hidden, segments, weights)[-1]
    return (
        conv_out.reshape(row_count * length, HEADS * HEAD_DIM).astype(lowered),
        jnp.zeros((row_count, HEADS, length), jnp.float32),
    )


def conv_backward(hidden, segments, weights, conv_grad):
    (
        query_weight,
        query_bias,
        depthwise_weight,
        pointwise_weight,
        pointwise_bias,
        kernel_weight,
        kernel_bias,
        conv_value_weight,
        conv_value_bias,
    ) = weights
    row_count, length = segments.shape
    token_count = row_count * length
    width = HEADS * HEAD_DIM
    (
        tap_list,
        padded_grid,
        depth_low,
        query_pre,
        key_conv,
        conv_attn,
        conv_kernel,
        value_grid,
        conv_out,
    ) = conv_pieces(hidden, segments, weights)
    upstream = conv_grad.astype(jnp.float32).reshape(row_count, length, HEADS, HEAD_DIM)
    kernel_grad = jnp.stack(
        [
            jnp.sum(upstream * value_grid[:, j : j + length], axis=-1) * tap_list[j][:, :, None]
            for j in range(KERNEL)
        ],
        axis=-1,
    )
    value_terms = [
        conv_kernel[..., j, None] * tap_list[j][:, :, None, None] * upstream for j in range(KERNEL)
    ]
    conv_value_low = spread_back(value_terms, length).reshape(token_count, width).astype(lowered)
    logit_grad = conv_kernel * (
        kernel_grad - jnp.sum(kernel_grad * conv_kernel, axis=-1, keepdims=True)
    )
    logit_low = logit_grad.reshape(token_count, HEADS * KERNEL).astype(lowered)
    span_low = matmul_right(logit_low, kernel_weight).astype(lowered)
    span_full = span_low.astype(jnp.float32)
    key_conv_low = (span_full * query_pre).astype(lowered)
    query_conv_low = (span_full * key_conv).astype(lowered)
    depth_grad = matmul_right(key_conv_low, pointwise_weight).reshape(row_count, length, D)
    depthwise_grad = jnp.stack(
        [
            jnp.sum(
                padded_grid[:, j : j + length] * tap_list[j][:, :, None] * depth_grad, axis=(0, 1)
            )
            for j in range(KERNEL)
        ],
        axis=-1,
    )
    depth_terms = [
        depthwise_weight[j].astype(jnp.float32) * tap_list[j][:, :, None] * depth_grad
        for j in range(KERNEL)
    ]
    input_part = (
        matmul_right(query_conv_low, query_weight)
        + matmul_right(conv_value_low, conv_value_weight)
        + spread_back(depth_terms, length).reshape(token_count, D)
    )
    zero_wide = jnp.zeros((D, width), jnp.float32)
    big_grads = (
        matmul_left(hidden, query_conv_low),
        zero_wide,
        zero_wide,
        depthwise_grad,
        matmul_left(depth_low, key_conv_low),
        matmul_left(hidden, conv_value_low),
    )
    small_grads = (
        column_sums(query_conv_low),
        jnp.zeros((width,), jnp.float32),
        column_sums(key_conv_low),
        matmul_left(conv_attn, logit_low),
        column_sums(logit_low),
        column_sums(conv_value_low),
    )
    return (input_part, big_grads, small_grads)


def local(
    hidden,
    segment_ids,
    query_weight,
    query_bias,
    key_weight,
    value_weight,
    value_bias,
    depthwise_weight,
    pointwise_weight,
    pointwise_bias,
    kernel_weight,
    kernel_bias,
    conv_value_weight,
    conv_value_bias,
    output_weight,
    output_bias,
    norm1_gain,
    norm1_shift,
    ffn_in_weight,
    ffn_in_bias,
    ffn_out_weight,
    ffn_out_bias,
    norm2_gain,
    norm2_shift,
    cotangent,
):
    branch_index = lax.axis_index("branch")
    attend_weights = (query_weight, query_bias, key_weight, value_weight, value_bias)
    conv_weights = (
        query_weight,
        query_bias,
        depthwise_weight,
        pointwise_weight,
        pointwise_bias,
        kernel_weight,
        kernel_bias,
        conv_value_weight,
        conv_value_bias,
    )
    context, log_sums = lax.cond(
        branch_index == 0,
        lambda operands: attention_forward(operands[0], operands[1], attend_weights),
        lambda operands: conv_forward(operands[0], operands[1], conv_weights),
        (hidden, segment_ids),
    )
    joined = lax.all_to_all(context, "branch", split_axis=0, concat_axis=1, tiled=True)
    own_count = joined.shape[0]
    own_hidden = lax.dynamic_slice_in_dim(hidden, branch_index * own_count, own_count, 0)
    residual = own_hidden.astype(jnp.float32) + matmul(joined, output_weight) + output_bias
    normed, norm1_back = jax.vjp(
        layer_norm, residual, norm1_gain.astype(jnp.float32), norm1_shift.astype(jnp.float32)
    )
    normed_low = normed.astype(lowered)
    inner_act = grouped_forward(normed_low, ffn_in_weight) + ffn_in_bias
    activated, gelu_back = jax.vjp(gelu_exact, inner_act)
    active_low = activated.astype(lowered)
    summed = normed + grouped_forward(active_low, ffn_out_weight) + ffn_out_bias
    result, norm2_back = jax.vjp(
        layer_norm, summed, norm2_gain.astype(jnp.float32), norm2_shift.astype(jnp.float32)
    )
    layer_out = result.astype(lowered)
    sum_grad, gain2_grad, shift2_grad = norm2_back(cotangent.astype(jnp.float32))
    outer_low = sum_grad.astype(lowered)
    groups = ffn_in_weight.shape[0]
    active_pieces = active_low.reshape(own_count, groups, -1)
    outer_pieces = outer_low.reshape(own_count, groups, -1)
    ffn_out_grad = jnp.einsum(
        "ngi,ngo->igo", active_pieces, outer_pieces, preferred_element_type=jnp.float32
    )
    (inner_grad,) = gelu_back(grouped_input_grad(outer_low, ffn_out_weight))
    inner_low = inner_grad.astype(lowered)
    normed_pieces = normed_low.reshape(own_count, groups, -1)
    inner_pieces = inner_low.reshape(own_count, groups, -1)
    ffn_in_grad = jnp.einsum(
        "ngi,ngo->ogi", normed_pieces, inner_pieces, preferred_element_type=jnp.float32
    )
    normed_grad = sum_grad + grouped_input_grad(inner_low, ffn_in_weight)
    residual_grad, gain1_grad, shift1_grad = norm1_back(normed_grad)
    attn_low = residual_grad.astype(lowered)
    output_weight_grad = matmul_left(joined, attn_low)
    joined_grad = matmul_right(attn_low, output_weight).astype(lowered)
    context_grad = lax.all_to_all(joined_grad, "branch", split_axis=1, concat_axis=0, tiled=True)
    input_part, big_grads, branch_small = lax.cond(
        branch_index == 0,
        lambda operands: attention_backward(
            operands[0], operands[1], attend_weights, operands[2], operands[3]
        ),
        lambda operands: conv_backward(operands[0], operands[1], conv_weights, operands[3]),
        (hidden, segment_ids, log_sums, context_grad),
    )
    input_grad = (
        lax.psum_scatter(
            input_part.astype(jnp.bfloat16), "branch", scatter_dimension=0, tiled=True
        ).astype(jnp.float32)
        + residual_grad
    )
    weight_grads = big_grads + (output_weight_grad, ffn_in_grad, ffn_out_grad)
    reduced = lax.psum_scatter(weight_grads, ("dp", "branch"), scatter_dimension=0, tiled=True)
    (
        query_w_grad,
        key_w_grad,
        value_w_grad,
        depth_w_grad,
        point_w_grad,
        conv_w_grad,
        out_w_grad,
        ffn_in_w_grad,
        ffn_out_w_grad,
    ) = reduced
    small_terms = branch_small + (
        column_sums(attn_low),
        gain1_grad,
        shift1_grad,
        column_sums(inner_low),
        column_sums(outer_low),
        gain2_grad,
        shift2_grad,
    )
    smalls = lax.psum(small_terms, ("dp", "branch"))
    (
        query_b_grad,
        value_b_grad,
        point_b_grad,
        kern_w_grad,
        kern_b_grad,
        conv_b_grad,
        out_b_grad,
        gain_one,
        shift_one,
        ffn_in_b_grad,
        ffn_out_b_grad,
        gain_two,
        shift_two,
    ) = smalls
    return (
        layer_out,
        input_grad,
        query_w_grad,
        query_b_grad,
        key_w_grad,
        value_w_grad,
        value_b_grad,
        jnp.transpose(depth_w_grad),
        point_w_grad,
        point_b_grad,
        kern_w_grad,
        kern_b_grad,
        conv_w_grad,
        conv_b_grad,
        out_w_grad,
        out_b_grad,
        gain_one,
        shift_one,
        jnp.transpose(ffn_in_w_grad, (1, 2, 0)),
        ffn_in_b_grad,
        jnp.transpose(ffn_out_w_grad, (1, 0, 2)),
        ffn_out_b_grad,
        gain_two,
        shift_two,
    )


def solution(mesh):
    in_specs = (
        P("dp", None),
        P("dp", None),
        P(),
        P(),
        P(),
        P(),
        P(),
        P(),
        P(),
        P(),
        P(),
        P(),
        P(),
        P(),
        P(),
        P(),
        P(),
        P(),
        P(),
        P(),
        P(),
        P(),
        P(),
        P(),
        P(("dp", "branch"), None),
    )
    out_specs = (
        P(("dp", "branch"), None),
        P(("dp", "branch"), None),
        P(("dp", "branch"), None),
        P(),
        P(("dp", "branch"), None),
        P(("dp", "branch"), None),
        P(),
        P(None, ("dp", "branch")),
        P(("dp", "branch"), None),
        P(),
        P(),
        P(),
        P(("dp", "branch"), None),
        P(),
        P(("dp", "branch"), None),
        P(),
        P(),
        P(),
        P(None, None, ("dp", "branch")),
        P(),
        P(None, ("dp", "branch"), None),
        P(),
        P(),
        P(),
    )
    return jax.shard_map(local, mesh=mesh, in_specs=in_specs, out_specs=out_specs, check_vma=False)
```

profile of v0, /device:TPU:0, one launch (start us, length us, event | category | flops | bytes accessed | tf_op | source)
XLA Modules:
  0.0 1150.9 jit_solution(13357889554204640990)
XLA Ops:
  8.0 68.1 %conditional.2 = (f32[3,6,512]{2,1,0:T(8,128)}, bf16[3,512,6,64]{1,0,3,2:T(4,128)(2,1)}) conditional(s32[]{:T(128)} %convert_element_type.563, (bf16[9,768]{1,0:T(8,128)(2,1)}, bf16[1536,768]{1,0:T(8,128)(2,1)}, s32[3,512]{1,0:T(4,128)}, bf16[768,384]{1,0:T(8,128)(2,1)}, bf16[384]{0:T(512)(128)(2,1)}, /*index=5*/bf16[768,384]{1,0:T(8,128)(2,1)}, ...), branch_computations={%region_0.3_spmd, %region_3.8_spmd} | conditional | flops 3142842112 | bytes 64671504 | solution.py:373
  28.1 4.7 reshape.600
  37.2 4.7 reshape.601
  46.2 26.3 %while.24 = (s32[]{:T(128)}, bf16[3,512,6,64]{1,3,2,0:T(8,128)(2,1)}, f32[3,6,512]{2,1,0:T(8,128)}, bf16[3,512,6,64]{1,3,2,0:T(8,128)(2,1)}, s32[3,512]{1,0:T(4,...) while((s32[]{:T(128)}, bf16[3,512,6,64]{1,3,2,0:T(8,128)(2,1)}, ...), condition=%wide.region_7.7_spmd, body=%wide.region_4.6_spmd.sunk | while | flops 421983232 | bytes 21606500 | solution.py:112
  81.3 21.3 %all-to-all-start = ((bf16[2,768,384]{1,2,0:T(8,128)(2,1)}), bf16[2,768,384]{1,2,0:T(8,128)(2,1)}, u32[]{:S(2)}, u32[]{:S(2)}) async-start(bf16[2,768,384]{1,2,0:T(8,128)(2,1)} %copy.169), calls=%async_computation | async-start | bytes 2359296 | tf_op jit(solution)/shard_map/all_to_all | solution.py:379
  111.5 7.9 all-to-all-done
  123.4 25.2 %fusion.220 = (bf16[768,2,1536]{2,0,1:T(8,128)(2,1)S(1)}, f32[768,2,1536]{2,0,1:T(8,128)}, f32[2,768,1536]{2,1,0:T(8,128)}) fusion(f32[2,1536]{1,0:T(2,128)S(1)} %copy-done.73, bf16[768,2,384]{0,2,1:T(8,128)(2,1)S(1)} %bitcast.467, bf16[2,384,1536]{2,1,0:T(8,128)(2,1)S(1)} %copy-done), kind=kOutput, calls=%fused_computation.403 | convolution fusion | flops 1967652864 | bytes 27144192 | tf_op jit(solution)/shard_map/ngi,gio->ngo/dot_general | solution.py:50
  156.5 10.9 convert_reduce_fusion.24
  180.2 4.5 all-to-all-start.1
  184.8 6.6 convolution_bitcast_fusion.5
  191.4 8.3 copy.181
  202.2 113.4 %conditional.3 = (bf16[1536,768]{1,0:T(8,128)(2,1)}, f32[768,384]{0,1:T(8,128)}, f32[768,384]{1,0:T(8,128)}, f32[768,384]{1,0:T(8,128)}, f32[768,9]{0,1:T(8,128)...) conditional(s32[]{:T(128)} %convert_element_type.563, ...), branch_computations={%region_16.42_spmd, %region_42.48_spmd} | conditional | flops 9194042368 | bytes 389707072 | solution.py:416
  232.5 4.7 reshape.605
  241.6 43.1 %while.25 = (s32[]{:T(128)}, bf16[3,512,6,64]{1,3,2,0:T(8,128)(2,1)}, bf16[3,512,6,64]{1,3,2,0:T(8,128)(2,1)}, bf16[3,512,6,64]{1,3,2,0:T(8,128)(2,1)}, bf16[3,5...) while((s32[]{:T(128)}, ...), condition=%wide.region_45.45_spmd, body=%wide.region_43.44_spmd.sunk | while | flops 1031468032 | bytes 66428112 | solution.py:150
  315.6 4.6 copy.176
  329.7 7.9 convolution_bitcast_fusion.6
  340.4 101.0 %all-reduce.29 = (f32[384]{0:T(512)}, f32[384]{0:T(512)}, f32[768,9]{0,1:T(8,128)S(1)}, f32[384]{0:T(512)}, f32[54]{0:T(128)}, /*index=5*/f32[384]{0:T(512)}, f3...) all-reduce(f32[384]{0:T(512)S(1)} %copy-done.74, ...), channel_id=1, replica_groups=mesh['dp'=16,'branch'=2] {'dp','branch'}, use_global_device_ids=true, to_apply=%region_50.51 | all-reduce | flops 16182 | bytes 129456 | tf_op jit(solution)/shard_map/psum | solution.py:452
  442.1 100.1 %all-reduce.33.cloned.1.call-done = (f32[384,54]{0,1:T(8,128)}, f32[1536,2,384]{2,1,0:T(2,128)}) async-done(((f32[384,54]{0,1:T(8,128)}, f32[1536,2,384]{2,1,0:T(2,128)}), (f32[384,54]{0,1:T(8,128)}, f32[1536,2,384]{2,1,0:T(2,128)})) %all-reduce.33.cloned.1.call-update) | async-done | bytes 4801552 | tf_op jit(solution)/shard_map/psum | solution.py:452
  550.8 69.4 %reduce-scatter.30.cloned.1.call-done = f32[24,384]{1,0:T(8,128)} async-done(((f32[768,384]{1,0:T(8,128)}), f32[24,384]{1,0:T(8,128)}) %reduce-scatter.30.cloned.1.call-update) | async-done | bytes 36880
  620.2 101.8 %reduce-scatter.32.cloned.1.call-done = f32[24,384]{1,0:T(8,128)} async-done(((f32[768,384]{1,0:T(8,128)}), f32[24,384]{1,0:T(8,128)}) %reduce-scatter.32.cloned.1.call-update) | async-done | bytes 36880
  722.0 101.8 %reduce-scatter.34.cloned.1.call-done = f32[24,384]{1,0:T(8,128)} async-done(((f32[768,384]{1,0:T(8,128)}), f32[24,384]{1,0:T(8,128)}) %reduce-scatter.34.cloned.1.call-update) | async-done | bytes 36880
  823.8 101.8 %reduce-scatter.26.cloned.1.call-done = f32[24,384]{1,0:T(8,128)} async-done(((f32[768,384]{1,0:T(8,128)}), f32[24,384]{1,0:T(8,128)}) %reduce-scatter.26.cloned.1.call-update) | async-done | bytes 36880
  925.6 104.5 %reduce-scatter.22.cloned.1.call-done = f32[24,768]{1,0:T(8,128)} async-done(((f32[768,768]{1,0:T(8,128)}), f32[24,768]{1,0:T(8,128)}) %reduce-scatter.22.cloned.1.call-update) | async-done | bytes 73744 | tf_op jit(solution)/shard_map/reduce_scatter | solution.py:431
  1030.0 112.6 %reduce-scatter.24.cloned.1.call-done = f32[48,2,384]{2,0,1:T(8,128)} async-done(((f32[1536,2,384]{2,0,1:T(8,128)}), f32[48,2,384]{2,0,1:T(8,128)}) %reduce-scatter.24.cloned.1.call-update) | async-done | bytes 147472 | tf_op jit(solution)/shard_map/reduce_scatter | solution.py:431
  (298 shorter events, 222.3 us)
Async XLA Ops:
  8.0 115.4 %copy-start = (bf16[2,384,1536]{2,1,0:T(8,128)(2,1)S(1)}, bf16[2,384,1536]{2,1,0:T(8,128)(2,1)}, u32[]{:S(2)}) copy-start(bf16[2,384,1536]{2,1,0:T(8,128)(2,1)} %param.51) | copy-start | bytes 7077892
  76.2 26.4 %copy-start.79 = (bf16[768]{0:T(1024)(128)(2,1)S(1)}, bf16[768]{0:T(1024)(128)(2,1)}, u32[]{:S(2)}) copy-start(bf16[768]{0:T(1024)(128)(2,1)} %param.49) | copy-start | bytes 4612
  76.2 26.4 %copy-start.80 = (bf16[768]{0:T(1024)(128)(2,1)S(1)}, bf16[768]{0:T(1024)(128)(2,1)}, u32[]{:S(2)}) copy-start(bf16[768]{0:T(1024)(128)(2,1)} %param.55) | copy-start | bytes 4612
  76.2 26.4 %copy-start.81 = (bf16[768]{0:T(1024)(128)(2,1)S(1)}, bf16[768]{0:T(1024)(128)(2,1)}, u32[]{:S(2)}) copy-start(bf16[768]{0:T(1024)(128)(2,1)} %param.50) | copy-start | bytes 4612
  81.3 38.1 %all-to-all-start = ((bf16[2,768,384]{1,2,0:T(8,128)(2,1)}), bf16[2,768,384]{1,2,0:T(8,128)(2,1)}, u32[]{:S(2)}, u32[]{:S(2)}) async-start(bf16[2,768,384]{1,2,0:T(8,128)(2,1)} %copy.169), calls=%async_computation | async-start | bytes 2359296 | tf_op jit(solution)/shard_map/all_to_all | solution.py:379
  123.4 25.2 %copy-start.36 = (bf16[768,768]{0,1:T(8,128)(2,1)}, bf16[768,768]{0,1:T(8,128)(2,1)S(1)}, u32[]{:S(2)}) copy-start(bf16[768,768]{0,1:T(8,128)(2,1)S(1)} %fusion.238) | copy-start | bytes 3538948
  123.4 25.2 %copy-start.82 = (bf16[2,1536,384]{2,1,0:T(8,128)(2,1)S(1)}, bf16[2,1536,384]{2,1,0:T(8,128)(2,1)}, u32[]{:S(2)}) copy-start(bf16[2,1536,384]{2,1,0:T(8,128)(2,1)} %param.53) | copy-start | bytes 7077892
  156.5 10.9 copy-start.40
  180.2 19.5 %all-to-all-start.1 = ((bf16[768,2,384]{0,2,1:T(8,128)(2,1)}), bf16[768,2,384]{0,2,1:T(8,128)(2,1)}, u32[]{:S(2)}, u32[]{:S(2)}) async-start(bf16[768,2,384]{0,2,1:T(8,128)(2,1)} %bitcast.68), calls=%async_computation.1 | async-start | bytes 2359296 | tf_op jit(solution)/shard_map/all_to_all | solution.py:415
  184.7 357.5 %all-reduce.33.cloned.1.call-start = ((), (), s32[]{:S(2)}) async-start(), calls=%async_computation.18 | async-start | bytes 9609216 | tf_op jit(solution)/shard_map/psum | solution.py:452
  191.3 10.8 copy-start.58
  191.3 10.8 copy-start.70
  191.4 10.8 copy-start.76
  315.6 228.2 %reduce-scatter.20.cloned.1.call-start = ((), (), s32[]{:S(2)}) async-start(), calls=%async_computation.10 | async-start | bytes 3538944 | tf_op jit(solution)/shard_map/reduce_scatter | solution.py:425
  320.3 230.4 %reduce-scatter.28.cloned.1.call-start = ((), (), s32[]{:S(2)}) async-start(), calls=%async_computation.14 | async-start | bytes 1216512
  320.9 299.3 %reduce-scatter.30.cloned.1.call-start = ((), (), s32[]{:S(2)}) async-start(), calls=%async_computation.15 | async-start | bytes 1216512
  321.5 400.5 %reduce-scatter.32.cloned.1.call-start = ((), (), s32[]{:S(2)}) async-start(), calls=%async_computation.16 | async-start | bytes 1216512
  322.2 501.5 %reduce-scatter.34.cloned.1.call-start = ((), (), s32[]{:S(2)}) async-start(), calls=%async_computation.17 | async-start | bytes 1216512
  323.0 602.6 %reduce-scatter.26.cloned.1.call-start = ((), (), s32[]{:S(2)}) async-start(), calls=%async_computation.13 | async-start | bytes 1216512
  325.7 704.3 %reduce-scatter.22.cloned.1.call-start = ((), (), s32[]{:S(2)}) async-start(), calls=%async_computation.11 | async-start | bytes 2433024 | tf_op jit(solution)/shard_map/reduce_scatter | solution.py:431
  329.7 813.0 %reduce-scatter.24.cloned.1.call-start = ((), (), s32[]{:S(2)}) async-start(), calls=%async_computation.12 | async-start | bytes 4866048 | tf_op jit(solution)/shard_map/reduce_scatter | solution.py:431
  337.7 206.1 %copy-start.61 = (f32[768]{0:T(1024)S(1)}, f32[768]{0:T(1024)}, u32[]{:S(2)}) copy-start(f32[768]{0:T(1024)} %copy-done.60) | copy-start | bytes 9220
  543.8 599.5 %copy-start.1 = (bf16[2,384,1536]{2,1,0:T(8,128)(2,1)S(1)}, bf16[2,384,1536]{2,1,0:T(8,128)(2,1)}, u32[]{:S(2)}) copy-start(bf16[2,384,1536]{2,1,0:T(8,128)(2,1)} %param.51) | copy-start | bytes 7077892
  547.7 595.0 %copy-start.59 = (f32[384,54]{0,1:T(8,128)S(1)}, f32[384,54]{0,1:T(8,128)}, u32[]{:S(2)}) copy-start(f32[384,54]{0,1:T(8,128)} %get-tuple-element.895) | copy-start | bytes 248836
  (56 other events, 205.9 us)
Sparse Core Ops, SparseCore 0:
  315.7 226.4 all-reduce.32
Sparse Core Ops, SparseCore 1:
  320.4 95.0 reduce-scatter.19
  421.0 97.2 reduce-scatter.27
  523.9 96.3 reduce-scatter.29
  625.9 96.0 reduce-scatter.31
  727.7 96.0 reduce-scatter.33
  829.4 96.1 reduce-scatter.25
  931.3 98.7 reduce-scatter.21
  1036.0 106.6 reduce-scatter.23
where the time goes:
time: 1160 us; the launch traced here: 1150 us
  waiting for transfers between devices  702 us (61%)
  matrix products  145 us (12%)
  local copies, waits for them, and re-layouts  116 us (10%)
  blocking collectives  101 us (9%)
  other arithmetic  35.8 us (3%)
  starting transfers between devices  26.1 us (2%)
  between operations  16.4 us (1%)
    unnamed x14, waiting for transfers between devices  377 us
    reduce_scatter x2, waiting for transfers between devices, local(): lax.psum_scatter(weight_grads, ('dp', 'branch'), scatter_dimension=0, til...  217 us
    psum x1, blocking collectives, local(): smalls = lax.psum(small_terms, ('dp', 'branch'))  101 us
    psum x1, waiting for transfers between devices, local(): smalls = lax.psum(small_terms, ('dp', 'branch'))  100 us
    dot_general x2, matrix products, grouped_forward(): jnp.einsum('ngi,gio->ngo', pieces, weight, preferred_element_type=jnp.flo...  27.4 us
  transfers between devices with their start and end apart: 11, of which 8 were waited for; matrix products, arithmetic and copies ran while one was open for 5% of the time, Pallas kernels for 0%

commit v1 on v0

--- a/solution.py
+++ b/solution.py
@@ -1,7 +1,177 @@
+import functools
+import math
+
 import jax
 import jax.numpy as jnp
 from jax import lax
+from jax.experimental import pallas as pl
+from jax.experimental.pallas import tpu as pltpu
 from jax.sharding import PartitionSpec as P
+
+MESH = pl.DeviceIdType.MESH
+CHUNK = 48
+
+def comm_plan(dp_size):
+    bits = int(math.log2(dp_size)) + 1
+    extra = max(0, bits - 5)
+    return bits, extra
+
+def orders(bits, extra):
+    halving = list(range(extra, bits))
+    first = [1] if 1 in halving else []
+    rest = [b for b in halving if b not in first]
+    if len(rest) >= 4:
+        a = [rest[0], rest[2], rest[1]] + rest[3:]
+        b = [rest[1], rest[2], rest[0]] + rest[3:]
+    else:
+        a, b = rest, rest[::-1]
+    ex = list(range(extra))
+    return (first + a), (first + b), ex
+
+def comm_kernel(dp_size, rows, g_ref, s_ref, out_ref, sout_ref, rb, srb, erb, send, recv, ssend, srecv, esend, erecv):
+    bits, extra = comm_plan(dp_size)
+    order_a, order_b, ex = orders(bits, extra)
+    nh = len(order_a)
+    dp = lax.axis_index("dp")
+    br = lax.axis_index("branch")
+    my = [br] + [lax.rem(lax.div(dp, 1 << (k - 1)), 2) for k in range(1, bits)]
+
+    def partner(k):
+        if k == 0:
+            return (dp, 1 - br)
+        return (dp + (1 << (k - 1)) * (1 - 2 * my[k]), br)
+
+    barrier = pltpu.get_barrier_semaphore()
+    for k in range(bits):
+        pl.semaphore_signal(barrier, inc=1, device_id=partner(k), device_id_type=MESH)
+    pl.semaphore_wait(barrier, bits)
+
+    n_chunks = rows // CHUNK
+
+    def axis_of(k):
+        return bits - 1 - k
+
+    pending = {}
+
+    def start(c, s, order):
+        fixed = {k: my[k] for k in order[:s]}
+        k = order[s]
+        fixed[k] = 1 - my[k]
+        left = nh - 1 - s
+        off = sum(1 << (nh - 1 - t) for t in range(s))
+        free = [i for i in range(nh) if (bits - 1 - i) not in fixed]
+        copies = []
+        total = 1 << left
+        for u in range(total):
+            idx = []
+            pos = 0
+            for i in range(nh):
+                kk = bits - 1 - i
+                if kk in fixed:
+                    idx.append(fixed[kk])
+                else:
+                    idx.append((u >> (left - 1 - pos)) & 1)
+                    pos += 1
+            cp = pltpu.make_async_remote_copy(
+                src_ref=g_ref.at[tuple(idx) + (pl.ds(c * CHUNK, CHUNK),)],
+                dst_ref=rb.at[c, off + u],
+                send_sem=send.at[c, s], recv_sem=recv.at[c, s],
+                device_id=partner(k), device_id_type=MESH)
+            cp.start()
+        whole = pltpu.make_async_remote_copy(
+            src_ref=rb.at[c, pl.ds(off, total)], dst_ref=rb.at[c, pl.ds(off, total)],
+            send_sem=send.at[c, s], recv_sem=recv.at[c, s],
+            device_id=partner(k), device_id_type=MESH)
+        pending[(c, s)] = whole
+
+    def add(c, s, order):
+        pending[(c, s)].wait_recv()
+        left = nh - 1 - s
+        off = sum(1 << (nh - 1 - t) for t in range(s))
+        fixed = {k: my[k] for k in order[:s + 1]}
+        for u in range(1 << left):
+            idx = []
+            pos = 0
+            for i in range(nh):
+                kk = bits - 1 - i
+                if kk in fixed:
+                    idx.append(fixed[kk])
+                else:
+                    idx.append((u >> (left - 1 - pos)) & 1)
+                    pos += 1
+            at = tuple(idx) + (pl.ds(c * CHUNK, CHUNK),)
+            tot = g_ref[at].astype(jnp.float32) + rb[c, off + u].astype(jnp.float32)
+            if s == nh - 1:
+                out_ref[pl.ds(c * CHUNK, CHUNK), :] = tot
+            else:
+                g_ref[at] = tot.astype(g_ref.dtype)
+
+    def small_start(s, k):
+        cp = pltpu.make_async_remote_copy(
+            src_ref=sout_ref, dst_ref=srb.at[s], send_sem=ssend.at[s], recv_sem=srecv.at[s],
+            device_id=partner(k), device_id_type=MESH)
+        cp.start()
+        pending[("s", s)] = cp
+
+    sout_ref[...] = s_ref[...]
+    small_order = order_a + ex
+    half = n_chunks // 2
+    for w in range(half + nh):
+        for p in range(half - 1, -1, -1):
+            s = w - p
+            for col, order in ((0, order_a), (1, order_b)):
+                c = 2 * p + col
+                if 1 <= s <= nh:
+                    add(c, s - 1, order)
+                if 0 <= s < nh:
+                    start(c, s, order)
+        if w >= 1 and w <= bits:
+            pending[("s", w - 1)].wait()
+            sout_ref[...] = sout_ref[...] + srb[w - 1]
+        if w < bits:
+            small_start(w, small_order[w])
+    for w in range(half + nh, bits + 1):
+        pending[("s", w - 1)].wait()
+        sout_ref[...] = sout_ref[...] + srb[w - 1]
+        if w < bits:
+            small_start(w, small_order[w])
+    for i, k in enumerate(ex):
+        cp = pltpu.make_async_remote_copy(
+            src_ref=out_ref, dst_ref=erb.at[i], send_sem=esend.at[i], recv_sem=erecv.at[i],
+            device_id=partner(k), device_id_type=MESH)
+        cp.start()
+        cp.wait()
+        out_ref[...] = out_ref[...] + erb[i]
+    for c in range(n_chunks):
+        for s in range(nh):
+            pending[(c, s)].wait_send()
+
+def comm_call(dp_size, g, s):
+    bits, extra = comm_plan(dp_size)
+    nh = bits - extra
+    rows = g.shape[-2]
+    n_chunks = rows // CHUNK
+    gg = g.reshape((2,) * nh + g.shape[-2:])
+    vm = pl.BlockSpec(memory_space=pltpu.VMEM)
+    return pl.pallas_call(
+        functools.partial(comm_kernel, dp_size, rows),
+        out_shape=(jax.ShapeDtypeStruct((rows, g.shape[-1]), jnp.float32),
+                   jax.ShapeDtypeStruct(s.shape, jnp.float32)),
+        in_specs=[vm, vm], out_specs=(vm, vm),
+        scratch_shapes=[
+            pltpu.VMEM((n_chunks, (1 << nh) - 1, CHUNK, g.shape[-1]), jnp.bfloat16),
+            pltpu.VMEM((bits,) + s.shape, jnp.float32),
+            pltpu.VMEM((max(extra, 1), rows if extra else 8, g.shape[-1]), jnp.float32),
+            pltpu.SemaphoreType.DMA((n_chunks, nh)),
+            pltpu.SemaphoreType.DMA((n_chunks, nh)),
+            pltpu.SemaphoreType.DMA((bits,)),
+            pltpu.SemaphoreType.DMA((bits,)),
+            pltpu.SemaphoreType.DMA((max(extra, 1),)),
+            pltpu.SemaphoreType.DMA((max(extra, 1),)),
+        ],
+        compiler_params=pltpu.CompilerParams(collective_id=0, has_side_effects=True, vmem_limit_bytes=60 << 20),
+        name="grad_reduce",
+    )(gg, s)
 
 D = 768
 HEADS = 6
@@ -427,19 +597,18 @@
         ).astype(jnp.float32)
         + residual_grad
     )
-    weight_grads = big_grads + (output_weight_grad, ffn_in_grad, ffn_out_grad)
-    reduced = lax.psum_scatter(weight_grads, ("dp", "branch"), scatter_dimension=0, tiled=True)
-    (
-        query_w_grad,
-        key_w_grad,
-        value_w_grad,
-        depth_w_grad,
-        point_w_grad,
-        conv_w_grad,
-        out_w_grad,
-        ffn_in_w_grad,
-        ffn_out_w_grad,
-    ) = reduced
+    dp_size = lax.axis_size("dp")
+    units = 32
+    q_g, k_g, v_g, depth_g, p_g, cv_g = big_grads
+    unit_parts = [
+        jnp.transpose(ffn_out_grad.reshape(units, -1, groups, D // groups), (0, 2, 1, 3)).reshape(units, -1, 384),
+        jnp.transpose(ffn_in_grad.reshape(units, -1, groups, D // groups), (0, 2, 1, 3)).reshape(units, -1, 384),
+        output_weight_grad[:, :384].reshape(units, -1, 384),
+        output_weight_grad[:, 384:].reshape(units, -1, 384),
+    ] + [x.reshape(units, -1, 384) for x in (q_g, k_g, v_g, p_g, cv_g)] + [
+        jnp.pad(depth_g, ((0, 0), (0, 384 - KERNEL))).reshape(units, -1, 384)
+    ]
+    packed = jnp.concatenate([x.astype(lowered) for x in unit_parts], axis=1)
     small_terms = branch_small + (
         column_sums(attn_low),
         gain1_grad,
@@ -449,7 +618,30 @@
         gain2_grad,
         shift2_grad,
     )
-    smalls = lax.psum(small_terms, ("dp", "branch"))
+    flat = [jnp.transpose(x).reshape(-1) for x in small_terms]
+    sizes = [x.shape[0] for x in flat]
+    total = sum(sizes)
+    small = jnp.pad(jnp.concatenate(flat), (0, 96 * 384 - total)).reshape(96, 384)
+    out_sum, small_sum = comm_call(dp_size, packed, small)
+    device = lax.axis_index("dp") * 2 + branch_index
+    share = 2 * dp_size // units
+
+    def piece(start, rows):
+        n = rows // share
+        return lax.dynamic_slice_in_dim(out_sum, start + lax.rem(device, share) * n, n, 0)
+
+    ffn_out_w_grad = jnp.stack([piece(0, 48), piece(48, 48)])
+    ffn_in_w_grad = jnp.stack([piece(96, 48), piece(144, 48)])
+    out_w_grad = jnp.concatenate([piece(192, 24), piece(216, 24)], axis=1)
+    query_w_grad, key_w_grad, value_w_grad, point_w_grad, conv_w_grad = [
+        piece(240 + 24 * i, 24) for i in range(5)
+    ]
+    depth_w_grad = piece(360, 24)[:, :KERNEL]
+    small_flat = small_sum.reshape(-1)
+    parts, at = [], 0
+    for n in sizes:
+        parts.append(small_flat[at : at + n])
+        at += n
     (
         query_b_grad,
         value_b_grad,
@@ -464,7 +656,8 @@
         ffn_out_b_grad,
         gain_two,
         shift_two,
-    ) = smalls
+    ) = parts
+    kern_w_grad = jnp.transpose(kern_w_grad.reshape(HEADS * KERNEL, HEADS * HEAD_DIM))
     return (
         layer_out,
         input_grad,
@@ -484,9 +677,9 @@
         out_b_grad,
         gain_one,
         shift_one,
-        jnp.transpose(ffn_in_w_grad, (1, 2, 0)),
+        jnp.transpose(ffn_in_w_grad, (0, 2, 1)),
         ffn_in_b_grad,
-        jnp.transpose(ffn_out_w_grad, (1, 0, 2)),
+        ffn_out_w_grad,
         ffn_out_b_grad,
         gain_two,
         shift_two,

time: 1160 us -> 515 us (0.44)
  waiting for transfers between devices: 702 us -> 7.9 us
  Pallas kernels: 0 us -> 120 us
  blocking collectives: 101 us -> 17.4 us
  local copies, waits for them, and re-layouts: 116 us -> 138 us
    unnamed x14 -> x1, waiting for transfers between devices: 377 us -> 0.02 us
    reduce_scatter x2 -> x0, waiting for transfers between devices: 217 us -> none  [local(): lax.psum_scatter(weight_grads, ('dp', 'branch'), scatter_dimension=0, til...]
    pallas_call x0 -> x1, Pallas kernels: none -> 120 us  [comm_call(): pl.pallas_call(functools.partial(comm_kernel, dp_size, rows), out_shape=(...]
    psum x1 -> x0, blocking collectives: 101 us -> none  [local(): smalls = lax.psum(small_terms, ('dp', 'branch'))]
    psum x1 -> x0, waiting for transfers between devices: 100 us -> none  [local(): smalls = lax.psum(small_terms, ('dp', 'branch'))]
    all_to_all x0 -> x1, blocking collectives: none -> 17.4 us  [local(): lax.all_to_all(joined_grad, 'branch', split_axis=1, concat_axis=0, tiled=...]
    unnamed x90 -> x96, local copies, waits for them, and re-layouts: 13.6 us -> 26.8 us
    convert_element_type x0 -> x6, local copies, waits for them, and re-layouts: none -> 12.4 us  [local(): packed = jnp.concatenate([x.astype(lowered) for x in unit_parts], axis=1)]
  transfers between devices with their start and end apart: 11 -> 2, of which waited for: 8 -> 1; matrix products, arithmetic and copies ran while one was open for 5% -> 11% of each run, Pallas kernels for 0% -> 24%
where the time goes in v1:
time: 515 us; the launch traced here: 506 us
  matrix products  140 us (27%)
  local copies, waits for them, and re-layouts  138 us (27%)
  Pallas kernels  120 us (23%)
  other arithmetic  37.8 us (7%)
  starting transfers between devices  21.2 us (4%)
  blocking collectives  17.4 us (3%)
  between operations  14.9 us (3%)
  loops' own time  8.34 us (2%)
  waiting for transfers between devices  7.9 us (2%)
    pallas_call x1, Pallas kernels, comm_call(): pl.pallas_call(functools.partial(comm_kernel, dp_size, rows), out_shape=(...  120 us
    dot_general x2, matrix products, grouped_forward(): jnp.einsum('ngi,gio->ngo', pieces, weight, preferred_element_type=jnp.flo...  27.4 us
    unnamed x96, local copies, waits for them, and re-layouts  26.8 us
    all_to_all x1, starting transfers between devices, local(): lax.all_to_all(context, 'branch', split_axis=0, concat_axis=1, tiled=True)  21.2 us
    dot_general x7, matrix products, matmul(): return jnp.dot(first_op, second_op, preferred_element_type=jnp.float32)  20.9 us
    all_to_all x1, blocking collectives, local(): lax.all_to_all(joined_grad, 'branch', split_axis=1, concat_axis=0, tiled=...  17.4 us
    while x7, local copies, waits for them, and re-layouts, attention_backward(): lax.map(per_sequence, (queries, keys_low, values_low, segments, log_sums,...  16 us
    dot_general x2, matrix products, grouped_input_grad(): jnp.einsum('ngo,gio->ngi', pieces, weight, preferred_element_type=jnp.flo...  12.8 us
  transfers between devices with their start and end apart: 2, of which 1 were waited for; matrix products, arithmetic and copies ran while one was open for 11% of the time, Pallas kernels for 24%

profile of v1, /device:TPU:0, one launch (start us, length us, event | category | flops | bytes accessed | tf_op | source)
XLA Modules:
  0.0 505.6 jit_solution(7540239105040437964)
XLA Ops:
  7.2 68.3 %conditional.4 = (f32[3,6,512]{2,1,0:T(8,128)}, bf16[3,512,6,64]{1,0,3,2:T(4,128)(2,1)}) conditional(s32[]{:T(128)} %convert_element_type.671, (bf16[9,768]{1,0:T(8,128)(2,1)}, bf16[1536,768]{1,0:T(8,128)(2,1)}, s32[3,512]{1,0:T(4,128)}, bf16[768,384]{1,0:T(8,128)(2,1)}, bf16[384]{0:T(512)(128)(2,1)}, /*index=5*/bf16[768,384]{1,0:T(8,128)(2,1)}, ...), branch_computations={%region_0.3_spmd, %region_3.8_spmd} | conditional | flops 3142842112 | bytes 64671504 | solution.py:543
  12.1 4.3 fusion.18
  27.5 4.7 reshape.687
  32.2 4.4 copy.201
  36.6 4.7 reshape.688
  41.2 4.4 copy.202
  45.6 26.3 %while.24 = (s32[]{:T(128)}, bf16[3,512,6,64]{1,3,2,0:T(8,128)(2,1)}, f32[3,6,512]{2,1,0:T(8,128)}, bf16[3,512,6,64]{1,3,2,0:T(8,128)(2,1)}, s32[3,512]{1,0:T(4,...) while((s32[]{:T(128)}, bf16[3,512,6,64]{1,3,2,0:T(8,128)(2,1)}, ...), condition=%wide.region_7.7_spmd, body=%wide.region_4.6_spmd.sunk | while | flops 421983232 | bytes 21606500 | solution.py:282
  67.6 3.7 fusion.372
  75.5 4.0 all_to_all.28
  80.6 21.2 %all-to-all-start = ((bf16[2,768,384]{1,2,0:T(8,128)(2,1)}), bf16[2,768,384]{1,2,0:T(8,128)(2,1)}, u32[]{:S(2)}, u32[]{:S(2)}) async-start(bf16[2,768,384]{1,2,0:T(8,128)(2,1)} %copy.228), calls=%async_computation | async-start | bytes 2359296 | tf_op jit(solution)/shard_map/all_to_all | solution.py:549
  110.8 7.9 %all-to-all-done = bf16[2,768,384]{1,2,0:T(8,128)(2,1)} async-done(((bf16[2,768,384]{1,2,0:T(8,128)(2,1)}), bf16[2,768,384]{1,2,0:T(8,128)(2,1)}, u32[]{:S(2)}, u32[]{:S(2)}) %all-to-all-start) | async-done | bytes 1179680 | tf_op jit(solution)/shard_map/all_to_all | solution.py:549
  122.7 25.2 %fusion.226 = (bf16[768,2,1536]{2,0,1:T(8,128)(2,1)S(1)}, f32[768,2,1536]{2,0,1:T(8,128)}, f32[2,768,1536]{2,1,0:T(8,128)}) fusion(f32[2,1536]{1,0:T(2,128)S(1)} %copy-done.111, bf16[768,2,384]{0,2,1:T(8,128)(2,1)S(1)} %bitcast.509, bf16[2,384,1536]{2,1,0:T(8,128)(2,1)S(1)} %copy-done), kind=kOutput, calls=%fused_computation.410 | convolution fusion | flops 1967652864 | bytes 27144192 | tf_op jit(solution)/shard_map/ngi,gio->ngo/dot_general | solution.py:220
  155.8 10.8 %convert_reduce_fusion.24 = (f32[2,1536]{1,0:T(2,128)}, bf16[768,2,1536]{2,0,1:T(8,128)(2,1)S(1)}) fusion(f32[768,2,1536]{2,0,1:T(8,128)} %get-tuple-element.682, bf16[768,2,384]{0,2,1:T(8,128)(2,1)S(1)} %bitcast.512, bf16[2,1536,384]{2,1,0:T(8,128)(2,1)S(1)} %copy-done.122, f32[2,768,1536]{2,1,0:T(8,128)} %get-tuple-element.769, f32[2,1536]{1,0:T(2,128)S(1)} %copy-done.111), kind=kOutput, calls=%fused_computation.411 | convolution fusion | flops 1852044288 | bytes 27156480 | tf_op jit(solution)/shard_map/ngo,gio->ngi/dot_general | solution.py:227
  170.7 3.7 multiply_reduce_fusion.4
  178.5 17.4 %all_to_all.38 = bf16[768,2,384]{0,2,1:T(8,128)(2,1)S(1)} all-to-all(bf16[768,2,384]{0,2,1:T(8,128)(2,1)S(1)} %bitcast.511), channel_id=1, replica_groups=mesh['dp'=16,'branch'=2] {'branch'}, dimensions={1} | all-to-all | bytes 2359296 | tf_op jit(solution)/shard_map/all_to_all | solution.py:585
  197.1 119.4 %conditional.5 = (bf16[1536,768]{1,0:T(8,128)(2,1)}, f32[384]{0:T(512)}, f32[384]{0:T(512)S(1)}, f32[384]{0:T(512)}, f32[384,54]{0,1:T(8,128)}, /*index=5*/f32[5...) conditional(s32[]{:T(128)} %convert_element_type.671, ...), branch_computations={%region_16.42_spmd, %region_42.48_spmd} | conditional | flops 9194927104 | bytes 373991840
  228.4 4.7 reshape.692
  233.0 4.4 copy.219
  237.4 45.1 %while.25 = (s32[]{:T(128)}, bf16[3,512,6,64]{1,3,2,0:T(8,128)(2,1)}, bf16[3,512,6,64]{1,3,2,0:T(8,128)(2,1)}, bf16[3,512,6,64]{1,3,2,0:T(8,128)(2,1)}, bf16[3,5...) while((s32[]{:T(128)}, ...), condition=%wide.region_45.45_spmd, body=%wide.region_43.44_spmd.sunk | while | flops 1031468032 | bytes 66428112 | solution.py:320
  316.5 4.5 copy.235
  321.1 4.7 fusion.239
  330.2 5.7 %convolution_convert_fusion.9 = bf16[2,1536,384]{2,1,0:T(8,128)(2,1)S(1)} fusion(bf16[768,2,1536]{2,0,1:T(8,128)(2,1)} %copy-done.126, bf16[768,2,384]{0,2,1:T(8,128)(2,1)S(1)} %bitcast.510), kind=kOutput, calls=%fused_computation.430 | convolution fusion | flops 1813118976 | bytes 8257536 | tf_op jit(solution)/shard_map/ngi,ngo->ogi/dot_general | solution.py:577
  359.5 120.5 %grad_reduce.1 = (f32[384,384]{1,0:T(8,128)}, f32[96,384]{1,0:T(8,128)}) custom-call(bf16[2,2,2,2,2,384,384]{6,5,4,3,2,1,0:T(8,128)(2,1)} %constant_dynamic-update-slice_fusion.g_ref, f32[96,384]{1,0:T(8,128)} %reshape.660.s_ref), custom_call_target="tpu_custom_call" | custom-call | tf_op jit(solution)/shard_map/grad_reduce/pallas_call | solution.py:156
  491.7 3.8 convert_add_fusion
  (299 shorter events, 217.8 us)
Async XLA Ops:
  7.2 115.4 %copy-start = (bf16[2,384,1536]{2,1,0:T(8,128)(2,1)S(1)}, bf16[2,384,1536]{2,1,0:T(8,128)(2,1)}, u32[]{:S(2)}) copy-start(bf16[2,384,1536]{2,1,0:T(8,128)(2,1)} %param.51) | copy-start | bytes 7077892
  12.1 4.4 copy-start.4
  12.1 4.4 copy-start.52
  75.5 26.3 %copy-start.118 = (bf16[768]{0:T(1024)(128)(2,1)S(1)}, bf16[768]{0:T(1024)(128)(2,1)}, u32[]{:S(2)}) copy-start(bf16[768]{0:T(1024)(128)(2,1)} %param.49) | copy-start | bytes 4612
  75.5 26.3 %copy-start.119 = (bf16[768]{0:T(1024)(128)(2,1)S(1)}, bf16[768]{0:T(1024)(128)(2,1)}, u32[]{:S(2)}) copy-start(bf16[768]{0:T(1024)(128)(2,1)} %param.55) | copy-start | bytes 4612
  75.5 26.3 %copy-start.120 = (bf16[768]{0:T(1024)(128)(2,1)S(1)}, bf16[768]{0:T(1024)(128)(2,1)}, u32[]{:S(2)}) copy-start(bf16[768]{0:T(1024)(128)(2,1)} %param.50) | copy-start | bytes 4612
  80.6 38.0 %all-to-all-start = ((bf16[2,768,384]{1,2,0:T(8,128)(2,1)}), bf16[2,768,384]{1,2,0:T(8,128)(2,1)}, u32[]{:S(2)}, u32[]{:S(2)}) async-start(bf16[2,768,384]{1,2,0:T(8,128)(2,1)} %copy.228), calls=%async_computation | async-start | bytes 2359296 | tf_op jit(solution)/shard_map/all_to_all | solution.py:549
  101.8 389.9 %reduce-scatter.2.cloned.1.call-start = ((), (), s32[]{:S(2)}) async-start(), calls=%async_computation.3 | async-start | bytes 3538944 | tf_op jit(solution)/shard_map/reduce_scatter | solution.py:595
  122.6 25.2 %copy-start.37 = (bf16[768,768]{0,1:T(8,128)(2,1)}, bf16[768,768]{0,1:T(8,128)(2,1)S(1)}, u32[]{:S(2)}) copy-start(bf16[768,768]{0,1:T(8,128)(2,1)S(1)} %fusion.245) | copy-start | bytes 3538948
  122.7 25.2 %copy-start.122 = (bf16[2,1536,384]{2,1,0:T(8,128)(2,1)S(1)}, bf16[2,1536,384]{2,1,0:T(8,128)(2,1)}, u32[]{:S(2)}) copy-start(bf16[2,1536,384]{2,1,0:T(8,128)(2,1)} %param.53) | copy-start | bytes 7077892
  155.8 10.8 %copy-start.41 = (bf16[768,768]{0,1:T(8,128)(2,1)}, bf16[768,768]{0,1:T(8,128)(2,1)S(1)}, u32[]{:S(2)}) copy-start(bf16[768,768]{0,1:T(8,128)(2,1)S(1)} %get-tuple-element.673) | copy-start | bytes 3538948
  178.4 18.6 %copy-start.3 = (bf16[1536,768]{1,0:T(8,128)(2,1)S(1)}, bf16[1536,768]{1,0:T(8,128)(2,1)}, u32[]{:S(2)}) copy-start(bf16[1536,768]{1,0:T(8,128)(2,1)} %param.33) | copy-start | bytes 7077892
  178.4 18.6 %copy-start.46 = (bf16[768,384]{1,0:T(8,128)(2,1)S(1)}, bf16[768,384]{1,0:T(8,128)(2,1)}, u32[]{:S(2)}) copy-start(bf16[768,384]{1,0:T(8,128)(2,1)} %param.45) | copy-start | bytes 1769476
  178.4 18.6 %copy-start.88 = (bf16[9,768]{1,0:T(8,128)(2,1)S(1)}, bf16[9,768]{1,0:T(8,128)(2,1)}, u32[]{:S(2)}) copy-start(bf16[9,768]{1,0:T(8,128)(2,1)} %param.40) | copy-start | bytes 41476
  178.4 18.6 %copy-start.115 = (bf16[384]{0:T(512)(128)(2,1)S(1)}, bf16[384]{0:T(512)(128)(2,1)}, u32[]{:S(2)}) copy-start(bf16[384]{0:T(512)(128)(2,1)} %param.42) | copy-start | bytes 2308
  178.4 18.6 %copy-start.116 = (bf16[384]{0:T(512)(128)(2,1)S(1)}, bf16[384]{0:T(512)(128)(2,1)}, u32[]{:S(2)}) copy-start(bf16[384]{0:T(512)(128)(2,1)} %param.46) | copy-start | bytes 2308
  178.5 18.6 %copy-start.124 = (bf16[54]{0:T(256)(128)(2,1)S(1)}, bf16[54]{0:T(256)(128)(2,1)}, u32[]{:S(2)}) copy-start(bf16[54]{0:T(256)(128)(2,1)} %param.44) | copy-start | bytes 328
  200.7 9.4 %copy-start.5 = (bf16[1536,768]{1,0:T(8,128)(2,1)}, bf16[1536,768]{1,0:T(8,128)(2,1)S(1)}, u32[]{:S(2)}) copy-start(bf16[1536,768]{1,0:T(8,128)(2,1)S(1)} %get-tuple-element.232) | copy-start | bytes 7077892 | tf_op jit(solution)/shard_map/conditional.1
  309.1 7.0 %copy-start.32 = (bf16[2,2,2,2,2,24,384]{6,5,4,3,2,1,0:T(8,128)(2,1)S(1)}, bf16[2,2,2,2,2,24,384]{6,5,4,3,2,1,0:T(8,128)(2,1)}, u32[]{:S(2)}) copy-start(bf16[2,2,2,2,2,24,384]{6,5,4,3,2,1,0:T(8,128)(2,1)} %reshape.645) | copy-start | bytes 1769476 | tf_op jit(solution)/shard_map/conditional.1
  316.5 4.6 copy-start.33
  316.5 4.6 copy-start.110
  349.1 9.5 %copy-start.34 = (bf16[2,2,2,2,2,24,384]{6,5,4,3,2,1,0:T(8,128)(2,1)S(1)}, bf16[2,2,2,2,2,24,384]{6,5,4,3,2,1,0:T(8,128)(2,1)}, u32[]{:S(2)}) copy-start(bf16[2,2,2,2,2,24,384]{6,5,4,3,2,1,0:T(8,128)(2,1)} %copy-done.33) | copy-start | bytes 1769476
  359.5 132.2 %copy-start.90 = (f32[768]{0:T(1024)S(1)}, f32[768]{0:T(1024)}, u32[]{:S(2)}) copy-start(f32[768]{0:T(1024)} %copy-done.89) | copy-start | bytes 9220
  491.7 6.9 %copy-start.1 = (bf16[2,384,1536]{2,1,0:T(8,128)(2,1)S(1)}, bf16[2,384,1536]{2,1,0:T(8,128)(2,1)}, u32[]{:S(2)}) copy-start(bf16[2,384,1536]{2,1,0:T(8,128)(2,1)} %param.51) | copy-start | bytes 7077892
  (46 other events, 119.1 us)
Sparse Core Ops, SparseCore 0:
  321.2 94.1 reduce-scatter.1

commit v2 on v0

v2 whole, which is shorter than its diff:
```python
import functools
import math

import jax
import jax.numpy as jnp
from jax import lax
from jax.experimental import pallas as pl
from jax.experimental.pallas import tpu as pltpu
from jax.sharding import PartitionSpec as P

HEADS = 6
HEAD_DIM = 64
KERNEL = 9
WIDTH = HEADS * HEAD_DIM
D = 768
TILE = 256
PAD = 8
NEG = -1e30
norm_eps = 1e-12
low_type = jnp.bfloat16
f32 = jnp.float32

VEC_SIZES = (
    ("query_bias", 384), ("value_bias", 384), ("pointwise_bias", 384), ("conv_value_bias", 384),
    ("output_bias", 768), ("norm1_gain", 768), ("norm1_shift", 768), ("ffn_in_bias", 3072),
    ("ffn_out_bias", 768), ("norm2_gain", 768), ("norm2_shift", 768), ("kernel_bias", 128),
)
VEC_AT = {}
_at = 0
for _name, _size in VEC_SIZES:
    VEC_AT[_name] = (_at, _size)
    _at += _size
VEC_TOTAL = _at


def vec(vecs_ref, name):
    at, size = VEC_AT[name]
    return vecs_ref[0:1, at : at + size]


def mm(a, b):
    return jnp.dot(a, b, preferred_element_type=f32)


def mm_nt(a, b):
    return lax.dot_general(a, b, (((1,), (1,)), ((), ())), preferred_element_type=f32)


def mm_tn(a, b):
    return lax.dot_general(a, b, (((0,), (0,)), ((), ())), preferred_element_type=f32)


def tap_permutation():
    row = lax.broadcasted_iota(jnp.int32, (72, 54), 0)
    col = lax.broadcasted_iota(jnp.int32, (72, 54), 1)
    head = lax.rem(row, 8)
    return jnp.where((head * 9 + lax.div(row, 8) == col) & (head < HEADS), 1.0, 0.0)


def head_spread(j):
    row = lax.broadcasted_iota(jnp.int32, (72, WIDTH), 0)
    col = lax.broadcasted_iota(jnp.int32, (72, WIDTH), 1)
    return jnp.where(row == j * 8 + lax.div(col, HEAD_DIM), 1.0, 0.0).astype(low_type)


def tap_spread():
    row = lax.broadcasted_iota(jnp.int32, (72, KERNEL * 128), 0)
    col = lax.broadcasted_iota(jnp.int32, (72, KERNEL * 128), 1)
    return jnp.where(row == lax.div(col, 128) * 8, 1.0, 0.0).astype(low_type)


def aligned(start, size):
    return pl.ds(pl.multiple_of(start, size), size)


def half_rows(block, odd):
    zero = jnp.zeros((HEAD_DIM, block.shape[1]), block.dtype)
    kept = block[HEAD_DIM:] if odd else block[:HEAD_DIM]
    return jnp.concatenate([zero, kept] if odd else [kept, zero], axis=0)


def half_lanes(block, odd):
    lane = lax.broadcasted_iota(jnp.int32, block.shape, 1)
    keep = (lane >= HEAD_DIM) if odd else (lane < HEAD_DIM)
    return jnp.where(keep, block, jnp.zeros_like(block))


def shifted(pad_ref, c, start, j, size):
    return pad_ref[c, pl.ds(start + (PAD - 4 + j), size), :]


def depth_conv(pad_ref, mask_ref, weight, start, out, flip):
    for lo in range(0, TILE, 64):
        for c in range(D // 128):
            total = None
            for j in range(KERNEL):
                w = weight[KERNEL - 1 - j if flip else j][:, c * 128 : c * 128 + 128]
                term = shifted(pad_ref, c, start + lo, j, 64) * w
                if j != KERNEL // 2:
                    term = term * mask_ref[lo : lo + 64, j * 128 : j * 128 + 128]
                total = term if total is None else total + term
            out(c, lo, total)


def span_conv(pad_ref, taps, start):
    totals = [None] * (WIDTH // 128)
    for j in range(KERNEL):
        spread = mm(taps, head_spread(j))
        for c in range(WIDTH // 128):
            term = spread[:, c * 128 : c * 128 + 128] * shifted(pad_ref, c, start, j, TILE)
            totals[c] = term if totals[c] is None else totals[c] + term
    return jnp.concatenate(totals, axis=1)


def taps_softmax(logits):
    parts = [logits[j * 8 : j * 8 + 8] for j in range(KERNEL)]
    peak = functools.reduce(jnp.maximum, parts)
    parts = [jnp.exp(x - peak) for x in parts]
    scale = 1.0 / functools.reduce(jnp.add, parts)
    return jnp.concatenate([x * scale for x in parts], axis=0)


def mix_kernel(
    hidden, segments, query_w, key_w, value_w, point_w, conv_w, depth_w, kernel_w, vecs,
    joined, q_out, k_out, v_out, probs, conv_pad, taps_out, tap_mask, query_pre, key_conv, depth_low, conv_attn,
    x_pad, v_t, ctx_t, bias, seg_rows, mask_cols,
):
    b = lax.axis_index("branch")
    base = b * 512
    segs = segments[...].astype(f32)
    row0 = jnp.where(b == 0, segs[0:1], segs[1:2])
    row1 = jnp.where(b == 0, segs[1:2], segs[2:3])
    seg_rows[0:1, :] = row0
    seg_rows[1:2, :] = row1
    seg_t = jnp.transpose(jnp.concatenate([row0, row1] * 4, axis=0))
    both = jnp.concatenate([row0, row1 + 1024.0], axis=1)
    both = jnp.broadcast_to(both, (8, 1024))
    for j in range(KERNEL):
        moved = both if j == 4 else pltpu.roll(both, (4 - j) % 1024, 1)
        tap_mask[j * 8 : j * 8 + 8, :] = jnp.where(moved == both, 1.0, 0.0)
    for c in range(D // 128):
        x_pad[c, 0:PAD, :] = jnp.zeros((PAD, 128), f32)
        x_pad[c, 1024 + PAD : 1024 + 2 * PAD, :] = jnp.zeros((PAD, 128), f32)
    for c in range(WIDTH // 128):
        conv_pad[c, 0:PAD, :] = jnp.zeros((PAD, 128), f32)
        conv_pad[c, 1024 + PAD : 1024 + 2 * PAD, :] = jnp.zeros((PAD, 128), f32)
    taps_out[...] = jnp.zeros_like(taps_out)

    def project(e, carry):
        x = hidden[aligned(base + e * TILE, TILE), :]
        rows = aligned(e * TILE, TILE)
        k_out[rows, :] = mm(x, key_w[...]).astype(low_type)
        v = mm(x, value_w[...]) + vec(vecs, "value_bias")
        v_out[rows, :] = v.astype(low_type)
        v_t[:, rows] = jnp.transpose(v).astype(low_type)
        cv = mm(x, conv_w[...]) + vec(vecs, "conv_value_bias")
        place = pl.ds(pl.multiple_of(e * TILE + PAD, 8), TILE)
        for c in range(WIDTH // 128):
            conv_pad[c, place, :] = cv[:, c * 128 : c * 128 + 128]
        for c in range(D // 128):
            x_pad[c, place, :] = x[:, c * 128 : c * 128 + 128].astype(f32)
        return carry

    lax.fori_loop(0, 4, project, 0)
    kernel_rows = mm_nt(tap_permutation().astype(low_type), kernel_w[...]).astype(low_type)
    kernel_bias = jnp.sum(tap_permutation() * vec(vecs, "kernel_bias")[:, :54], axis=1, keepdims=True)
    depth_weights = [depth_w[j : j + 1, :].astype(f32) for j in range(KERNEL)]

    def own(i, carry):
        e = b + i
        rows = aligned(i * TILE, TILE)
        ext = aligned(e * TILE, TILE)
        x = hidden[aligned(base + e * TILE, TILE), :]
        q_pre = mm(x, query_w[...]) + vec(vecs, "query_bias")
        query_pre[rows, :] = q_pre
        q = q_pre.astype(low_type).astype(f32) * 0.125
        q_out[rows, :] = q.astype(low_type)
        q_t = jnp.transpose(q).astype(low_type)
        row = lax.div(e, 2)
        keys = aligned(row * 512, 512)
        seg_q = jnp.where(row == 0, seg_rows[0:1, :], seg_rows[1:2, :])
        seg_q = jnp.where(lax.rem(e, 2) == 0, seg_q[:, :TILE], seg_q[:, TILE:])
        seg_k = jnp.where(row == 0, seg_t[:, 0:1], seg_t[:, 1:2])
        bias[...] = jnp.where(seg_k == seg_q, 0.0, NEG)
        for h in range(HEADS):
            p = h // 2
            k_pair = k_out[keys, p * 128 : p * 128 + 128]
            scores = mm(k_pair, half_rows(q_t[p * 128 : p * 128 + 128], h % 2)) + bias[...]
            peak = jnp.max(scores, axis=0, keepdims=True)
            weight = jnp.exp(scores - peak)
            weight = (weight * (1.0 / jnp.sum(weight, axis=0, keepdims=True))).astype(low_type)
            probs[i * HEADS + h] = weight
            ctx_t[h * HEAD_DIM : (h + 1) * HEAD_DIM, :] = mm(v_t[h * HEAD_DIM : (h + 1) * HEAD_DIM, keys], weight)
        joined[rows, 0:WIDTH] = jnp.transpose(ctx_t[...]).astype(low_type)

        masks = tap_mask[:, ext]
        mask_cols[...] = mm(jnp.transpose(masks).astype(low_type), tap_spread())

        def keep(c, lo, value):
            at = pl.ds(pl.multiple_of(i * TILE + lo, 64), 64)
            depth_low[at, c * 128 : c * 128 + 128] = value.astype(low_type)

        depth_conv(x_pad, mask_cols, depth_weights, e * TILE, keep, False)
        kc = mm(depth_low[rows, :], point_w[...]) + vec(vecs, "pointwise_bias")
        key_conv[rows, :] = kc
        attn = (kc * q_pre).astype(low_type)
        conv_attn[rows, :] = attn
        taps = taps_softmax(mm_nt(kernel_rows, attn) + kernel_bias)
        taps_out[:, ext] = taps
        spread = span_conv(conv_pad, jnp.transpose(taps * masks).astype(low_type), e * TILE)
        joined[rows, WIDTH : 2 * WIDTH] = spread.astype(low_type)
        return carry

    lax.fori_loop(0, 3, own, 0)


VM = pl.BlockSpec(memory_space=pltpu.VMEM)


def mix_call(hidden, segments, query_w, key_w, value_w, point_w, conv_w, depth_w, kernel_w, vecs):
    shape = jax.ShapeDtypeStruct
    outs = (
        shape((768, 768), low_type), shape((768, WIDTH), low_type), shape((1024, WIDTH), low_type),
        shape((1024, WIDTH), low_type), shape((18, 512, TILE), low_type), shape((3, 1024 + 2 * PAD, 128), f32),
        shape((72, 1024), f32), shape((72, 1024), f32), shape((768, WIDTH), f32), shape((768, WIDTH), f32),
        shape((768, D), low_type), shape((768, WIDTH), low_type),
    )
    return pl.pallas_call(
        mix_kernel, out_shape=outs, in_specs=[VM] * 10, out_specs=(VM,) * len(outs),
        scratch_shapes=[
            pltpu.VMEM((6, 1024 + 2 * PAD, 128), f32), pltpu.VMEM((WIDTH, 1024), low_type),
            pltpu.VMEM((WIDTH, TILE), f32), pltpu.VMEM((512, TILE), f32), pltpu.VMEM((8, 512), f32),
            pltpu.VMEM((TILE, KERNEL * 128), f32),
        ],
        compiler_params=pltpu.CompilerParams(vmem_limit_bytes=60 << 20),
        name="mix_forward",
    )(hidden, segments, query_w, key_w, value_w, point_w, conv_w, depth_w, kernel_w, vecs)


SMALL2 = (("output_bias", 2), ("norm1_gain", 2), ("norm1_shift", 2), ("ffn_in_bias", 8), ("ffn_out_bias", 2), ("norm2_gain", 2), ("norm2_shift", 2))


def fold_rows(values):
    return jnp.sum(values.reshape(values.shape[0] // 8, 8, values.shape[1]), axis=0)


def normalize(values):
    centered = values - jnp.mean(values, axis=1, keepdims=True)
    scale = lax.rsqrt(jnp.mean(centered * centered, axis=1, keepdims=True) + norm_eps)
    return centered * scale, scale


def norm_back(grad, unit, scale, gain):
    e = grad * gain
    return (e - jnp.mean(e, axis=1, keepdims=True) - unit * jnp.mean(e * unit, axis=1, keepdims=True)) * scale


def write_small(small, row, total):
    line = jnp.sum(total, axis=0, keepdims=True)
    for k in range(line.shape[1] // 384):
        small[row + k : row + k + 1, :] = line[:, k * 384 : k * 384 + 384]


def ffn_kernel(
    hidden, joined, cotangent, out_w, in_w, ffo_w, vecs,
    layer_out, residual_grad, joined_grad, units, small,
    active, inner, normed_low, outer_low, attn_low, slope, total, unit1, sums, sums_in,
):
    b = lax.axis_index("branch")
    sums[...] = jnp.zeros_like(sums)
    sums_in[...] = jnp.zeros_like(sums_in)

    def block(i, carry):
        rows = aligned(i * TILE, TILE)
        x = hidden[aligned(b * 768 + i * TILE, TILE), :].astype(f32)
        n1, scale1 = normalize(x + mm(joined[rows, :], out_w[...]) + vec(vecs, "output_bias"))
        unit1[...] = n1
        normed = n1 * vec(vecs, "norm1_gain") + vec(vecs, "norm1_shift")
        normed_low[rows, :] = normed.astype(low_type)
        total[...] = normed + vec(vecs, "ffn_out_bias")

        def forward(c, carry):
            g, part = lax.div(c, 2), lax.rem(c, 2)
            lanes = pl.ds(pl.multiple_of(g * 384, 128), 384)
            wide = pl.ds(pl.multiple_of(part * 768, 128), 768)
            here = pl.ds(pl.multiple_of(c * 768, 128), 768)
            at = pl.ds(pl.multiple_of(VEC_AT["ffn_in_bias"][0] + c * 768, 128), 768)
            z = mm(normed_low[rows, lanes], in_w[g, :, wide]) + vecs[0:1, at]
            phi = 0.5 + 0.5 * lax.erf(z * (0.5**0.5))
            act = (z * phi).astype(low_type)
            active[rows, here] = act
            slope[:, here] = phi + z * jnp.exp(-0.5 * z * z) * ((2.0 * math.pi) ** -0.5)
            total[:, lanes] += mm(act, ffo_w[g, pl.ds(pl.multiple_of(part * 768, 128), 768), :])
            return carry

        lax.fori_loop(0, 4, forward, 0)
        n2, scale2 = normalize(total[...])
        layer_out[rows, :] = (n2 * vec(vecs, "norm2_gain") + vec(vecs, "norm2_shift")).astype(low_type)
        grad = cotangent[rows, :].astype(f32)
        sums[5] += fold_rows(grad * n2)
        sums[6] += fold_rows(grad)
        sum_grad = norm_back(grad, n2, scale2, vec(vecs, "norm2_gain"))
        outer = sum_grad.astype(low_type)
        outer_low[rows, :] = outer
        sums[4] += fold_rows(outer.astype(f32))
        total[...] = sum_grad

        def backward(c, carry):
            g, part = lax.div(c, 2), lax.rem(c, 2)
            lanes = pl.ds(pl.multiple_of(g * 384, 128), 384)
            wide = pl.ds(pl.multiple_of(part * 768, 128), 768)
            here = pl.ds(pl.multiple_of(c * 768, 128), 768)
            grad_in = mm_nt(outer_low[rows, lanes], ffo_w[g, wide, :]) * slope[:, here]
            grad_low = grad_in.astype(low_type)
            inner[rows, here] = grad_low
            sums_in[:, here] += fold_rows(grad_low.astype(f32))
            total[:, lanes] += mm_nt(grad_low, in_w[g, :, wide])
            return carry

        lax.fori_loop(0, 4, backward, 0)
        normed_grad = total[...]
        n1 = unit1[...]
        sums[1] += fold_rows(normed_grad * n1)
        sums[2] += fold_rows(normed_grad)
        grad1 = norm_back(normed_grad, n1, scale1, vec(vecs, "norm1_gain"))
        residual_grad[rows, :] = grad1
        attn = grad1.astype(low_type)
        attn_low[rows, :] = attn
        sums[0] += fold_rows(attn.astype(f32))
        joined_grad[rows, :] = mm_nt(attn, out_w[...]).astype(low_type)
        return carry

    lax.fori_loop(0, 3, block, 0)

    for g in range(2):
        lanes = slice(g * 384, g * 384 + 384)

        def weights(m, carry, g=g, lanes=lanes):
            wide = pl.ds(pl.multiple_of(g * 1536 + m * 384, 128), 384)
            group = pl.ds(m * 8, 8)
            grad_out = mm_tn(active[:, wide], outer_low[:, lanes])
            units[group, g * 48 : g * 48 + 48, :] = grad_out.reshape(8, 48, 384).astype(low_type)
            grad_in = mm_tn(inner[:, wide], normed_low[:, lanes])
            units[group, 96 + g * 48 : 144 + g * 48, :] = grad_in.reshape(8, 48, 384).astype(low_type)
            return carry

        lax.fori_loop(0, 4, weights, 0)
    for m in range(2):
        grad_w = mm_tn(joined[:, m * 384 : m * 384 + 384], attn_low[...])
        halves = [grad_w[:, :384].reshape(16, 24, 384), grad_w[:, 384:].reshape(16, 24, 384)]
        units[m * 16 : m * 16 + 16, 192:240, :] = jnp.concatenate(halves, axis=1).astype(low_type)
    small[...] = jnp.zeros_like(small)
    row = 0
    for k, (name, count) in enumerate(SMALL2):
        if name == "ffn_in_bias":
            write_small(small, row, sums_in[...])
        else:
            write_small(small, row, sums[k])
        row += count


def ffn_call(hidden, joined, cotangent, out_w, in_w, ffo_w, vecs):
    shape = jax.ShapeDtypeStruct
    outs = (
        shape((768, D), low_type), shape((768, D), f32), shape((768, D), low_type),
        shape((32, 240, 384), low_type), shape((32, 384), f32),
    )
    return pl.pallas_call(
        ffn_kernel, out_shape=outs, in_specs=[VM] * 7, out_specs=(VM,) * len(outs),
        scratch_shapes=[
            pltpu.VMEM((768, 3072), low_type), pltpu.VMEM((768, 3072), low_type),
            pltpu.VMEM((768, D), low_type), pltpu.VMEM((768, D), low_type), pltpu.VMEM((768, D), low_type),
            pltpu.VMEM((TILE, 3072), f32), pltpu.VMEM((TILE, D), f32), pltpu.VMEM((TILE, D), f32),
            pltpu.VMEM((7, 8, D), f32), pltpu.VMEM((8, 3072), f32),
        ],
        compiler_params=pltpu.CompilerParams(vmem_limit_bytes=60 << 20),
        name="ffn",
    )(hidden, joined, cotangent, out_w, in_w, ffo_w, vecs)


def back_kernel(
    hidden, joined_grad, residual_grad, q_in, k_in, v_in, probs, conv_pad, taps, tap_mask, query_pre, key_conv, depth_low,
    conv_attn, query_w, key_w, value_w, point_w, conv_w, depth_w, kernel_w,
    grad_own, grad_other, units, small,
    dk_acc, dv_acc, k_t, dq_low, kvc, key_conv_low, dg_pad, cg_pad, x_pad, mask_cols, dw_acc, dq_t, kernel_acc, bias_acc, moved_taps, part,
    sums,
):
    b = lax.axis_index("branch")
    base = b * 512
    for ref in (dk_acc, dv_acc, dg_pad, cg_pad, dw_acc, kernel_acc, bias_acc, sums):
        ref[...] = jnp.zeros_like(ref)
    for c in range(D // 128):
        x_pad[c, 0:PAD, :] = jnp.zeros((PAD, 128), f32)
        x_pad[c, 1024 + PAD : 1024 + 2 * PAD, :] = jnp.zeros((PAD, 128), f32)

    def prepare(e, carry):
        rows = aligned(e * TILE, TILE)
        k_t[:, rows] = jnp.transpose(k_in[rows, :].astype(f32)).astype(low_type)
        x = hidden[aligned(base + e * TILE, TILE), :]
        place = pl.ds(pl.multiple_of(e * TILE + PAD, 8), TILE)
        for c in range(D // 128):
            x_pad[c, place, :] = x[:, c * 128 : c * 128 + 128].astype(f32)
        return carry

    lax.fori_loop(0, 4, prepare, 0)
    kernel_rows = mm_nt(tap_permutation().astype(low_type), kernel_w[...]).astype(low_type)
    depth_weights = [depth_w[j : j + 1, :].astype(f32) for j in range(KERNEL)]
    head_rows = head_spread(0)[:8]
    moved = []
    for j in range(KERNEL):
        rows = taps[(8 - j) * 8 : (8 - j) * 8 + 8, :]
        rows = rows if j == 4 else pltpu.roll(rows, (4 - j) % 1024, 1)
        moved.append(rows * tap_mask[j * 8 : j * 8 + 8, :])
    moved_taps[...] = jnp.transpose(jnp.concatenate(moved, axis=0)).astype(low_type)

    def own(i, carry):
        e = b + i
        rows = aligned(i * TILE, TILE)
        ext = aligned(e * TILE, TILE)
        place = pl.ds(pl.multiple_of(e * TILE + PAD, 8), TILE)
        keys = aligned(lax.div(e, 2) * 512, 512)
        d_ctx = joined_grad[rows, 0:WIDTH]
        d_ctx_t = jnp.transpose(d_ctx.astype(f32)).astype(low_type)
        for p in range(HEADS // 2):
            lanes = slice(p * 128, p * 128 + 128)
            v_pair = v_in[keys, lanes]
            q_pair = q_in[rows, lanes]
            d_pair = d_ctx[:, lanes]
            scores, weights = [], []
            for odd in range(2):
                h = 2 * p + odd
                weight = probs[i * HEADS + h]
                prob_grad = mm(v_pair, half_rows(d_ctx_t[lanes], odd))
                wide = weight.astype(f32)
                term = wide * prob_grad
                score = (term - wide * jnp.sum(term, axis=0, keepdims=True)).astype(low_type)
                dq_t[h * HEAD_DIM : (h + 1) * HEAD_DIM, :] = mm(k_t[h * HEAD_DIM : (h + 1) * HEAD_DIM, keys], score)
                scores.append(score)
                weights.append(weight)
            q_both = jnp.concatenate([half_lanes(q_pair, 0), half_lanes(q_pair, 1)], axis=0)
            d_both = jnp.concatenate([half_lanes(d_pair, 0), half_lanes(d_pair, 1)], axis=0)
            dk_acc[keys, lanes] += mm(jnp.concatenate(scores, axis=1), q_both)
            dv_acc[keys, lanes] += mm(jnp.concatenate(weights, axis=1), d_both)
        query_low = (jnp.transpose(dq_t[...]) * 0.125).astype(low_type)

        grad = joined_grad[rows, WIDTH : 2 * WIDTH].astype(f32)
        for c in range(WIDTH // 128):
            cg_pad[c, place, :] = grad[:, c * 128 : c * 128 + 128]
        grads = []
        for j in range(KERNEL):
            pieces = [
                (grad[:, c * 128 : c * 128 + 128] * shifted(conv_pad, c, e * TILE, j, TILE)).astype(low_type)
                for c in range(WIDTH // 128)
            ]
            grads.append(mm_nt(head_rows, jnp.concatenate(pieces, axis=1)) * tap_mask[j * 8 : j * 8 + 8, ext])
        kept = taps[:, ext]
        level = functools.reduce(jnp.add, [grads[j] * kept[j * 8 : j * 8 + 8] for j in range(KERNEL)])
        logit = kept * jnp.concatenate([x - level for x in grads], axis=0)
        logit_low = logit.astype(low_type)
        logit_wide = logit_low.astype(f32)
        kernel_acc[...] += mm(logit_low, conv_attn[rows, :])
        bias_acc[...] += logit_wide[:, :128] + logit_wide[:, 128:]
        span = mm(jnp.transpose(logit_wide).astype(low_type), kernel_rows).astype(low_type).astype(f32)
        point_low = (span * query_pre[rows, :]).astype(low_type)
        query_conv = (span * key_conv[rows, :]).astype(low_type)
        key_conv_low[rows, :] = point_low
        sums[2] += fold_rows(point_low.astype(f32))
        both = query_low.astype(f32) + query_conv.astype(f32)
        sums[0] += fold_rows(both)
        dq_low[rows, :] = both.astype(low_type)
        d_depth = mm_nt(point_low, point_w[...])
        for c in range(D // 128):
            dg_pad[c, place, :] = d_depth[:, c * 128 : c * 128 + 128]
        mask_cols[...] = mm(jnp.transpose(tap_mask[:, ext]).astype(low_type), tap_spread())
        for c in range(D // 128):
            totals = [None] * KERNEL
            for lo in range(0, TILE, 64):
                grad_rows = dg_pad[c, pl.ds(e * TILE + (PAD + lo), 64), :]
                for j in range(KERNEL):
                    term = shifted(x_pad, c, e * TILE + lo, j, 64) * grad_rows
                    if j != KERNEL // 2:
                        term = term * mask_cols[lo : lo + 64, j * 128 : j * 128 + 128]
                    term = fold_rows(term)
                    totals[j] = term if lo == 0 else totals[j] + term
            for j in range(KERNEL):
                dw_acc[j, :, c * 128 : c * 128 + 128] += totals[j]
        return carry

    lax.fori_loop(0, 3, own, 0)

    def spread(e):
        ext = aligned(e * TILE, TILE)
        dk = dk_acc[ext, :].astype(low_type)
        dv = dv_acc[ext, :].astype(low_type)
        dc = span_conv(cg_pad, moved_taps[ext, :], e * TILE).astype(low_type)
        kvc[ext, 0:WIDTH] = dk
        kvc[ext, WIDTH : 2 * WIDTH] = dv
        kvc[ext, 2 * WIDTH : 3 * WIDTH] = dc
        sums[1] += fold_rows(dv.astype(f32))
        sums[3] += fold_rows(dc.astype(f32))
        mask_cols[...] = mm(jnp.transpose(tap_mask[:, ext]).astype(low_type), tap_spread())

        def keep(c, lo, value):
            part[lo : lo + 64, c * 128 : c * 128 + 128] = value

        depth_conv(dg_pad, mask_cols, depth_weights, e * TILE, keep, True)
        return part[...] + mm_nt(dk, key_w[...]) + mm_nt(dv, value_w[...]) + mm_nt(dc, conv_w[...])

    def finish(i, carry):
        rows = aligned(i * TILE, TILE)
        grad_own[rows, :] = spread(b + i) + mm_nt(dq_low[rows, :], query_w[...]) + residual_grad[rows, :]
        return carry

    lax.fori_loop(0, 3, finish, 0)
    grad_other[...] = spread(3 * (1 - b)).astype(low_type)

    depth_total = jnp.sum(dw_acc[...], axis=1)
    depth_t = jnp.transpose(jnp.concatenate([depth_total, jnp.zeros((128 - KERNEL, D), f32)], axis=0))
    for m in range(2):
        lanes = slice(m * 384, m * 384 + 384)
        group = slice(m * 16, m * 16 + 16)
        grad_kvc = mm_tn(hidden[aligned(base, 512), lanes], kvc[0:512, :]) + mm_tn(hidden[aligned(base + 512, 512), lanes], kvc[512:1024, :])
        grad_q = mm_tn(hidden[pl.ds(pl.multiple_of(b * 768, 256), 768), lanes], dq_low[...])
        grad_p = mm_tn(depth_low[:, lanes], key_conv_low[...])
        grad_d = jnp.concatenate([depth_t[lanes], jnp.zeros((384, 256), f32)], axis=1)
        pieces = [grad_q] + [grad_kvc[:, k * WIDTH : (k + 1) * WIDTH] for k in range(3)] + [grad_p, grad_d]
        pieces = [x.reshape(16, 24, 384) for x in pieces]
        for k in range(3):
            units[group, k * 48 : k * 48 + 48, :] = jnp.concatenate(pieces[2 * k : 2 * k + 2], axis=1).astype(low_type)
    small[...] = jnp.zeros_like(small)
    small[0:72, :] = kernel_acc[...]
    for k in range(4):
        small[72 + k : 73 + k, :] = jnp.sum(sums[k], axis=0, keepdims=True)
    column = jnp.concatenate([bias_acc[...], jnp.zeros((56, 128), f32)], axis=0)
    small[76:77, 0:128] = jnp.sum(jnp.transpose(column), axis=0, keepdims=True)


def back_call(hidden, joined_grad, residual_grad, saved, weights):
    shape = jax.ShapeDtypeStruct
    outs = (shape((768, D), f32), shape((256, D), low_type), shape((32, 144, 384), low_type), shape((96, 384), f32))
    operands = (hidden, joined_grad, residual_grad) + tuple(saved) + tuple(weights)
    ext = 1024 + 2 * PAD
    return pl.pallas_call(
        back_kernel, out_shape=outs, in_specs=[VM] * len(operands), out_specs=(VM,) * len(outs),
        scratch_shapes=[
            pltpu.VMEM((1024, WIDTH), f32), pltpu.VMEM((1024, WIDTH), f32), pltpu.VMEM((WIDTH, 1024), low_type),
            pltpu.VMEM((768, WIDTH), low_type), pltpu.VMEM((1024, 3 * WIDTH), low_type), pltpu.VMEM((768, WIDTH), low_type),
            pltpu.VMEM((6, ext, 128), f32), pltpu.VMEM((3, ext, 128), f32), pltpu.VMEM((6, ext, 128), f32),
            pltpu.VMEM((TILE, KERNEL * 128), f32), pltpu.VMEM((KERNEL, 8, D), f32), pltpu.VMEM((WIDTH, TILE), f32),
            pltpu.VMEM((72, WIDTH), f32), pltpu.VMEM((72, 128), f32), pltpu.VMEM((1024, 72), low_type), pltpu.VMEM((TILE, D), f32),
            pltpu.VMEM((4, 8, WIDTH), f32),
        ],
        compiler_params=pltpu.CompilerParams(vmem_limit_bytes=60 << 20),
        name="mix_backward",
    )(*operands)


MESH = pl.DeviceIdType.MESH
CHUNK = 48


def comm_orders(bits, extra):
    halving = list(range(extra, bits))
    first = [1] if 1 in halving else []
    rest = [k for k in halving if k not in first]
    a = [rest[0], rest[2], rest[1]] + rest[3:]
    b = [rest[1], rest[2], rest[0]] + rest[3:]
    return first + a, first + b


def comm_kernel(dp_size, g2, g3, s2, s3, other, out, s_out, got, rb, srb, erb, send, recv, ssend, srecv, esend, erecv, osem):
    bits = int(math.log2(dp_size)) + 1
    extra = max(0, bits - 5)
    orders = comm_orders(bits, extra)
    nh = bits - extra
    dp = lax.axis_index("dp")
    br = lax.axis_index("branch")
    my = [br] + [lax.rem(lax.div(dp, 1 << (k - 1)), 2) for k in range(1, bits)]
    chunks2 = g2.shape[-2] // CHUNK
    n_chunks = chunks2 + g3.shape[-2] // CHUNK

    def partner(k):
        if k == 0:
            return (dp, 1 - br)
        return (dp + (1 << (k - 1)) * (1 - 2 * my[k]), br)

    barrier = pltpu.get_barrier_semaphore()
    for k in range(bits):
        pl.semaphore_signal(barrier, inc=1, device_id=partner(k), device_id_type=MESH)
    pl.semaphore_wait(barrier, bits)

    def copy(src, dst, ssem, rsem, k):
        return pltpu.make_async_remote_copy(
            src_ref=src, dst_ref=dst, send_sem=ssem, recv_sem=rsem, device_id=partner(k), device_id_type=MESH
        )

    def offset(s):
        return sum(1 << (nh - 1 - t) for t in range(s))

    def source(c):
        return (g2, c * CHUNK) if c < chunks2 else (g3, (c - chunks2) * CHUNK)

    def place(u, free, fixed):
        names = sorted(free + list(fixed), reverse=True)
        index, at = 0, len(free) - 1
        for k in names:
            if k in fixed:
                value = fixed[k]
            else:
                value = (u >> at) & 1
                at -= 1
            index = index * 2 + value
        return index

    waits = {}

    def free_bits(order, s):
        return sorted(set(order[s:]), reverse=True)

    def start(c, s, order):
        k = order[s]
        free = free_bits(order, s + 1)
        count = 1 << len(free)
        for u in range(count):
            at = place(u, free, {k: 1 - my[k]})
            if s == 0:
                ref, row = source(c)
                src = ref.at[at, pl.ds(row, CHUNK)]
            else:
                src = rb.at[c, offset(s - 1) + at]
            copy(src, rb.at[c, offset(s) + u], send.at[c, s], recv.at[c, s], k).start()
        whole = rb.at[c, pl.ds(offset(s), count)]
        waits[(c, s)] = copy(whole, whole, send.at[c, s], recv.at[c, s], k)

    def add(c, s, order):
        waits[(c, s)].wait_recv()
        k = order[s]
        free = free_bits(order, s + 1)
        for u in range(1 << len(free)):
            at = place(u, free, {k: my[k]})
            if s == 0:
                ref, row = source(c)
                mine = ref[at, row : row + CHUNK, :]
            else:
                mine = rb[c, offset(s - 1) + at]
            total = mine.astype(jnp.float32) + rb[c, offset(s) + u].astype(jnp.float32)
            if s == nh - 1:
                out[c * CHUNK : (c + 1) * CHUNK, :] = total
            else:
                rb[c, offset(s) + u] = total.astype(rb.dtype)

    small_order = orders[0] + list(range(extra))

    def small_start(s):
        cp = copy(s_out, srb.at[s], ssend.at[s], srecv.at[s], small_order[s])
        cp.start()
        waits[("s", s)] = cp

    def small_add(s):
        waits[("s", s)].wait()
        s_out[...] = s_out[...] + srb[s]

    other_copy = copy(other, got, osem.at[0], osem.at[1], 0)
    other_copy.start()
    s_out[0 : s3.shape[0], :] = s3[...]
    s_out[s3.shape[0] :, :] = s2[...]
    half = n_chunks // 2
    for w in range(max(half + nh, bits + 1)):
        for p in range(half - 1, -1, -1):
            s = w - p
            for c, order in ((2 * p, orders[0]), (2 * p + 1, orders[1])):
                if 1 <= s <= nh:
                    add(c, s - 1, order)
                if 0 <= s < nh:
                    start(c, s, order)
        if 1 <= w <= bits:
            small_add(w - 1)
        if w < bits:
            small_start(w)
    for k in range(extra):
        cp = copy(out, erb.at[k], esend.at[k], erecv.at[k], k)
        cp.start()
        cp.wait()
        out[...] = out[...] + erb[k]
    for c in range(n_chunks):
        for s in range(nh):
            waits[(c, s)].wait_send()
    other_copy.wait()


def comm_call(dp_size, g2, g3, s2, s3, other):
    bits = int(math.log2(dp_size)) + 1
    extra = max(0, bits - 5)
    nh = bits - extra
    rows = g2.shape[1] + g3.shape[1]
    n_chunks = rows // CHUNK
    shape = jax.ShapeDtypeStruct
    small_shape = (s2.shape[0] + s3.shape[0], 384)
    dma = pltpu.SemaphoreType.DMA
    return pl.pallas_call(
        functools.partial(comm_kernel, dp_size),
        out_shape=(shape((rows, 384), jnp.float32), shape(small_shape, jnp.float32), shape(other.shape, other.dtype)),
        in_specs=[VM] * 5,
        out_specs=(VM, VM, VM),
        scratch_shapes=[
            pltpu.VMEM((n_chunks, (1 << nh) - 1, CHUNK, 384), jnp.bfloat16),
            pltpu.VMEM((bits,) + small_shape, jnp.float32),
            pltpu.VMEM((max(extra, 1), rows if extra else 8, 384), jnp.float32),
            dma((n_chunks, nh)), dma((n_chunks, nh)), dma((bits,)), dma((bits,)),
            dma((max(extra, 1),)), dma((max(extra, 1),)), dma((2,)),
        ],
        compiler_params=pltpu.CompilerParams(collective_id=0, has_side_effects=True, vmem_limit_bytes=60 << 20),
        name="grad_reduce",
    )(g2, g3, s2, s3, other)


def local(
    hidden, segment_ids, query_weight, query_bias, key_weight, value_weight, value_bias, depthwise_weight,
    pointwise_weight, pointwise_bias, kernel_weight, kernel_bias, conv_value_weight, conv_value_bias, output_weight,
    output_bias, norm1_gain, norm1_shift, ffn_in_weight, ffn_in_bias, ffn_out_weight, ffn_out_bias, norm2_gain,
    norm2_shift, cotangent,
):
    dp_size = lax.axis_size("dp")
    branch = lax.axis_index("branch")
    named = dict(
        query_bias=query_bias, value_bias=value_bias, pointwise_bias=pointwise_bias, conv_value_bias=conv_value_bias,
        output_bias=output_bias, norm1_gain=norm1_gain, norm1_shift=norm1_shift, ffn_in_bias=ffn_in_bias,
        ffn_out_bias=ffn_out_bias, norm2_gain=norm2_gain, norm2_shift=norm2_shift,
        kernel_bias=jnp.pad(kernel_bias, (0, 128 - kernel_bias.shape[0])),
    )
    vecs = jnp.concatenate([named[name] for name, _ in VEC_SIZES]).astype(f32).reshape(1, VEC_TOTAL)
    joined, *saved = mix_call(
        hidden, segment_ids, query_weight, key_weight, value_weight, pointwise_weight, conv_value_weight,
        depthwise_weight, kernel_weight, vecs,
    )
    layer_out, residual_grad, joined_grad, units2, small2 = ffn_call(
        hidden, joined, cotangent, output_weight, ffn_in_weight, ffn_out_weight, vecs
    )
    grad_own, grad_other, units3, small3 = back_call(
        hidden, joined_grad, residual_grad, saved,
        (query_weight, key_weight, value_weight, pointwise_weight, conv_value_weight, depthwise_weight, kernel_weight),
    )
    out_sum, small_sum, got = comm_call(dp_size, units2, units3, small2, small3, grad_other)
    start = (1 - branch) * 512
    block = lax.dynamic_slice_in_dim(grad_own, start, 256, 0) + got.astype(f32)
    input_grad = lax.dynamic_update_slice_in_dim(grad_own, block, start, 0)
    share = 2 * dp_size // 32
    device = lax.axis_index("dp") * 2 + branch

    def piece(start, rows):
        n = rows // share
        return lax.dynamic_slice_in_dim(out_sum, start + lax.rem(device, share) * n, n, 0)

    def small(row, size):
        return small_sum[row : row + -(-size // 384)].reshape(-1)[:size]

    kern_w = jnp.transpose(small_sum[:72].reshape(9, 8, 384)[:, :6], (2, 1, 0)).reshape(384, 54)
    kern_b = jnp.transpose(small_sum[76, :72].reshape(9, 8)[:, :6]).reshape(54)
    in_g = jnp.stack([piece(96, 48), piece(144, 48)])
    return (
        layer_out,
        input_grad,
        piece(240, 24),
        small(72, 384),
        piece(264, 24),
        piece(288, 24),
        small(73, 384),
        jnp.transpose(piece(360, 24)[:, :KERNEL]),
        piece(336, 24),
        small(74, 384),
        kern_w,
        kern_b,
        piece(312, 24),
        small(75, 384),
        jnp.concatenate([piece(192, 24), piece(216, 24)], axis=1),
        small(96, 768),
        small(98, 768),
        small(100, 768),
        jnp.transpose(in_g, (0, 2, 1)),
        small(102, 3072),
        jnp.stack([piece(0, 48), piece(48, 48)]),
        small(110, 768),
        small(112, 768),
        small(114, 768),
    )


def solution(mesh):
    tokens, copied = P(("dp", "branch"), None), P()
    in_specs = (P("dp", None), P("dp", None)) + (copied,) * 22 + (tokens,)
    out_specs = (
        tokens, tokens, tokens, copied, tokens, tokens, copied, P(None, ("dp", "branch")), tokens, copied, copied, copied,
        tokens, copied, tokens, copied, copied, copied, P(None, None, ("dp", "branch")), copied,
        P(None, ("dp", "branch"), None), copied, copied, copied,
    )
    return jax.shard_map(local, mesh=mesh, in_specs=in_specs, out_specs=out_specs, check_vma=False)
```

time: 1160 us -> 198 us (0.17)
  waiting for transfers between devices: 702 us -> 0 us
  Pallas kernels: 0 us -> 173 us
  matrix products: 145 us -> 0 us
  blocking collectives: 101 us -> 0 us
  local copies, waits for them, and re-layouts: 116 us -> 20.2 us
  other arithmetic: 35.8 us -> 3.14 us
  starting transfers between devices: 26.1 us -> 0 us
  between operations: 16.4 us -> 0.74 us
    unnamed x14 -> x0, waiting for transfers between devices: 377 us -> none
    reduce_scatter x3 -> x0, waiting for transfers between devices: 217 us -> none  [the longest x2 217 us: local(): lax.psum_scatter(weight_grads, ('dp', 'branch'), scatter_dimension=0, til...]
    pallas_call x0 -> x4, Pallas kernels: none -> 173 us  [the longest x1 70.8 us: comm_call(): pl.pallas_call(functools.partial(comm_kernel, dp_size), out_shape=(shape(...]
    dot_general x42 -> x0, matrix products: 145 us -> none  [the longest x2 27.4 us: grouped_forward(): jnp.einsum('ngi,gio->ngo', pieces, weight, preferred_element_type=jnp.flo...]
    psum x1 -> x0, blocking collectives: 101 us -> none  [local(): smalls = lax.psum(small_terms, ('dp', 'branch'))]
    psum x1 -> x0, waiting for transfers between devices: 100 us -> none  [local(): smalls = lax.psum(small_terms, ('dp', 'branch'))]
    while x28 -> x0, local copies, waits for them, and re-layouts: 28.9 us -> none  [the longest x7 16 us: attention_backward(): lax.map(per_sequence, (queries, keys_low, values_low, segments, log_sums,...]
    all_to_all x2 -> x0, starting transfers between devices: 25.7 us -> none  [the longest x1 21.3 us: local(): lax.all_to_all(context, 'branch', split_axis=0, concat_axis=1, tiled=True)]
  transfers between devices with their start and end apart: 11 -> 0, of which waited for: 8 -> 0; matrix products, arithmetic and copies ran while one was open for 5% -> 0% of each run, Pallas kernels for 0% -> 0%
where the time goes in v2:
time: 198 us; the launch traced here: 197 us
  Pallas kernels  173 us (87%)
  local copies, waits for them, and re-layouts  20.2 us (10%)
  other arithmetic  3.14 us (2%)
    pallas_call x1, Pallas kernels, comm_call(): pl.pallas_call(functools.partial(comm_kernel, dp_size), out_shape=(shape(...  70.8 us
    pallas_call x1, Pallas kernels, ffn_call(): pl.pallas_call(ffn_kernel, out_shape=outs, in_specs=[VM] * 7, out_specs=(...  38.7 us
    pallas_call x1, Pallas kernels, back_call(): pl.pallas_call(back_kernel, out_shape=outs, in_specs=[VM] * len(operands)...  37.4 us
    pallas_call x1, Pallas kernels, mix_call(): pl.pallas_call(mix_kernel, out_shape=outs, in_specs=[VM] * 10, out_specs=...  26.4 us
    unnamed x20, local copies, waits for them, and re-layouts  9.85 us
    reshape x7, local copies, waits for them, and re-layouts, small(): return small_sum[row:row + -(-size // 384)].reshape(-1)[:size]  4.2 us

profile of v2, /device:TPU:0, one launch (start us, length us, event | category | flops | bytes accessed | tf_op | source)
XLA Modules:
  0.0 197.4 jit_solution(8905019580380936690)
XLA Ops:
  0.7 0.7 constant_dynamic-update-slice_fusion.11
  1.3 0.7 constant_dynamic-update-slice_fusion.10
  2.0 0.7 constant_dynamic-update-slice_fusion.9
  2.7 0.7 constant_dynamic-update-slice_fusion.8
  3.4 0.7 constant_dynamic-update-slice_fusion.7
  4.1 0.7 constant_dynamic-update-slice_fusion.6
  4.8 0.7 constant_dynamic-update-slice_fusion.5
  5.5 0.7 constant_dynamic-update-slice_fusion.4
  6.2 0.7 constant_dynamic-update-slice_fusion.3
  6.9 0.7 constant_dynamic-update-slice_fusion.2
  7.6 0.7 constant_dynamic-update-slice_fusion.1
  8.3 0.7 constant_dynamic-update-slice_fusion
  9.6 1.5 copy.54.kernel_w
  11.1 26.4 %mix_forward.1 = (bf16[768,768]{1,0:T(8,128)(2,1)}, bf16[768,384]{1,0:T(8,128)(2,1)}, bf16[1024,384]{1,0:T(8,128)(2,1)}, bf16[1024,384]{1,0:T(8,128)(2,1)}, bf16...) custom-call(bf16[1536,768]{1,0:T(8,128)(2,1)} %hidden.5, ...), custom_call_target="tpu_custom_call" | custom-call | tf_op jit(solution)/shard_map/mix_forward/pallas_call | solution.py:228
  37.5 38.7 %ffn.1 = (bf16[768,768]{1,0:T(8,128)(2,1)}, f32[768,768]{1,0:T(8,128)}, bf16[768,768]{1,0:T(8,128)(2,1)}, bf16[32,240,384]{2,1,0:T(8,128)(2,1)}, f32[32,384]{1,0:T(8,128)}) custom-call(bf16[1536,768]{1,0:T(8,128)(2,1)} %hidden.5, bf16[768,768]{1,0:T(8,128)(2,1)} %get-tuple-element.48.joined, bf16[768,768]{1,0:T(8,128)(2,1)} %cotangent.1, ...), custom_call_target="tpu_custom_call" | custom-call | tf_op jit(solution)/shard_map/ffn/pallas_call | solution.py:368
  76.2 37.4 %mix_backward.1 = (f32[768,768]{1,0:T(8,128)}, bf16[256,768]{1,0:T(8,128)(2,1)}, bf16[32,144,384]{2,1,0:T(8,128)(2,1)}, f32[96,384]{1,0:T(8,128)}) custom-call(bf16[1536,768]{1,0:T(8,128)(2,1)} %hidden.5, bf16[768,768]{1,0:T(8,128)(2,1)} %get-tuple-element.50.joined_grad, f32[768,768]{1,0:T(8,128)} %get-tuple-element.51.residual_grad, ...), custom_call_target="tpu_custom_call" | custom-call | tf_op jit(solution)/shard_map/mix_backward/pallas_call | solution.py:543
  113.7 70.8 %grad_reduce.1 = (f32[384,384]{1,0:T(8,128)}, f32[128,384]{1,0:T(8,128)}, bf16[256,768]{1,0:T(8,128)(2,1)}) custom-call(bf16[32,240,384]{2,1,0:T(8,128)(2,1)} %get-tuple-element.64.g2, bf16[32,144,384]{2,1,0:T(8,128)(2,1)} %get-tuple-element.65.g3, f32[32,384]{1,0:T(8,128)} %get-tuple-element.66.s2, f32[96,384]{1,0:T(8,128)} %get-tuple-element.67.s3, ...), custom_call_target="tpu_custom_call" | custom-call | tf_op jit(solution)/shard_map/grad_reduce/pallas_call | solution.py:700
  184.5 1.1 slice_bitcast_fusion.2
  185.6 0.7 maximum_bitcast_fusion
  186.3 1.5 fusion
  188.5 1.1 add_dynamic-update-slice_fusion
  189.7 0.8 reshape.254
  195.4 0.7 slice_bitcast_fusion.5
  196.1 0.7 copy.58
  (25 shorter events, 7.0 us)
Async XLA Ops:
  113.7 74.8 %copy-start = (f32[768,768]{1,0:T(8,128)S(1)}, f32[768,768]{1,0:T(8,128)}, u32[]{:S(2)}) copy-start(f32[768,768]{1,0:T(8,128)} %get-tuple-element.63) | copy-start | bytes 7077892
  184.5 5.1 %copy-start.2 = (f32[128,384]{1,0:T(8,128)S(1)}, f32[128,384]{1,0:T(8,128)}, u32[]{:S(2)}) copy-start(f32[128,384]{1,0:T(8,128)} %get-tuple-element.71) | copy-start | bytes 589828
  189.6 7.8 %copy-start.1 = (f32[768,768]{1,0:T(8,128)}, f32[768,768]{1,0:T(8,128)S(1)}, u32[]{:S(2)}) copy-start(f32[768,768]{1,0:T(8,128)S(1)} %add_dynamic-update-slice_fusion) | copy-start | bytes 7077892

commit v3 on v2

--- a/solution.py
+++ b/solution.py
@@ -38,6 +38,18 @@
     return vecs_ref[0:1, at : at + size]
 
 
+def load_vecs(vecs, names, refs):
+    for name, ref in zip(names, refs):
+        at, size = VEC_AT[name]
+        if name == "kernel_bias":
+            size = ref.shape[0]
+        vecs[0:1, at : at + size] = ref[...].astype(f32).reshape(1, size)
+
+
+MIX_VECS = ("query_bias", "value_bias", "pointwise_bias", "conv_value_bias", "kernel_bias")
+FFN_VECS = ("output_bias", "norm1_gain", "norm1_shift", "ffn_in_bias", "ffn_out_bias", "norm2_gain", "norm2_shift")
+
+
 def mm(a, b):
     return jnp.dot(a, b, preferred_element_type=f32)
 
@@ -121,10 +133,11 @@
 
 
 def mix_kernel(
-    hidden, segments, query_w, key_w, value_w, point_w, conv_w, depth_w, kernel_w, vecs,
-    joined, q_out, k_out, v_out, probs, conv_pad, taps_out, tap_mask, query_pre, key_conv, depth_low, conv_attn,
-    x_pad, v_t, ctx_t, bias, seg_rows, mask_cols,
+    hidden, segments, query_w, key_w, value_w, point_w, conv_w, depth_w, kernel_w,
+    vec0, vec1, vec2, vec3, vec4, joined, q_out, k_out, v_out, probs, conv_pad, taps_out, tap_mask, query_pre, key_conv, depth_low, conv_attn,
+    x_pad, v_t, ctx_t, bias, seg_rows, mask_cols, vecs,
 ):
+    load_vecs(vecs, MIX_VECS, (vec0, vec1, vec2, vec3, vec4))
     b = lax.axis_index("branch")
     base = b * 512
     segs = segments[...].astype(f32)
@@ -162,7 +175,7 @@
         return carry
 
     lax.fori_loop(0, 4, project, 0)
-    kernel_rows = mm_nt(tap_permutation().astype(low_type), kernel_w[...]).astype(low_type)
+    kernel_rows = mm(tap_permutation().astype(low_type), kernel_w[...]).astype(low_type)
     kernel_bias = jnp.sum(tap_permutation() * vec(vecs, "kernel_bias")[:, :54], axis=1, keepdims=True)
     depth_weights = [depth_w[j : j + 1, :].astype(f32) for j in range(KERNEL)]
 
@@ -217,7 +230,7 @@
 VM = pl.BlockSpec(memory_space=pltpu.VMEM)
 
 
-def mix_call(hidden, segments, query_w, key_w, value_w, point_w, conv_w, depth_w, kernel_w, vecs):
+def mix_call(*operands):
     shape = jax.ShapeDtypeStruct
     outs = (
         shape((768, 768), low_type), shape((768, WIDTH), low_type), shape((1024, WIDTH), low_type),
@@ -226,15 +239,15 @@
         shape((768, D), low_type), shape((768, WIDTH), low_type),
     )
     return pl.pallas_call(
-        mix_kernel, out_shape=outs, in_specs=[VM] * 10, out_specs=(VM,) * len(outs),
+        mix_kernel, out_shape=outs, in_specs=[VM] * len(operands), out_specs=(VM,) * len(outs),
         scratch_shapes=[
             pltpu.VMEM((6, 1024 + 2 * PAD, 128), f32), pltpu.VMEM((WIDTH, 1024), low_type),
             pltpu.VMEM((WIDTH, TILE), f32), pltpu.VMEM((512, TILE), f32), pltpu.VMEM((8, 512), f32),
-            pltpu.VMEM((TILE, KERNEL * 128), f32),
+            pltpu.VMEM((TILE, KERNEL * 128), f32), pltpu.VMEM((1, VEC_TOTAL), f32),
         ],
         compiler_params=pltpu.CompilerParams(vmem_limit_bytes=60 << 20),
         name="mix_forward",
-    )(hidden, segments, query_w, key_w, value_w, point_w, conv_w, depth_w, kernel_w, vecs)
+    )(*operands)
 
 
 SMALL2 = (("output_bias", 2), ("norm1_gain", 2), ("norm1_shift", 2), ("ffn_in_bias", 8), ("ffn_out_bias", 2), ("norm2_gain", 2), ("norm2_shift", 2))
@@ -262,10 +275,12 @@
 
 
 def ffn_kernel(
-    hidden, joined, cotangent, out_w, in_w, ffo_w, vecs,
+    hidden, joined, cotangent, out_w, in_w, ffo_w,
+    vec0, vec1, vec2, vec3, vec4, vec5, vec6,
     layer_out, residual_grad, joined_grad, units, small,
-    active, inner, normed_low, outer_low, attn_low, slope, total, unit1, sums, sums_in,
+    active, inner, normed_low, outer_low, attn_low, slope, total, unit1, sums, sums_in, vecs,
 ):
+    load_vecs(vecs, FFN_VECS, (vec0, vec1, vec2, vec3, vec4, vec5, vec6))
     b = lax.axis_index("branch")
     sums[...] = jnp.zeros_like(sums)
     sums_in[...] = jnp.zeros_like(sums_in)
@@ -359,23 +374,23 @@
         row += count
 
 
-def ffn_call(hidden, joined, cotangent, out_w, in_w, ffo_w, vecs):
+def ffn_call(*operands):
     shape = jax.ShapeDtypeStruct
     outs = (
         shape((768, D), low_type), shape((768, D), f32), shape((768, D), low_type),
         shape((32, 240, 384), low_type), shape((32, 384), f32),
     )
     return pl.pallas_call(
-        ffn_kernel, out_shape=outs, in_specs=[VM] * 7, out_specs=(VM,) * len(outs),
+        ffn_kernel, out_shape=outs, in_specs=[VM] * len(operands), out_specs=(VM,) * len(outs),
         scratch_shapes=[
             pltpu.VMEM((768, 3072), low_type), pltpu.VMEM((768, 3072), low_type),
             pltpu.VMEM((768, D), low_type), pltpu.VMEM((768, D), low_type), pltpu.VMEM((768, D), low_type),
             pltpu.VMEM((TILE, 3072), f32), pltpu.VMEM((TILE, D), f32), pltpu.VMEM((TILE, D), f32),
-            pltpu.VMEM((7, 8, D), f32), pltpu.VMEM((8, 3072), f32),
+            pltpu.VMEM((7, 8, D), f32), pltpu.VMEM((8, 3072), f32), pltpu.VMEM((1, VEC_TOTAL), f32),
         ],
         compiler_params=pltpu.CompilerParams(vmem_limit_bytes=60 << 20),
         name="ffn",
-    )(hidden, joined, cotangent, out_w, in_w, ffo_w, vecs)
+    )(*operands)
 
 
 def back_kernel(
@@ -403,7 +418,7 @@
         return carry
 
     lax.fori_loop(0, 4, prepare, 0)
-    kernel_rows = mm_nt(tap_permutation().astype(low_type), kernel_w[...]).astype(low_type)
+    kernel_rows = mm(tap_permutation().astype(low_type), kernel_w[...]).astype(low_type)
     depth_weights = [depth_w[j : j + 1, :].astype(f32) for j in range(KERNEL)]
     head_rows = head_spread(0)[:8]
     moved = []
@@ -714,6 +729,54 @@
     )(g2, g3, s2, s3, other)
 
 
+def exact_columns(table, rows):
+    return lax.dot_general(table, rows, (((0,), (0,)), ((), ())), precision=lax.Precision.HIGHEST, preferred_element_type=f32)
+
+
+FINAL_SMALL = (
+    ("query_b", 72, 384), ("value_b", 73, 384), ("point_b", 74, 384), ("conv_b", 75, 384), ("out_b", 96, 768), ("gain1", 98, 768),
+    ("shift1", 100, 768), ("in_b", 102, 3072), ("ffo_b", 110, 768), ("gain2", 112, 768), ("shift2", 114, 768),
+)
+
+
+def final_kernel(
+    grad_own, got, total, small,
+    input_grad, query_w, key_w, value_w, depth_w, point_w, kernel_w, kernel_b, conv_w, out_w, in_w, ffo_w, *vectors,
+):
+    b = lax.axis_index("branch")
+    input_grad[...] = grad_own[...]
+    rows = aligned((1 - b) * 512, 256)
+    input_grad[rows, :] = grad_own[rows, :] + got[...].astype(f32)
+    for ref, row in ((query_w, 240), (key_w, 264), (value_w, 288), (conv_w, 312), (point_w, 336)):
+        ref[...] = total[row : row + 24, :]
+    ffo_w[0] = total[0:48, :]
+    ffo_w[1] = total[48:96, :]
+    out_w[:, 0:384] = total[192:216, :]
+    out_w[:, 384:768] = total[216:240, :]
+    in_w[0] = total[96:144, :]
+    in_w[1] = total[144:192, :]
+    depth = jnp.concatenate([total[360:384, 0:128], jnp.zeros((104, 128), f32)], axis=0)
+    depth_w[...] = jnp.transpose(depth)[0:KERNEL, 0:24]
+    table = tap_permutation()
+    kernel_w[...] = exact_columns(table, small[0:72, :])
+    column = jnp.transpose(jnp.concatenate([small[76:77, 0:128]] * 128, axis=0))[0:72, :]
+    kernel_b[...] = jnp.sum(column[:, 0:54] * table, axis=0, keepdims=True).reshape(54)
+    for ref, (_, row, size) in zip(vectors, FINAL_SMALL):
+        ref[...] = jnp.concatenate([small[row + k : row + k + 1, :] for k in range(size // 384)], axis=1).reshape(size)
+
+
+def final_call(grad_own, got, total, small):
+    shape = lambda *s: jax.ShapeDtypeStruct(s, f32)
+    outs = (
+        shape(768, D), shape(24, 384), shape(24, 384), shape(24, 384), shape(KERNEL, 24), shape(24, 384), shape(54, 384), shape(54),
+        shape(24, 384), shape(24, 768), shape(2, 48, 384), shape(2, 48, 384),
+    ) + tuple(shape(size) for _, _, size in FINAL_SMALL)
+    return pl.pallas_call(
+        final_kernel, out_shape=outs, in_specs=[VM] * 4, out_specs=(VM,) * len(outs),
+        compiler_params=pltpu.CompilerParams(vmem_limit_bytes=32 << 20), name="finish",
+    )(grad_own, got, total, small)
+
+
 def local(
     hidden, segment_ids, query_weight, query_bias, key_weight, value_weight, value_bias, depthwise_weight,
     pointwise_weight, pointwise_bias, kernel_weight, kernel_bias, conv_value_weight, conv_value_bias, output_weight,
@@ -722,29 +785,33 @@
 ):
     dp_size = lax.axis_size("dp")
     branch = lax.axis_index("branch")
-    named = dict(
-        query_bias=query_bias, value_bias=value_bias, pointwise_bias=pointwise_bias, conv_value_bias=conv_value_bias,
-        output_bias=output_bias, norm1_gain=norm1_gain, norm1_shift=norm1_shift, ffn_in_bias=ffn_in_bias,
-        ffn_out_bias=ffn_out_bias, norm2_gain=norm2_gain, norm2_shift=norm2_shift,
-        kernel_bias=jnp.pad(kernel_bias, (0, 128 - kernel_bias.shape[0])),
-    )
-    vecs = jnp.concatenate([named[name] for name, _ in VEC_SIZES]).astype(f32).reshape(1, VEC_TOTAL)
+    kernel_rows = jnp.transpose(kernel_weight)
     joined, *saved = mix_call(
         hidden, segment_ids, query_weight, key_weight, value_weight, pointwise_weight, conv_value_weight,
-        depthwise_weight, kernel_weight, vecs,
+        depthwise_weight, kernel_rows, query_bias, value_bias, pointwise_bias, conv_value_bias, kernel_bias,
     )
     layer_out, residual_grad, joined_grad, units2, small2 = ffn_call(
-        hidden, joined, cotangent, output_weight, ffn_in_weight, ffn_out_weight, vecs
+        hidden, joined, cotangent, output_weight, ffn_in_weight, ffn_out_weight, output_bias, norm1_gain, norm1_shift,
+        ffn_in_bias, ffn_out_bias, norm2_gain, norm2_shift,
     )
     grad_own, grad_other, units3, small3 = back_call(
         hidden, joined_grad, residual_grad, saved,
-        (query_weight, key_weight, value_weight, pointwise_weight, conv_value_weight, depthwise_weight, kernel_weight),
+        (query_weight, key_weight, value_weight, pointwise_weight, conv_value_weight, depthwise_weight, kernel_rows),
     )
     out_sum, small_sum, got = comm_call(dp_size, units2, units3, small2, small3, grad_other)
+    share = 2 * dp_size // 32
+    if share == 1:
+        (
+            input_grad, query_w, key_w, value_w, depth_w, point_w, kernel_w, kernel_b, conv_w, out_w, in_w, ffo_w,
+            query_b, value_b, point_b, conv_b, out_b, gain1, shift1, in_b, ffo_b, gain2, shift2,
+        ) = final_call(grad_own, got, out_sum, small_sum)
+        return (
+            layer_out, input_grad, query_w, query_b, key_w, value_w, value_b, depth_w, point_w, point_b, jnp.transpose(kernel_w),
+            kernel_b, conv_w, conv_b, out_w, out_b, gain1, shift1, jnp.transpose(in_w, (0, 2, 1)), in_b, ffo_w, ffo_b, gain2, shift2,
+        )
     start = (1 - branch) * 512
     block = lax.dynamic_slice_in_dim(grad_own, start, 256, 0) + got.astype(f32)
     input_grad = lax.dynamic_update_slice_in_dim(grad_own, block, start, 0)
-    share = 2 * dp_size // 32
     device = lax.axis_index("dp") * 2 + branch
 
     def piece(start, rows):

time: 198 us -> 179 us (0.904)
  local copies, waits for them, and re-layouts: 20.2 us -> 2.98 us
  other arithmetic: 3.14 us -> 0 us
  Pallas kernels: 173 us -> 175 us
    unnamed x20 -> x8, local copies, waits for them, and re-layouts: 9.85 us -> 2.98 us
    reshape x10 -> x0, local copies, waits for them, and re-layouts: 5.56 us -> none  [the longest x7 4.2 us: small(): return small_sum[row:row + -(-size // 384)].reshape(-1)[:size]]
    pallas_call x2 -> x3, Pallas kernels: 65.1 us -> 67.2 us  [the longest x1 38.9 us: ffn_call(): pl.pallas_call(ffn_kernel, out_shape=outs, in_specs=[VM] * len(operands),...]
where the time goes in v3:
time: 179 us
  Pallas kernels  175 us (98%)
  local copies, waits for them, and re-layouts  2.98 us (2%)
    pallas_call x1, Pallas kernels, comm_call(): pl.pallas_call(functools.partial(comm_kernel, dp_size), out_shape=(shape(...  70.8 us
    pallas_call x1, Pallas kernels, ffn_call(): pl.pallas_call(ffn_kernel, out_shape=outs, in_specs=[VM] * len(operands),...  38.9 us
    pallas_call x1, Pallas kernels, back_call(): pl.pallas_call(back_kernel, out_shape=outs, in_specs=[VM] * len(operands)...  37.4 us
    pallas_call x1, Pallas kernels, mix_call(): pl.pallas_call(mix_kernel, out_shape=outs, in_specs=[VM] * len(operands),...  26.3 us

profile of v3, /device:TPU:0, one launch (start us, length us, event | category | flops | bytes accessed | tf_op | source)
XLA Modules:
  0.0 179.2 jit_solution(14548802863343412583)
XLA Ops:
  0.7 26.3 %mix_forward.1 = (bf16[768,768]{1,0:T(8,128)(2,1)}, bf16[768,384]{1,0:T(8,128)(2,1)}, bf16[1024,384]{1,0:T(8,128)(2,1)}, bf16[1024,384]{1,0:T(8,128)(2,1)}, bf16...) custom-call(bf16[1536,768]{1,0:T(8,128)(2,1)} %hidden.5, ...), custom_call_target="tpu_custom_call" | custom-call | tf_op jit(solution)/shard_map/mix_forward/pallas_call | solution.py:241
  27.0 38.9 %ffn.1 = (bf16[768,768]{1,0:T(8,128)(2,1)}, f32[768,768]{1,0:T(8,128)}, bf16[768,768]{1,0:T(8,128)(2,1)}, bf16[32,240,384]{2,1,0:T(8,128)(2,1)}, f32[32,384]{1,0:T(8,128)}) custom-call(bf16[1536,768]{1,0:T(8,128)(2,1)} %hidden.5, bf16[768,768]{1,0:T(8,128)(2,1)} %get-tuple-element.71.joined, bf16[768,768]{1,0:T(8,128)(2,1)} %cotangent.1, ...), custom_call_target="tpu_custom_call" | custom-call | tf_op jit(solution)/shard_map/ffn/pallas_call | solution.py:383
  65.8 37.4 %mix_backward.1 = (f32[768,768]{1,0:T(8,128)}, bf16[256,768]{1,0:T(8,128)(2,1)}, bf16[32,144,384]{2,1,0:T(8,128)(2,1)}, f32[96,384]{1,0:T(8,128)}) custom-call(bf16[1536,768]{1,0:T(8,128)(2,1)} %hidden.5, bf16[768,768]{1,0:T(8,128)(2,1)} %get-tuple-element.73.joined_grad, f32[768,768]{1,0:T(8,128)} %get-tuple-element.74.residual_grad, ...), custom_call_target="tpu_custom_call" | custom-call | tf_op jit(solution)/shard_map/mix_backward/pallas_call | solution.py:558
  103.3 0.0 copy-start
  103.3 70.8 %grad_reduce.1 = (f32[384,384]{1,0:T(8,128)}, f32[128,384]{1,0:T(8,128)}, bf16[256,768]{1,0:T(8,128)(2,1)}) custom-call(bf16[32,240,384]{2,1,0:T(8,128)(2,1)} %get-tuple-element.87.g2, bf16[32,144,384]{2,1,0:T(8,128)(2,1)} %get-tuple-element.88.g3, f32[32,384]{1,0:T(8,128)} %get-tuple-element.89.s2, f32[96,384]{1,0:T(8,128)} %get-tuple-element.90.s3, ...), custom_call_target="tpu_custom_call" | custom-call | tf_op jit(solution)/shard_map/grad_reduce/pallas_call | solution.py:715
  174.1 0.0 copy-done
  174.1 0.0 copy-start.1
  174.1 1.1 copy-done.1
  175.2 0.0 copy-start.2
  175.2 1.0 copy-done.2
  176.2 0.0 copy-start.3
  176.2 0.9 copy-done.3
  177.1 2.0 %finish.1 = (f32[768,768]{1,0:T(8,128)}, f32[24,384]{1,0:T(8,128)}, f32[24,384]{1,0:T(8,128)}, f32[24,384]{1,0:T(8,128)}, f32[9,24]{1,0:T(8,128)}, /*index=5*/f3...) custom-call(f32[768,768]{1,0:T(8,128)S(1)} %copy-done, ...), custom_call_target="tpu_custom_call" | custom-call | tf_op jit(solution)/shard_map/finish/pallas_call | solution.py:774
Async XLA Ops:
  103.3 70.8 %copy-start = (f32[768,768]{1,0:T(8,128)S(1)}, f32[768,768]{1,0:T(8,128)}, u32[]{:S(2)}) copy-start(f32[768,768]{1,0:T(8,128)} %get-tuple-element.86.grad_own) | copy-start | bytes 7077892
  174.1 1.1 copy-start.1
  175.2 1.0 copy-start.2
  176.2 0.9 copy-start.3

commit v4 on v3

--- a/solution.py
+++ b/solution.py
@@ -185,7 +185,7 @@
         ext = aligned(e * TILE, TILE)
         x = hidden[aligned(base + e * TILE, TILE), :]
         q_pre = mm(x, query_w[...]) + vec(vecs, "query_bias")
-        query_pre[rows, :] = q_pre
+        query_pre[rows, :] = q_pre.astype(low_type)
         q = q_pre.astype(low_type).astype(f32) * 0.125
         q_out[rows, :] = q.astype(low_type)
         q_t = jnp.transpose(q).astype(low_type)
@@ -215,7 +215,7 @@
 
         depth_conv(x_pad, mask_cols, depth_weights, e * TILE, keep, False)
         kc = mm(depth_low[rows, :], point_w[...]) + vec(vecs, "pointwise_bias")
-        key_conv[rows, :] = kc
+        key_conv[rows, :] = kc.astype(low_type)
         attn = (kc * q_pre).astype(low_type)
         conv_attn[rows, :] = attn
         taps = taps_softmax(mm_nt(kernel_rows, attn) + kernel_bias)
@@ -235,7 +235,7 @@
     outs = (
         shape((768, 768), low_type), shape((768, WIDTH), low_type), shape((1024, WIDTH), low_type),
         shape((1024, WIDTH), low_type), shape((18, 512, TILE), low_type), shape((3, 1024 + 2 * PAD, 128), f32),
-        shape((72, 1024), f32), shape((72, 1024), f32), shape((768, WIDTH), f32), shape((768, WIDTH), f32),
+        shape((72, 1024), f32), shape((72, 1024), f32), shape((768, WIDTH), low_type), shape((768, WIDTH), low_type),
         shape((768, D), low_type), shape((768, WIDTH), low_type),
     )
     return pl.pallas_call(
@@ -393,13 +393,167 @@
     )(*operands)
 
 
+MESH = pl.DeviceIdType.MESH
+CHUNK = 48
+
+
+class Reducer:
+    def __init__(self, dp_size, sources, kept, kept_sem, buffer, out, send, recv):
+        self.bits = int(math.log2(dp_size)) + 1
+        self.extra = max(0, self.bits - 5)
+        self.nh = self.bits - self.extra
+        self.dp = lax.axis_index("dp")
+        self.br = lax.axis_index("branch")
+        self.my = [self.br] + [lax.rem(lax.div(self.dp, 1 << (k - 1)), 2) for k in range(1, self.bits)]
+        self.kept, self.kept_sem = kept, kept_sem
+        self.buffer, self.out, self.send, self.recv = buffer, out, send, recv
+        self.sources = [(ref, row) for ref in sources for row in range(0, ref.shape[1], CHUNK)]
+        halving = list(range(self.extra, self.bits))
+        first = [1] if 1 in halving else []
+        r = [k for k in halving if k not in first]
+        turns = [(0, 2, 1), (1, 2, 0), (0, 2, 1), (1, 2, 0), (2, 0, 1), (0, 2, 1), (1, 0, 2), (2, 1, 0)]
+        self.orders = [first + [r[t] for t in turn] + r[3:] for turn in turns]
+
+    def enter(self):
+        barrier = pltpu.get_barrier_semaphore()
+        for k in range(self.bits):
+            pl.semaphore_signal(barrier, inc=1, device_id=self.partner(k), device_id_type=MESH)
+        pl.semaphore_wait(barrier, self.bits)
+
+    def partner(self, k):
+        if k == 0:
+            return (self.dp, 1 - self.br)
+        return (self.dp + (1 << (k - 1)) * (1 - 2 * self.my[k]), self.br)
+
+    def copy(self, src, dst, ssem, rsem, k):
+        return pltpu.make_async_remote_copy(
+            src_ref=src, dst_ref=dst, send_sem=ssem, recv_sem=rsem, device_id=self.partner(k), device_id_type=MESH
+        )
+
+    def offset(self, s):
+        return sum(1 << (self.nh - 1 - t) for t in range(s))
+
+    def place(self, u, free, fixed, value):
+        index, at = 0, len(free) - 1
+        for k in sorted(free + [fixed], reverse=True):
+            if k == fixed:
+                index = index * 2 + value
+            else:
+                index = index * 2 + ((u >> at) & 1)
+                at -= 1
+        return index
+
+    def free(self, c, s):
+        return sorted(self.orders[c][s + 1 :], reverse=True)
+
+    def whole(self, c, s):
+        part = self.buffer.at[c, pl.ds(self.offset(s), 1 << (self.nh - 1 - s))]
+        return self.copy(part, part, self.send.at[c, s], self.recv.at[c, s], self.orders[c][s])
+
+    def start(self, c, s):
+        k, free = self.orders[c][s], self.free(c, s)
+        for u in range(1 << len(free)):
+            at = self.place(u, free, k, 1 - self.my[k])
+            if s == 0:
+                ref, row = self.sources[c]
+                src = ref.at[at, pl.ds(row, CHUNK)]
+            else:
+                src = self.buffer.at[c, self.offset(s - 1) + at]
+            self.copy(src, self.buffer.at[c, self.offset(s) + u], self.send.at[c, s], self.recv.at[c, s], k).start()
+
+    def fetch(self, c):
+        k, free = self.orders[c][0], self.free(c, 0)
+        ref, row = self.sources[c]
+        for u in range(1 << len(free)):
+            at = self.place(u, free, k, self.my[k])
+            pltpu.make_async_copy(ref.at[at, pl.ds(row, CHUNK)], self.kept.at[c, u], self.kept_sem.at[c]).start()
+
+    def add(self, c, s):
+        fetched = c < self.kept.shape[0]
+        if s == 0 and fetched:
+            pltpu.make_async_copy(self.kept.at[c], self.kept.at[c], self.kept_sem.at[c]).wait()
+        self.whole(c, s).wait_recv()
+        k, free = self.orders[c][s], self.free(c, s)
+        for u in range(1 << len(free)):
+            at = self.place(u, free, k, self.my[k])
+            if s == 0 and fetched:
+                mine = self.kept[c, u]
+            elif s == 0:
+                ref, row = self.sources[c]
+                mine = ref[at, row : row + CHUNK, :]
+            else:
+                mine = self.buffer[c, self.offset(s - 1) + at]
+            total = mine.astype(f32) + self.buffer[c, self.offset(s) + u].astype(f32)
+            if s == self.nh - 1:
+                self.out[c * CHUNK : (c + 1) * CHUNK, :] = total
+            else:
+                self.buffer[c, self.offset(s) + u] = total.astype(low_type)
+
+    def step(self, c, s):
+        if s > 0:
+            self.add(c, s - 1)
+        if s < self.nh:
+            self.start(c, s)
+
+    def drain(self):
+        for c in range(len(self.sources)):
+            for s in range(self.nh):
+                self.whole(c, s).wait_send()
+
+
+class Doubler:
+    def __init__(self, reducer, value, sent, got, send, recv):
+        self.reducer, self.value, self.sent, self.got, self.send, self.recv = reducer, value, sent, got, send, recv
+        self.order = reducer.orders[0] + list(range(reducer.extra))
+
+    def copy(self, s):
+        return self.reducer.copy(self.sent, self.got.at[s], self.send.at[s], self.recv.at[s], self.order[s])
+
+    def step(self, s):
+        if s > 0:
+            copy = self.copy(s - 1)
+            copy.wait()
+            self.value[...] = self.sent[...].astype(f32) + self.got[s - 1].astype(f32)
+        if s < len(self.order):
+            self.sent[...] = self.value[...].astype(self.sent.dtype)
+            self.copy(s).start()
+
+
 def back_kernel(
-    hidden, joined_grad, residual_grad, q_in, k_in, v_in, probs, conv_pad, taps, tap_mask, query_pre, key_conv, depth_low,
-    conv_attn, query_w, key_w, value_w, point_w, conv_w, depth_w, kernel_w,
-    grad_own, grad_other, units, small,
+    dp_size, hidden, joined_grad, residual_grad, q_in, k_in, v_in, probs, conv_pad, taps, tap_mask, query_pre, key_conv, depth_low,
+    conv_attn, units2, small2, query_w, key_w, value_w, point_w, conv_w, depth_w, kernel_w,
+    grad_own, got_other, out, sum2, sum3,
     dk_acc, dv_acc, k_t, dq_low, kvc, key_conv_low, dg_pad, cg_pad, x_pad, mask_cols, dw_acc, dq_t, kernel_acc, bias_acc, moved_taps, part,
-    sums,
+    sums, grad_other, units, small, buffer, sent2, got2, sent3, got3, extra_got,
+    send, recv, send2, recv2, send3, recv3, other_sem, extra_sem, kept, kept_sem,
 ):
+    reducer = Reducer(dp_size, (units2, units), kept, kept_sem, buffer, out, send, recv)
+    nh, bits, extra = reducer.nh, reducer.bits, reducer.extra
+    early, late = Doubler(reducer, sum2, sent2, got2, send2, recv2), Doubler(reducer, sum3, sent3, got3, send3, recv3)
+    other_copy = reducer.copy(grad_other, got_other, other_sem.at[0], other_sem.at[1], 0)
+    for c in range(5):
+        reducer.fetch(c)
+    reducer.enter()
+    for c in range(5):
+        reducer.step(c, 0)
+    sum2[...] = small2[...]
+    early.step(0)
+    starts = (0, 0, 1, 1, 2)
+
+    def advance(point):
+        for c in range(5):
+            s = point + 1 - starts[c]
+            if 1 <= s <= nh:
+                reducer.step(c, s)
+        if 1 <= point + 1 <= bits:
+            early.step(point + 1)
+
+    def advance_at(i, half):
+        for n in range(3):
+            @pl.when(i == n)
+            def _():
+                advance(2 * n + half)
+
     b = lax.axis_index("branch")
     base = b * 512
     for ref in (dk_acc, dv_acc, dg_pad, cg_pad, dw_acc, kernel_acc, bias_acc, sums):
@@ -456,6 +610,7 @@
             d_both = jnp.concatenate([half_lanes(d_pair, 0), half_lanes(d_pair, 1)], axis=0)
             dk_acc[keys, lanes] += mm(jnp.concatenate(scores, axis=1), q_both)
             dv_acc[keys, lanes] += mm(jnp.concatenate(weights, axis=1), d_both)
+        advance_at(i, 0)
         query_low = (jnp.transpose(dq_t[...]) * 0.125).astype(low_type)
 
         grad = joined_grad[rows, WIDTH : 2 * WIDTH].astype(f32)
@@ -476,8 +631,8 @@
         kernel_acc[...] += mm(logit_low, conv_attn[rows, :])
         bias_acc[...] += logit_wide[:, :128] + logit_wide[:, 128:]
         span = mm(jnp.transpose(logit_wide).astype(low_type), kernel_rows).astype(low_type).astype(f32)
-        point_low = (span * query_pre[rows, :]).astype(low_type)
-        query_conv = (span * key_conv[rows, :]).astype(low_type)
+        point_low = (span * query_pre[rows, :].astype(f32)).astype(low_type)
+        query_conv = (span * key_conv[rows, :].astype(f32)).astype(low_type)
         key_conv_low[rows, :] = point_low
         sums[2] += fold_rows(point_low.astype(f32))
         both = query_low.astype(f32) + query_conv.astype(f32)
@@ -499,35 +654,40 @@
                     totals[j] = term if lo == 0 else totals[j] + term
             for j in range(KERNEL):
                 dw_acc[j, :, c * 128 : c * 128 + 128] += totals[j]
+        advance_at(i, 1)
         return carry
 
     lax.fori_loop(0, 3, own, 0)
 
-    def spread(e):
+    def span_grads(e):
         ext = aligned(e * TILE, TILE)
-        dk = dk_acc[ext, :].astype(low_type)
         dv = dv_acc[ext, :].astype(low_type)
         dc = span_conv(cg_pad, moved_taps[ext, :], e * TILE).astype(low_type)
-        kvc[ext, 0:WIDTH] = dk
+        kvc[ext, 0:WIDTH] = dk_acc[ext, :].astype(low_type)
         kvc[ext, WIDTH : 2 * WIDTH] = dv
         kvc[ext, 2 * WIDTH : 3 * WIDTH] = dc
         sums[1] += fold_rows(dv.astype(f32))
         sums[3] += fold_rows(dc.astype(f32))
+
+    def input_part(e):
+        ext = aligned(e * TILE, TILE)
         mask_cols[...] = mm(jnp.transpose(tap_mask[:, ext]).astype(low_type), tap_spread())
 
         def keep(c, lo, value):
             part[lo : lo + 64, c * 128 : c * 128 + 128] = value
 
         depth_conv(dg_pad, mask_cols, depth_weights, e * TILE, keep, True)
-        return part[...] + mm_nt(dk, key_w[...]) + mm_nt(dv, value_w[...]) + mm_nt(dc, conv_w[...])
-
-    def finish(i, carry):
-        rows = aligned(i * TILE, TILE)
-        grad_own[rows, :] = spread(b + i) + mm_nt(dq_low[rows, :], query_w[...]) + residual_grad[rows, :]
+        pieces = [kvc[ext, k * WIDTH : (k + 1) * WIDTH] for k in range(3)]
+        return part[...] + mm_nt(pieces[0], key_w[...]) + mm_nt(pieces[1], value_w[...]) + mm_nt(pieces[2], conv_w[...])
+
+    def spans(i, carry):
+        span_grads(i)
         return carry
 
-    lax.fori_loop(0, 3, finish, 0)
-    grad_other[...] = spread(3 * (1 - b)).astype(low_type)
+    lax.fori_loop(0, 4, spans, 0)
+    grad_other[...] = input_part(3 * (1 - b)).astype(low_type)
+    other_copy.start()
+    advance(6)
 
     depth_total = jnp.sum(dw_acc[...], axis=1)
     depth_t = jnp.transpose(jnp.concatenate([depth_total, jnp.zeros((128 - KERNEL, D), f32)], axis=0))
@@ -548,15 +708,51 @@
         small[72 + k : 73 + k, :] = jnp.sum(sums[k], axis=0, keepdims=True)
     column = jnp.concatenate([bias_acc[...], jnp.zeros((56, 128), f32)], axis=0)
     small[76:77, 0:128] = jnp.sum(jnp.transpose(column), axis=0, keepdims=True)
-
-
-def back_call(hidden, joined_grad, residual_grad, saved, weights):
+    for c in range(5, 8):
+        reducer.step(c, 0)
+    sum3[...] = small[...]
+    late.step(0)
+
+    def finish(i, carry):
+        rows = aligned(i * TILE, TILE)
+        grad_own[rows, :] = input_part(b + i) + mm_nt(dq_low[rows, :], query_w[...]) + residual_grad[rows, :]
+        for n in range(3):
+            @pl.when(i == n)
+            def _():
+                for c in range(5, 8):
+                    reducer.step(c, n + 1)
+                late.step(n + 1)
+        return carry
+
+    lax.fori_loop(0, 3, finish, 0)
+    for s in range(4, nh + 1):
+        for c in range(5, 8):
+            reducer.step(c, s)
+        late.step(s)
+    for s in range(8, bits + 1):
+        early.step(s)
+    for s in range(nh + 1, bits + 1):
+        late.step(s)
+    for k in range(extra):
+        copy = reducer.copy(out, extra_got.at[k], extra_sem.at[2 * k], extra_sem.at[2 * k + 1], k)
+        copy.start()
+        copy.wait()
+        out[...] = out[...] + extra_got[k]
+    reducer.drain()
+    other_copy.wait()
+
+
+def back_call(dp_size, hidden, joined_grad, residual_grad, saved, units2, small2, weights):
     shape = jax.ShapeDtypeStruct
-    outs = (shape((768, D), f32), shape((256, D), low_type), shape((32, 144, 384), low_type), shape((96, 384), f32))
-    operands = (hidden, joined_grad, residual_grad) + tuple(saved) + tuple(weights)
+    outs = (shape((768, D), f32), shape((256, D), low_type), shape((384, 384), f32), shape(small2.shape, f32), shape((96, 384), f32))
+    operands = (hidden, joined_grad, residual_grad) + tuple(saved) + (units2, small2) + tuple(weights)
     ext = 1024 + 2 * PAD
+    bits = int(math.log2(dp_size)) + 1
+    extra = max(0, bits - 5)
+    nh = bits - extra
+    dma = pltpu.SemaphoreType.DMA
     return pl.pallas_call(
-        back_kernel, out_shape=outs, in_specs=[VM] * len(operands), out_specs=(VM,) * len(outs),
+        functools.partial(back_kernel, dp_size), out_shape=outs, in_specs=[VM] * 14 + [pl.BlockSpec(memory_space=pl.ANY)] + [VM] * (len(operands) - 15), out_specs=(VM,) * len(outs),
         scratch_shapes=[
             pltpu.VMEM((1024, WIDTH), f32), pltpu.VMEM((1024, WIDTH), f32), pltpu.VMEM((WIDTH, 1024), low_type),
             pltpu.VMEM((768, WIDTH), low_type), pltpu.VMEM((1024, 3 * WIDTH), low_type), pltpu.VMEM((768, WIDTH), low_type),
@@ -564,169 +760,17 @@
             pltpu.VMEM((TILE, KERNEL * 128), f32), pltpu.VMEM((KERNEL, 8, D), f32), pltpu.VMEM((WIDTH, TILE), f32),
             pltpu.VMEM((72, WIDTH), f32), pltpu.VMEM((72, 128), f32), pltpu.VMEM((1024, 72), low_type), pltpu.VMEM((TILE, D), f32),
             pltpu.VMEM((4, 8, WIDTH), f32),
+            pltpu.VMEM((256, D), low_type), pltpu.VMEM((32, 144, 384), low_type), pltpu.VMEM((96, 384), f32),
+            pltpu.VMEM((8, (1 << nh) - 1, CHUNK, 384), low_type),
+            pltpu.VMEM(small2.shape, f32), pltpu.VMEM((bits,) + small2.shape, f32),
+            pltpu.VMEM((96, 384), low_type), pltpu.VMEM((bits, 96, 384), low_type),
+            pltpu.VMEM((max(extra, 1), 384 if extra else 8, 384), f32),
+            dma((8, nh)), dma((8, nh)), dma((bits,)), dma((bits,)), dma((bits,)), dma((bits,)), dma((2,)), dma((max(2 * extra, 2),)),
+            pltpu.VMEM((5, 1 << (nh - 1), CHUNK, 384), low_type), dma((5,)),
         ],
-        compiler_params=pltpu.CompilerParams(vmem_limit_bytes=60 << 20),
-        name="mix_backward",
+        compiler_params=pltpu.CompilerParams(collective_id=0, has_side_effects=True, vmem_limit_bytes=67_000_000),
+        name="mix_backward_reduce",
     )(*operands)
-
-
-MESH = pl.DeviceIdType.MESH
-CHUNK = 48
-
-
-def comm_orders(bits, extra):
-    halving = list(range(extra, bits))
-    first = [1] if 1 in halving else []
-    rest = [k for k in halving if k not in first]
-    a = [rest[0], rest[2], rest[1]] + rest[3:]
-    b = [rest[1], rest[2], rest[0]] + rest[3:]
-    return first + a, first + b
-
-
-def comm_kernel(dp_size, g2, g3, s2, s3, other, out, s_out, got, rb, srb, erb, send, recv, ssend, srecv, esend, erecv, osem):
-    bits = int(math.log2(dp_size)) + 1
-    extra = max(0, bits - 5)
-    orders = comm_orders(bits, extra)
-    nh = bits - extra
-    dp = lax.axis_index("dp")
-    br = lax.axis_index("branch")
-    my = [br] + [lax.rem(lax.div(dp, 1 << (k - 1)), 2) for k in range(1, bits)]
-    chunks2 = g2.shape[-2] // CHUNK
-    n_chunks = chunks2 + g3.shape[-2] // CHUNK
-
-    def partner(k):
-        if k == 0:
-            return (dp, 1 - br)
-        return (dp + (1 << (k - 1)) * (1 - 2 * my[k]), br)
-
-    barrier = pltpu.get_barrier_semaphore()
-    for k in range(bits):
-        pl.semaphore_signal(barrier, inc=1, device_id=partner(k), device_id_type=MESH)
-    pl.semaphore_wait(barrier, bits)
-
-    def copy(src, dst, ssem, rsem, k):
-        return pltpu.make_async_remote_copy(
-            src_ref=src, dst_ref=dst, send_sem=ssem, recv_sem=rsem, device_id=partner(k), device_id_type=MESH
-        )
-
-    def offset(s):
-        return sum(1 << (nh - 1 - t) for t in range(s))
-
-    def source(c):
-        return (g2, c * CHUNK) if c < chunks2 else (g3, (c - chunks2) * CHUNK)
-
-    def place(u, free, fixed):
-        names = sorted(free + list(fixed), reverse=True)
-        index, at = 0, len(free) - 1
-        for k in names:
-            if k in fixed:
-                value = fixed[k]
-            else:
-                value = (u >> at) & 1
-                at -= 1
-            index = index * 2 + value
-        return index
-
-    waits = {}
-
-    def free_bits(order, s):
-        return sorted(set(order[s:]), reverse=True)
-
-    def start(c, s, order):
-        k = order[s]
-        free = free_bits(order, s + 1)
-        count = 1 << len(free)
-        for u in range(count):
-            at = place(u, free, {k: 1 - my[k]})
-            if s == 0:
-                ref, row = source(c)
-                src = ref.at[at, pl.ds(row, CHUNK)]
-            else:
-                src = rb.at[c, offset(s - 1) + at]
-            copy(src, rb.at[c, offset(s) + u], send.at[c, s], recv.at[c, s], k).start()
-        whole = rb.at[c, pl.ds(offset(s), count)]
-        waits[(c, s)] = copy(whole, whole, send.at[c, s], recv.at[c, s], k)
-
-    def add(c, s, order):
-        waits[(c, s)].wait_recv()
-        k = order[s]
-        free = free_bits(order, s + 1)
-        for u in range(1 << len(free)):
-            at = place(u, free, {k: my[k]})
-            if s == 0:
-                ref, row = source(c)
-                mine = ref[at, row : row + CHUNK, :]
-            else:
-                mine = rb[c, offset(s - 1) + at]
-            total = mine.astype(jnp.float32) + rb[c, offset(s) + u].astype(jnp.float32)
-            if s == nh - 1:
-                out[c * CHUNK : (c + 1) * CHUNK, :] = total
-            else:
-                rb[c, offset(s) + u] = total.astype(rb.dtype)
-
-    small_order = orders[0] + list(range(extra))
-
-    def small_start(s):
-        cp = copy(s_out, srb.at[s], ssend.at[s], srecv.at[s], small_order[s])
-        cp.start()
-        waits[("s", s)] = cp
-
-    def small_add(s):
-        waits[("s", s)].wait()
-        s_out[...] = s_out[...] + srb[s]
-
-    other_copy = copy(other, got, osem.at[0], osem.at[1], 0)
-    other_copy.start()
-    s_out[0 : s3.shape[0], :] = s3[...]
-    s_out[s3.shape[0] :, :] = s2[...]
-    half = n_chunks // 2
-    for w in range(max(half + nh, bits + 1)):
-        for p in range(half - 1, -1, -1):
-            s = w - p
-            for c, order in ((2 * p, orders[0]), (2 * p + 1, orders[1])):
-                if 1 <= s <= nh:
-                    add(c, s - 1, order)
-                if 0 <= s < nh:
-                    start(c, s, order)
-        if 1 <= w <= bits:
-            small_add(w - 1)
-        if w < bits:
-            small_start(w)
-    for k in range(extra):
-        cp = copy(out, erb.at[k], esend.at[k], erecv.at[k], k)
-        cp.start()
-        cp.wait()
-        out[...] = out[...] + erb[k]
-    for c in range(n_chunks):
-        for s in range(nh):
-            waits[(c, s)].wait_send()
-    other_copy.wait()
-
-
-def comm_call(dp_size, g2, g3, s2, s3, other):
-    bits = int(math.log2(dp_size)) + 1
-    extra = max(0, bits - 5)
-    nh = bits - extra
-    rows = g2.shape[1] + g3.shape[1]
-    n_chunks = rows // CHUNK
-    shape = jax.ShapeDtypeStruct
-    small_shape = (s2.shape[0] + s3.shape[0], 384)
-    dma = pltpu.SemaphoreType.DMA
-    return pl.pallas_call(
-        functools.partial(comm_kernel, dp_size),
-        out_shape=(shape((rows, 384), jnp.float32), shape(small_shape, jnp.float32), shape(other.shape, other.dtype)),
-        in_specs=[VM] * 5,
-        out_specs=(VM, VM, VM),
-        scratch_shapes=[
-            pltpu.VMEM((n_chunks, (1 << nh) - 1, CHUNK, 384), jnp.bfloat16),
-            pltpu.VMEM((bits,) + small_shape, jnp.float32),
-            pltpu.VMEM((max(extra, 1), rows if extra else 8, 384), jnp.float32),
-            dma((n_chunks, nh)), dma((n_chunks, nh)), dma((bits,)), dma((bits,)),
-            dma((max(extra, 1),)), dma((max(extra, 1),)), dma((2,)),
-        ],
-        compiler_params=pltpu.CompilerParams(collective_id=0, has_side_effects=True, vmem_limit_bytes=60 << 20),
-        name="grad_reduce",
-    )(g2, g3, s2, s3, other)
 
 
 def exact_columns(table, rows):
@@ -740,7 +784,7 @@
 
 
 def final_kernel(
-    grad_own, got, total, small,
+    grad_own, got, total, small2, small3,
     input_grad, query_w, key_w, value_w, depth_w, point_w, kernel_w, kernel_b, conv_w, out_w, in_w, ffo_w, *vectors,
 ):
     b = lax.axis_index("branch")
@@ -758,23 +802,24 @@
     depth = jnp.concatenate([total[360:384, 0:128], jnp.zeros((104, 128), f32)], axis=0)
     depth_w[...] = jnp.transpose(depth)[0:KERNEL, 0:24]
     table = tap_permutation()
-    kernel_w[...] = exact_columns(table, small[0:72, :])
-    column = jnp.transpose(jnp.concatenate([small[76:77, 0:128]] * 128, axis=0))[0:72, :]
+    kernel_w[...] = exact_columns(table, small3[0:72, :])
+    column = jnp.transpose(jnp.concatenate([small3[76:77, 0:128]] * 128, axis=0))[0:72, :]
     kernel_b[...] = jnp.sum(column[:, 0:54] * table, axis=0, keepdims=True).reshape(54)
     for ref, (_, row, size) in zip(vectors, FINAL_SMALL):
+        small, row = (small3, row) if row < 96 else (small2, row - 96)
         ref[...] = jnp.concatenate([small[row + k : row + k + 1, :] for k in range(size // 384)], axis=1).reshape(size)
 
 
-def final_call(grad_own, got, total, small):
+def final_call(*operands):
     shape = lambda *s: jax.ShapeDtypeStruct(s, f32)
     outs = (
         shape(768, D), shape(24, 384), shape(24, 384), shape(24, 384), shape(KERNEL, 24), shape(24, 384), shape(54, 384), shape(54),
         shape(24, 384), shape(24, 768), shape(2, 48, 384), shape(2, 48, 384),
     ) + tuple(shape(size) for _, _, size in FINAL_SMALL)
     return pl.pallas_call(
-        final_kernel, out_shape=outs, in_specs=[VM] * 4, out_specs=(VM,) * len(outs),
+        final_kernel, out_shape=outs, in_specs=[VM] * 5, out_specs=(VM,) * len(outs),
         compiler_params=pltpu.CompilerParams(vmem_limit_bytes=32 << 20), name="finish",
-    )(grad_own, got, total, small)
+    )(*operands)
 
 
 def local(
@@ -794,21 +839,21 @@
         hidden, joined, cotangent, output_weight, ffn_in_weight, ffn_out_weight, output_bias, norm1_gain, norm1_shift,
         ffn_in_bias, ffn_out_bias, norm2_gain, norm2_shift,
     )
-    grad_own, grad_other, units3, small3 = back_call(
-        hidden, joined_grad, residual_grad, saved,
+    grad_own, got, out_sum, sum2, sum3 = back_call(
+        dp_size, hidden, joined_grad, residual_grad, saved, units2, small2,
         (query_weight, key_weight, value_weight, pointwise_weight, conv_value_weight, depthwise_weight, kernel_rows),
     )
-    out_sum, small_sum, got = comm_call(dp_size, units2, units3, small2, small3, grad_other)
     share = 2 * dp_size // 32
     if share == 1:
         (
             input_grad, query_w, key_w, value_w, depth_w, point_w, kernel_w, kernel_b, conv_w, out_w, in_w, ffo_w,
             query_b, value_b, point_b, conv_b, out_b, gain1, shift1, in_b, ffo_b, gain2, shift2,
-        ) = final_call(grad_own, got, out_sum, small_sum)
+        ) = final_call(grad_own, got, out_sum, sum2, sum3)
         return (
             layer_out, input_grad, query_w, query_b, key_w, value_w, value_b, depth_w, point_w, point_b, jnp.transpose(kernel_w),
             kernel_b, conv_w, conv_b, out_w, out_b, gain1, shift1, jnp.transpose(in_w, (0, 2, 1)), in_b, ffo_w, ffo_b, gain2, shift2,
         )
+    small_sum = jnp.concatenate([sum3, sum2])
     start = (1 - branch) * 512
     block = lax.dynamic_slice_in_dim(grad_own, start, 256, 0) + got.astype(f32)
     input_grad = lax.dynamic_update_slice_in_dim(grad_own, block, start, 0)

time: 179 us -> 168 us (0.939)
  Pallas kernels: 175 us -> 162 us
  local copies, waits for them, and re-layouts: 2.98 us -> 5.42 us
    pallas_call x3 -> x2, Pallas kernels: 110 us -> 96.9 us  [the longest x1 95 us: back_call(): pl.pallas_call(functools.partial(back_kernel, dp_size), out_shape=outs, i...]
    unnamed x8 -> x10, local copies, waits for them, and re-layouts: 2.98 us -> 5.42 us
where the time goes in v4:
time: 168 us
  Pallas kernels  162 us (96%)
  local copies, waits for them, and re-layouts  5.42 us (3%)
    pallas_call x1, Pallas kernels, back_call(): pl.pallas_call(functools.partial(back_kernel, dp_size), out_shape=outs, i...  95 us
    pallas_call x1, Pallas kernels, ffn_call(): pl.pallas_call(ffn_kernel, out_shape=outs, in_specs=[VM] * len(operands),...  38.9 us
    pallas_call x1, Pallas kernels, mix_call(): pl.pallas_call(mix_kernel, out_shape=outs, in_specs=[VM] * len(operands),...  25.8 us
    unnamed x10, local copies, waits for them, and re-layouts  5.42 us

profile of v4, /device:TPU:0, one launch (start us, length us, event | category | flops | bytes accessed | tf_op | source)
XLA Modules:
  0.0 167.9 jit_solution(15642970192980626016)
XLA Ops:
  0.7 25.8 %mix_forward.1 = (bf16[768,768]{1,0:T(8,128)(2,1)}, bf16[768,384]{1,0:T(8,128)(2,1)}, bf16[1024,384]{1,0:T(8,128)(2,1)}, bf16[1024,384]{1,0:T(8,128)(2,1)}, bf16...) custom-call(bf16[1536,768]{1,0:T(8,128)(2,1)} %hidden.5, ...), custom_call_target="tpu_custom_call" | custom-call | tf_op jit(solution)/shard_map/mix_forward/pallas_call | solution.py:241
  26.5 38.9 %ffn.1 = (bf16[768,768]{1,0:T(8,128)(2,1)}, f32[768,768]{1,0:T(8,128)}, bf16[768,768]{1,0:T(8,128)(2,1)}, bf16[32,240,384]{2,1,0:T(8,128)(2,1)}, f32[32,384]{1,0:T(8,128)}) custom-call(bf16[1536,768]{1,0:T(8,128)(2,1)} %hidden.5, bf16[768,768]{1,0:T(8,128)(2,1)} %get-tuple-element.69.joined, bf16[768,768]{1,0:T(8,128)(2,1)} %cotangent.1, ...), custom_call_target="tpu_custom_call" | custom-call | tf_op jit(solution)/shard_map/ffn/pallas_call | solution.py:383
  65.3 95.0 %mix_backward_reduce.1 = (f32[768,768]{1,0:T(8,128)}, bf16[256,768]{1,0:T(8,128)(2,1)}, f32[384,384]{1,0:T(8,128)}, f32[32,384]{1,0:T(8,128)}, f32[96,384]{1,0:T(8,128)}) custom-call(bf16[1536,768]{1,0:T(8,128)(2,1)} %hidden.5, bf16[768,768]{1,0:T(8,128)(2,1)} %get-tuple-element.71.joined_grad, f32[768,768]{1,0:T(8,128)} %get-tuple-element.72.residual_grad, ...), custom_call_target="tpu_custom_call" | custom-call | tf_op jit(solution)/shard_map/mix_backward_reduce/pallas_call | solution.py:754
  160.3 0.0 copy-start
  160.3 1.7 copy-done
  162.0 0.0 copy-start.1
  162.0 1.1 copy-done.1
  163.0 0.0 copy-start.2
  163.0 1.0 copy-done.2
  164.0 0.0 copy-start.3
  164.0 0.9 copy-done.3
  164.9 0.0 copy-start.4
  164.9 0.8 copy-done.4
  165.7 2.0 %finish.1 = (f32[768,768]{1,0:T(8,128)}, f32[24,384]{1,0:T(8,128)}, f32[24,384]{1,0:T(8,128)}, f32[24,384]{1,0:T(8,128)}, f32[9,24]{1,0:T(8,128)}, /*index=5*/f3...) custom-call(f32[768,768]{1,0:T(8,128)S(1)} %copy-done, ...), custom_call_target="tpu_custom_call" | custom-call | tf_op jit(solution)/shard_map/finish/pallas_call | solution.py:819
Async XLA Ops:
  160.3 1.7 copy-start
  162.0 1.1 copy-start.1
  163.0 1.0 copy-start.2
  164.0 0.9 copy-start.3
  164.9 0.8 copy-start.4

commit v5 on v4

--- a/solution.py
+++ b/solution.py
@@ -411,7 +411,7 @@
         halving = list(range(self.extra, self.bits))
         first = [1] if 1 in halving else []
         r = [k for k in halving if k not in first]
-        turns = [(0, 2, 1), (1, 2, 0), (0, 2, 1), (1, 2, 0), (2, 0, 1), (0, 2, 1), (1, 0, 2), (2, 1, 0)]
+        turns = [(0, 2, 1), (1, 2, 0), (0, 2, 1), (1, 2, 0), (2, 0, 1), (0, 2, 1), (1, 2, 0), (2, 1, 0)]
         self.orders = [first + [r[t] for t in turn] + r[3:] for turn in turns]
 
     def enter(self):
@@ -519,40 +519,44 @@
             self.copy(s).start()
 
 
+EARLY_STEPS = {
+    (0, 1): [(0, 1), (1, 1)],
+    (0, 2): [(2, 1), (3, 1)],
+    (0, 3): [(4, 1)],
+    (1, 1): [(0, 2), (1, 2)],
+    (1, 3): [(2, 2), (3, 2), (4, 2)],
+    (2, 2): [(0, 3), (1, 3), (4, 3)],
+    (2, 3): [(0, 4), (1, 4), (4, 4)],
+}
+
+
 def back_kernel(
     dp_size, hidden, joined_grad, residual_grad, q_in, k_in, v_in, probs, conv_pad, taps, tap_mask, query_pre, key_conv, depth_low,
     conv_attn, units2, small2, query_w, key_w, value_w, point_w, conv_w, depth_w, kernel_w,
-    grad_own, got_other, out, sum2, sum3,
+    grad_own, got_other, out, small_sum,
     dk_acc, dv_acc, k_t, dq_low, kvc, key_conv_low, dg_pad, cg_pad, x_pad, mask_cols, dw_acc, dq_t, kernel_acc, bias_acc, moved_taps, part,
-    sums, grad_other, units, small, buffer, sent2, got2, sent3, got3, extra_got,
-    send, recv, send2, recv2, send3, recv3, other_sem, extra_sem, kept, kept_sem,
+    sums, grad_other, units, buffer, sent3, got3, extra_got,
+    send, recv, send3, recv3, other_sem, extra_sem, kept, kept_sem,
 ):
     reducer = Reducer(dp_size, (units2, units), kept, kept_sem, buffer, out, send, recv)
     nh, bits, extra = reducer.nh, reducer.bits, reducer.extra
-    early, late = Doubler(reducer, sum2, sent2, got2, send2, recv2), Doubler(reducer, sum3, sent3, got3, send3, recv3)
+    late = Doubler(reducer, small_sum, sent3, got3, send3, recv3)
     other_copy = reducer.copy(grad_other, got_other, other_sem.at[0], other_sem.at[1], 0)
     for c in range(5):
         reducer.fetch(c)
     reducer.enter()
     for c in range(5):
         reducer.step(c, 0)
-    sum2[...] = small2[...]
-    early.step(0)
-    starts = (0, 0, 1, 1, 2)
-
-    def advance(point):
-        for c in range(5):
-            s = point + 1 - starts[c]
-            if 1 <= s <= nh:
-                reducer.step(c, s)
-        if 1 <= point + 1 <= bits:
-            early.step(point + 1)
-
-    def advance_at(i, half):
-        for n in range(3):
-            @pl.when(i == n)
-            def _():
-                advance(2 * n + half)
+    def run(steps):
+        for c, stage in steps:
+            reducer.step(c, stage)
+
+    def advance_at(i, spot):
+        for (n, at), steps in EARLY_STEPS.items():
+            if at == spot:
+                @pl.when(i == n)
+                def _(steps=steps):
+                    run(steps)
 
     b = lax.axis_index("branch")
     base = b * 512
@@ -610,7 +614,7 @@
             d_both = jnp.concatenate([half_lanes(d_pair, 0), half_lanes(d_pair, 1)], axis=0)
             dk_acc[keys, lanes] += mm(jnp.concatenate(scores, axis=1), q_both)
             dv_acc[keys, lanes] += mm(jnp.concatenate(weights, axis=1), d_both)
-        advance_at(i, 0)
+            advance_at(i, p)
         query_low = (jnp.transpose(dq_t[...]) * 0.125).astype(low_type)
 
         grad = joined_grad[rows, WIDTH : 2 * WIDTH].astype(f32)
@@ -654,21 +658,64 @@
                     totals[j] = term if lo == 0 else totals[j] + term
             for j in range(KERNEL):
                 dw_acc[j, :, c * 128 : c * 128 + 128] += totals[j]
-        advance_at(i, 1)
+        advance_at(i, 3)
         return carry
 
     lax.fori_loop(0, 3, own, 0)
 
-    def span_grads(e):
+    def settle(e, carry):
         ext = aligned(e * TILE, TILE)
         dv = dv_acc[ext, :].astype(low_type)
-        dc = span_conv(cg_pad, moved_taps[ext, :], e * TILE).astype(low_type)
         kvc[ext, 0:WIDTH] = dk_acc[ext, :].astype(low_type)
         kvc[ext, WIDTH : 2 * WIDTH] = dv
+        sums[1] += fold_rows(dv.astype(f32))
+        return carry
+
+    def pack(k, first, second):
+        for m in range(2):
+            lanes = slice(m * 384, m * 384 + 384)
+            pieces = [part_of(lanes).reshape(16, 24, 384) for part_of in (first, second)]
+            units[m * 16 : m * 16 + 16, k * 48 : k * 48 + 48, :] = jnp.concatenate(pieces, axis=1).astype(low_type)
+
+    def token_grad(k):
+        return lambda lanes: mm_tn(hidden[aligned(base, 512), lanes], kvc[0:512, k * WIDTH : (k + 1) * WIDTH]) + mm_tn(
+            hidden[aligned(base + 512, 512), lanes], kvc[512:1024, k * WIDTH : (k + 1) * WIDTH]
+        )
+
+    lax.fori_loop(0, 4, settle, 0)
+    own_tokens = pl.ds(pl.multiple_of(b * 768, 256), 768)
+    pack(0, lambda lanes: mm_tn(hidden[own_tokens, lanes], dq_low[...]), token_grad(0))
+    run([(5, 0), (2, 3), (3, 3)])
+    depth_total = jnp.sum(dw_acc[...], axis=1)
+    depth_t = jnp.transpose(jnp.concatenate([depth_total, jnp.zeros((128 - KERNEL, D), f32)], axis=0))
+    pack(
+        2,
+        lambda lanes: mm_tn(depth_low[:, lanes], key_conv_low[...]),
+        lambda lanes: jnp.concatenate([depth_t[lanes], jnp.zeros((384, 256), f32)], axis=1),
+    )
+    run([(7, 0)])
+
+    def spans(e, carry):
+        ext = aligned(e * TILE, TILE)
+        dc = span_conv(cg_pad, moved_taps[ext, :], e * TILE).astype(low_type)
         kvc[ext, 2 * WIDTH : 3 * WIDTH] = dc
-        sums[1] += fold_rows(dv.astype(f32))
         sums[3] += fold_rows(dc.astype(f32))
-
+        return carry
+
+    lax.fori_loop(0, 4, spans, 0)
+    run([(2, 4), (3, 4), (0, 5), (1, 5), (4, 5)])
+    small_sum[...] = jnp.zeros_like(small_sum)
+    small_sum[0:72, :] = kernel_acc[...]
+    for k in range(4):
+        small_sum[72 + k : 73 + k, :] = jnp.sum(sums[k], axis=0, keepdims=True)
+    column = jnp.concatenate([bias_acc[...], jnp.zeros((56, 128), f32)], axis=0)
+    small_sum[76:77, 0:128] = jnp.sum(jnp.transpose(column), axis=0, keepdims=True)
+    small_sum[80:104, :] = small2[0:24, :]
+    late.step(0)
+    run([(5, 1), (7, 1)])
+    pack(1, token_grad(1), token_grad(2))
+    run([(6, 0)])
+    late.step(1)
     def input_part(e):
         ext = aligned(e * TILE, TILE)
         mask_cols[...] = mm(jnp.transpose(tap_mask[:, ext]).astype(low_type), tap_spread())
@@ -680,58 +727,23 @@
         pieces = [kvc[ext, k * WIDTH : (k + 1) * WIDTH] for k in range(3)]
         return part[...] + mm_nt(pieces[0], key_w[...]) + mm_nt(pieces[1], value_w[...]) + mm_nt(pieces[2], conv_w[...])
 
-    def spans(i, carry):
-        span_grads(i)
-        return carry
-
-    lax.fori_loop(0, 4, spans, 0)
     grad_other[...] = input_part(3 * (1 - b)).astype(low_type)
+    run([(6, 1), (2, 5), (3, 5)])
     other_copy.start()
-    advance(6)
-
-    depth_total = jnp.sum(dw_acc[...], axis=1)
-    depth_t = jnp.transpose(jnp.concatenate([depth_total, jnp.zeros((128 - KERNEL, D), f32)], axis=0))
-    for m in range(2):
-        lanes = slice(m * 384, m * 384 + 384)
-        group = slice(m * 16, m * 16 + 16)
-        grad_kvc = mm_tn(hidden[aligned(base, 512), lanes], kvc[0:512, :]) + mm_tn(hidden[aligned(base + 512, 512), lanes], kvc[512:1024, :])
-        grad_q = mm_tn(hidden[pl.ds(pl.multiple_of(b * 768, 256), 768), lanes], dq_low[...])
-        grad_p = mm_tn(depth_low[:, lanes], key_conv_low[...])
-        grad_d = jnp.concatenate([depth_t[lanes], jnp.zeros((384, 256), f32)], axis=1)
-        pieces = [grad_q] + [grad_kvc[:, k * WIDTH : (k + 1) * WIDTH] for k in range(3)] + [grad_p, grad_d]
-        pieces = [x.reshape(16, 24, 384) for x in pieces]
-        for k in range(3):
-            units[group, k * 48 : k * 48 + 48, :] = jnp.concatenate(pieces[2 * k : 2 * k + 2], axis=1).astype(low_type)
-    small[...] = jnp.zeros_like(small)
-    small[0:72, :] = kernel_acc[...]
-    for k in range(4):
-        small[72 + k : 73 + k, :] = jnp.sum(sums[k], axis=0, keepdims=True)
-    column = jnp.concatenate([bias_acc[...], jnp.zeros((56, 128), f32)], axis=0)
-    small[76:77, 0:128] = jnp.sum(jnp.transpose(column), axis=0, keepdims=True)
-    for c in range(5, 8):
-        reducer.step(c, 0)
-    sum3[...] = small[...]
-    late.step(0)
 
     def finish(i, carry):
         rows = aligned(i * TILE, TILE)
         grad_own[rows, :] = input_part(b + i) + mm_nt(dq_low[rows, :], query_w[...]) + residual_grad[rows, :]
-        for n in range(3):
-            @pl.when(i == n)
-            def _():
-                for c in range(5, 8):
-                    reducer.step(c, n + 1)
-                late.step(n + 1)
         return carry
 
     lax.fori_loop(0, 3, finish, 0)
-    for s in range(4, nh + 1):
-        for c in range(5, 8):
+    for stage in range(2, 6):
+        late.step(stage)
+        run([(c, stage) for c in (5, 7, 6)])
+    for s in range(6, nh + 1):
+        for c in range(8):
             reducer.step(c, s)
-        late.step(s)
-    for s in range(8, bits + 1):
-        early.step(s)
-    for s in range(nh + 1, bits + 1):
+    for s in range(6, bits + 1):
         late.step(s)
     for k in range(extra):
         copy = reducer.copy(out, extra_got.at[k], extra_sem.at[2 * k], extra_sem.at[2 * k + 1], k)
@@ -744,7 +756,7 @@
 
 def back_call(dp_size, hidden, joined_grad, residual_grad, saved, units2, small2, weights):
     shape = jax.ShapeDtypeStruct
-    outs = (shape((768, D), f32), shape((256, D), low_type), shape((384, 384), f32), shape(small2.shape, f32), shape((96, 384), f32))
+    outs = (shape((768, D), f32), shape((256, D), low_type), shape((384, 384), f32), shape((104, 384), f32))
     operands = (hidden, joined_grad, residual_grad) + tuple(saved) + (units2, small2) + tuple(weights)
     ext = 1024 + 2 * PAD
     bits = int(math.log2(dp_size)) + 1
@@ -760,12 +772,11 @@
             pltpu.VMEM((TILE, KERNEL * 128), f32), pltpu.VMEM((KERNEL, 8, D), f32), pltpu.VMEM((WIDTH, TILE), f32),
             pltpu.VMEM((72, WIDTH), f32), pltpu.VMEM((72, 128), f32), pltpu.VMEM((1024, 72), low_type), pltpu.VMEM((TILE, D), f32),
             pltpu.VMEM((4, 8, WIDTH), f32),
-            pltpu.VMEM((256, D), low_type), pltpu.VMEM((32, 144, 384), low_type), pltpu.VMEM((96, 384), f32),
+            pltpu.VMEM((256, D), low_type), pltpu.VMEM((32, 144, 384), low_type),
             pltpu.VMEM((8, (1 << nh) - 1, CHUNK, 384), low_type),
-            pltpu.VMEM(small2.shape, f32), pltpu.VMEM((bits,) + small2.shape, f32),
-            pltpu.VMEM((96, 384), low_type), pltpu.VMEM((bits, 96, 384), low_type),
+            pltpu.VMEM((104, 384), low_type), pltpu.VMEM((bits, 104, 384), low_type),
             pltpu.VMEM((max(extra, 1), 384 if extra else 8, 384), f32),
-            dma((8, nh)), dma((8, nh)), dma((bits,)), dma((bits,)), dma((bits,)), dma((bits,)), dma((2,)), dma((max(2 * extra, 2),)),
+            dma((8, nh)), dma((8, nh)), dma((bits,)), dma((bits,)), dma((2,)), dma((max(2 * extra, 2),)),
             pltpu.VMEM((5, 1 << (nh - 1), CHUNK, 384), low_type), dma((5,)),
         ],
         compiler_params=pltpu.CompilerParams(collective_id=0, has_side_effects=True, vmem_limit_bytes=67_000_000),
@@ -778,13 +789,13 @@
 
 
 FINAL_SMALL = (
-    ("query_b", 72, 384), ("value_b", 73, 384), ("point_b", 74, 384), ("conv_b", 75, 384), ("out_b", 96, 768), ("gain1", 98, 768),
-    ("shift1", 100, 768), ("in_b", 102, 3072), ("ffo_b", 110, 768), ("gain2", 112, 768), ("shift2", 114, 768),
+    ("query_b", 72, 384), ("value_b", 73, 384), ("point_b", 74, 384), ("conv_b", 75, 384), ("out_b", 80, 768), ("gain1", 82, 768),
+    ("shift1", 84, 768), ("in_b", 86, 3072), ("ffo_b", 94, 768), ("gain2", 96, 768), ("shift2", 98, 768),
 )
 
 
 def final_kernel(
-    grad_own, got, total, small2, small3,
+    grad_own, got, total, small,
     input_grad, query_w, key_w, value_w, depth_w, point_w, kernel_w, kernel_b, conv_w, out_w, in_w, ffo_w, *vectors,
 ):
     b = lax.axis_index("branch")
@@ -802,11 +813,10 @@
     depth = jnp.concatenate([total[360:384, 0:128], jnp.zeros((104, 128), f32)], axis=0)
     depth_w[...] = jnp.transpose(depth)[0:KERNEL, 0:24]
     table = tap_permutation()
-    kernel_w[...] = exact_columns(table, small3[0:72, :])
-    column = jnp.transpose(jnp.concatenate([small3[76:77, 0:128]] * 128, axis=0))[0:72, :]
+    kernel_w[...] = exact_columns(table, small[0:72, :])
+    column = jnp.transpose(jnp.concatenate([small[76:77, 0:128]] * 128, axis=0))[0:72, :]
     kernel_b[...] = jnp.sum(column[:, 0:54] * table, axis=0, keepdims=True).reshape(54)
     for ref, (_, row, size) in zip(vectors, FINAL_SMALL):
-        small, row = (small3, row) if row < 96 else (small2, row - 96)
         ref[...] = jnp.concatenate([small[row + k : row + k + 1, :] for k in range(size // 384)], axis=1).reshape(size)
 
 
@@ -817,7 +827,7 @@
         shape(24, 384), shape(24, 768), shape(2, 48, 384), shape(2, 48, 384),
     ) + tuple(shape(size) for _, _, size in FINAL_SMALL)
     return pl.pallas_call(
-        final_kernel, out_shape=outs, in_specs=[VM] * 5, out_specs=(VM,) * len(outs),
+        final_kernel, out_shape=outs, in_specs=[VM] * 4, out_specs=(VM,) * len(outs),
         compiler_params=pltpu.CompilerParams(vmem_limit_bytes=32 << 20), name="finish",
     )(*operands)
 
@@ -839,7 +849,7 @@
         hidden, joined, cotangent, output_weight, ffn_in_weight, ffn_out_weight, output_bias, norm1_gain, norm1_shift,
         ffn_in_bias, ffn_out_bias, norm2_gain, norm2_shift,
     )
-    grad_own, got, out_sum, sum2, sum3 = back_call(
+    grad_own, got, out_sum, small_sum = back_call(
         dp_size, hidden, joined_grad, residual_grad, saved, units2, small2,
         (query_weight, key_weight, value_weight, pointwise_weight, conv_value_weight, depthwise_weight, kernel_rows),
     )
@@ -848,12 +858,11 @@
         (
             input_grad, query_w, key_w, value_w, depth_w, point_w, kernel_w, kernel_b, conv_w, out_w, in_w, ffo_w,
             query_b, value_b, point_b, conv_b, out_b, gain1, shift1, in_b, ffo_b, gain2, shift2,
-        ) = final_call(grad_own, got, out_sum, sum2, sum3)
+        ) = final_call(grad_own, got, out_sum, small_sum)
         return (
             layer_out, input_grad, query_w, query_b, key_w, value_w, value_b, depth_w, point_w, point_b, jnp.transpose(kernel_w),
             kernel_b, conv_w, conv_b, out_w, out_b, gain1, shift1, jnp.transpose(in_w, (0, 2, 1)), in_b, ffo_w, ffo_b, gain2, shift2,
         )
-    small_sum = jnp.concatenate([sum3, sum2])
     start = (1 - branch) * 512
     block = lax.dynamic_slice_in_dim(grad_own, start, 256, 0) + got.astype(f32)
     input_grad = lax.dynamic_update_slice_in_dim(grad_own, block, start, 0)
@@ -885,15 +894,15 @@
         piece(312, 24),
         small(75, 384),
         jnp.concatenate([piece(192, 24), piece(216, 24)], axis=1),
+        small(80, 768),
+        small(82, 768),
+        small(84, 768),
+        jnp.transpose(in_g, (0, 2, 1)),
+        small(86, 3072),
+        jnp.stack([piece(0, 48), piece(48, 48)]),
+        small(94, 768),
         small(96, 768),
         small(98, 768),
-        small(100, 768),
-        jnp.transpose(in_g, (0, 2, 1)),
-        small(102, 3072),
-        jnp.stack([piece(0, 48), piece(48, 48)]),
-        small(110, 768),
-        small(112, 768),
-        small(114, 768),
     )
 
 

time: 168 us -> 150 us (0.89)
  Pallas kernels: 162 us -> 144 us
    pallas_call x1, Pallas kernels: 95 us -> 77.6 us  [back_call(): pl.pallas_call(functools.partial(back_kernel, dp_size), out_shape=outs, i...]
    unnamed x10 -> x8, local copies, waits for them, and re-layouts: 5.42 us -> 4.63 us
where the time goes in v5:
time: 150 us
  Pallas kernels  144 us (96%)
  local copies, waits for them, and re-layouts  4.63 us (3%)
    pallas_call x1, Pallas kernels, back_call(): pl.pallas_call(functools.partial(back_kernel, dp_size), out_shape=outs, i...  77.6 us
    pallas_call x1, Pallas kernels, ffn_call(): pl.pallas_call(ffn_kernel, out_shape=outs, in_specs=[VM] * len(operands),...  38.9 us
    pallas_call x1, Pallas kernels, mix_call(): pl.pallas_call(mix_kernel, out_shape=outs, in_specs=[VM] * len(operands),...  25.8 us
    unnamed x8, local copies, waits for them, and re-layouts  4.63 us

profile of v5, /device:TPU:0, one launch (start us, length us, event | category | flops | bytes accessed | tf_op | source)
XLA Modules:
  0.0 149.7 jit_solution(7492535603310730459)
XLA Ops:
  0.7 25.8 %mix_forward.1 = (bf16[768,768]{1,0:T(8,128)(2,1)}, bf16[768,384]{1,0:T(8,128)(2,1)}, bf16[1024,384]{1,0:T(8,128)(2,1)}, bf16[1024,384]{1,0:T(8,128)(2,1)}, bf16...) custom-call(bf16[1536,768]{1,0:T(8,128)(2,1)} %hidden.5, ...), custom_call_target="tpu_custom_call" | custom-call | tf_op jit(solution)/shard_map/mix_forward/pallas_call | solution.py:241
  26.5 38.9 %ffn.1 = (bf16[768,768]{1,0:T(8,128)(2,1)}, f32[768,768]{1,0:T(8,128)}, bf16[768,768]{1,0:T(8,128)(2,1)}, bf16[32,240,384]{2,1,0:T(8,128)(2,1)}, f32[32,384]{1,0:T(8,128)}) custom-call(bf16[1536,768]{1,0:T(8,128)(2,1)} %hidden.5, bf16[768,768]{1,0:T(8,128)(2,1)} %get-tuple-element.68.joined, bf16[768,768]{1,0:T(8,128)(2,1)} %cotangent.1, ...), custom_call_target="tpu_custom_call" | custom-call | tf_op jit(solution)/shard_map/ffn/pallas_call | solution.py:383
  65.3 77.6 %mix_backward_reduce.1 = (f32[768,768]{1,0:T(8,128)}, bf16[256,768]{1,0:T(8,128)(2,1)}, f32[384,384]{1,0:T(8,128)}, f32[104,384]{1,0:T(8,128)}) custom-call(bf16[1536,768]{1,0:T(8,128)(2,1)} %hidden.5, bf16[768,768]{1,0:T(8,128)(2,1)} %get-tuple-element.70.joined_grad, f32[768,768]{1,0:T(8,128)} %get-tuple-element.71.residual_grad, ...), custom_call_target="tpu_custom_call" | custom-call | tf_op jit(solution)/shard_map/mix_backward_reduce/pallas_call | solution.py:766
  142.9 0.0 copy-start
  142.9 1.7 %copy-done = f32[768,768]{1,0:T(8,128)S(1)} copy-done((f32[768,768]{1,0:T(8,128)S(1)}, f32[768,768]{1,0:T(8,128)}, u32[]{:S(2)}) %copy-start) | copy-done | bytes 2359320
  144.6 0.0 copy-start.1
  144.6 1.1 copy-done.1
  145.6 0.0 copy-start.2
  145.6 1.0 copy-done.2
  146.6 0.0 copy-start.3
  146.6 0.9 copy-done.3
  147.6 2.0 %finish.1 = (f32[768,768]{1,0:T(8,128)}, f32[24,384]{1,0:T(8,128)}, f32[24,384]{1,0:T(8,128)}, f32[24,384]{1,0:T(8,128)}, f32[9,24]{1,0:T(8,128)}, /*index=5*/f3...) custom-call(f32[768,768]{1,0:T(8,128)S(1)} %copy-done, ...), custom_call_target="tpu_custom_call" | custom-call | tf_op jit(solution)/shard_map/finish/pallas_call | solution.py:829
Async XLA Ops:
  142.9 1.7 %copy-start = (f32[768,768]{1,0:T(8,128)S(1)}, f32[768,768]{1,0:T(8,128)}, u32[]{:S(2)}) copy-start(f32[768,768]{1,0:T(8,128)} %get-tuple-element.85.grad_own) | copy-start | bytes 7077892
  144.6 1.1 copy-start.1
  145.6 1.0 copy-start.2
  146.6 0.9 copy-start.3

commit v6 on v5

--- a/solution.py
+++ b/solution.py
@@ -135,7 +135,7 @@
 def mix_kernel(
     hidden, segments, query_w, key_w, value_w, point_w, conv_w, depth_w, kernel_w,
     vec0, vec1, vec2, vec3, vec4, joined, q_out, k_out, v_out, probs, conv_pad, taps_out, tap_mask, query_pre, key_conv, depth_low, conv_attn,
-    x_pad, v_t, ctx_t, bias, seg_rows, mask_cols, vecs,
+    x_pad, v_t, ctx_t, bias, seg_rows, mask_cols, vecs, probs_held, pad_held, out_sem,
 ):
     load_vecs(vecs, MIX_VECS, (vec0, vec1, vec2, vec3, vec4))
     b = lax.axis_index("branch")
@@ -155,8 +155,8 @@
         x_pad[c, 0:PAD, :] = jnp.zeros((PAD, 128), f32)
         x_pad[c, 1024 + PAD : 1024 + 2 * PAD, :] = jnp.zeros((PAD, 128), f32)
     for c in range(WIDTH // 128):
-        conv_pad[c, 0:PAD, :] = jnp.zeros((PAD, 128), f32)
-        conv_pad[c, 1024 + PAD : 1024 + 2 * PAD, :] = jnp.zeros((PAD, 128), f32)
+        pad_held[c, 0:PAD, :] = jnp.zeros((PAD, 128), f32)
+        pad_held[c, 1024 + PAD : 1024 + 2 * PAD, :] = jnp.zeros((PAD, 128), f32)
     taps_out[...] = jnp.zeros_like(taps_out)
 
     def project(e, carry):
@@ -169,15 +169,22 @@
         cv = mm(x, conv_w[...]) + vec(vecs, "conv_value_bias")
         place = pl.ds(pl.multiple_of(e * TILE + PAD, 8), TILE)
         for c in range(WIDTH // 128):
-            conv_pad[c, place, :] = cv[:, c * 128 : c * 128 + 128]
+            pad_held[c, place, :] = cv[:, c * 128 : c * 128 + 128]
         for c in range(D // 128):
             x_pad[c, place, :] = x[:, c * 128 : c * 128 + 128].astype(f32)
         return carry
 
-    lax.fori_loop(0, 4, project, 0)
+    lax.fori_loop(0, 4, project, 0, unroll=2)
     kernel_rows = mm(tap_permutation().astype(low_type), kernel_w[...]).astype(low_type)
     kernel_bias = jnp.sum(tap_permutation() * vec(vecs, "kernel_bias")[:, :54], axis=1, keepdims=True)
     depth_weights = [depth_w[j : j + 1, :].astype(f32) for j in range(KERNEL)]
+
+    def probs_copy(i):
+        heads = pl.ds(i * HEADS, HEADS)
+        return pltpu.make_async_copy(probs_held.at[heads], probs.at[heads], out_sem.at[i])
+
+    pad_copy = pltpu.make_async_copy(pad_held, conv_pad, out_sem.at[3])
+    pad_copy.start()
 
     def own(i, carry):
         e = b + i
@@ -202,8 +209,9 @@
             peak = jnp.max(scores, axis=0, keepdims=True)
             weight = jnp.exp(scores - peak)
             weight = (weight * (1.0 / jnp.sum(weight, axis=0, keepdims=True))).astype(low_type)
-            probs[i * HEADS + h] = weight
+            probs_held[i * HEADS + h] = weight
             ctx_t[h * HEAD_DIM : (h + 1) * HEAD_DIM, :] = mm(v_t[h * HEAD_DIM : (h + 1) * HEAD_DIM, keys], weight)
+        probs_copy(i).start()
         joined[rows, 0:WIDTH] = jnp.transpose(ctx_t[...]).astype(low_type)
 
         masks = tap_mask[:, ext]
@@ -220,14 +228,18 @@
         conv_attn[rows, :] = attn
         taps = taps_softmax(mm_nt(kernel_rows, attn) + kernel_bias)
         taps_out[:, ext] = taps
-        spread = span_conv(conv_pad, jnp.transpose(taps * masks).astype(low_type), e * TILE)
+        spread = span_conv(pad_held, jnp.transpose(taps * masks).astype(low_type), e * TILE)
         joined[rows, WIDTH : 2 * WIDTH] = spread.astype(low_type)
         return carry
 
     lax.fori_loop(0, 3, own, 0)
+    for i in range(3):
+        probs_copy(i).wait()
+    pad_copy.wait()
 
 
 VM = pl.BlockSpec(memory_space=pltpu.VMEM)
+ANY = pl.BlockSpec(memory_space=pl.ANY)
 
 
 def mix_call(*operands):
@@ -239,11 +251,12 @@
         shape((768, D), low_type), shape((768, WIDTH), low_type),
     )
     return pl.pallas_call(
-        mix_kernel, out_shape=outs, in_specs=[VM] * len(operands), out_specs=(VM,) * len(outs),
+        mix_kernel, out_shape=outs, in_specs=[VM] * len(operands), out_specs=(VM,) * 4 + (ANY,) * 2 + (VM,) * (len(outs) - 6),
         scratch_shapes=[
             pltpu.VMEM((6, 1024 + 2 * PAD, 128), f32), pltpu.VMEM((WIDTH, 1024), low_type),
             pltpu.VMEM((WIDTH, TILE), f32), pltpu.VMEM((512, TILE), f32), pltpu.VMEM((8, 512), f32),
             pltpu.VMEM((TILE, KERNEL * 128), f32), pltpu.VMEM((1, VEC_TOTAL), f32),
+            pltpu.VMEM((18, 512, TILE), low_type), pltpu.VMEM((3, 1024 + 2 * PAD, 128), f32), pltpu.SemaphoreType.DMA((4,)),
         ],
         compiler_params=pltpu.CompilerParams(vmem_limit_bytes=60 << 20),
         name="mix_forward",
@@ -308,7 +321,7 @@
             total[:, lanes] += mm(act, ffo_w[g, pl.ds(pl.multiple_of(part * 768, 128), 768), :])
             return carry
 
-        lax.fori_loop(0, 4, forward, 0)
+        lax.fori_loop(0, 4, forward, 0, unroll=True)
         n2, scale2 = normalize(total[...])
         layer_out[rows, :] = (n2 * vec(vecs, "norm2_gain") + vec(vecs, "norm2_shift")).astype(low_type)
         grad = cotangent[rows, :].astype(f32)
@@ -332,7 +345,7 @@
             total[:, lanes] += mm_nt(grad_low, in_w[g, :, wide])
             return carry
 
-        lax.fori_loop(0, 4, backward, 0)
+        lax.fori_loop(0, 4, backward, 0, unroll=True)
         normed_grad = total[...]
         n1 = unit1[...]
         sums[1] += fold_rows(normed_grad * n1)
@@ -359,7 +372,7 @@
             units[group, 96 + g * 48 : 144 + g * 48, :] = grad_in.reshape(8, 48, 384).astype(low_type)
             return carry
 
-        lax.fori_loop(0, 4, weights, 0)
+        lax.fori_loop(0, 4, weights, 0, unroll=2)
     for m in range(2):
         grad_w = mm_tn(joined[:, m * 384 : m * 384 + 384], attn_low[...])
         halves = [grad_w[:, :384].reshape(16, 24, 384), grad_w[:, 384:].reshape(16, 24, 384)]
@@ -483,11 +496,11 @@
                 mine = ref[at, row : row + CHUNK, :]
             else:
                 mine = self.buffer[c, self.offset(s - 1) + at]
-            total = mine.astype(f32) + self.buffer[c, self.offset(s) + u].astype(f32)
+            theirs = self.buffer[c, self.offset(s) + u]
             if s == self.nh - 1:
-                self.out[c * CHUNK : (c + 1) * CHUNK, :] = total
+                self.out[c * CHUNK : (c + 1) * CHUNK, :] = mine.astype(f32) + theirs.astype(f32)
             else:
-                self.buffer[c, self.offset(s) + u] = total.astype(low_type)
+                self.buffer[c, self.offset(s) + u] = mine + theirs
 
     def step(self, c, s):
         if s > 0:
@@ -523,21 +536,40 @@
     (0, 1): [(0, 1), (1, 1)],
     (0, 2): [(2, 1), (3, 1)],
     (0, 3): [(4, 1)],
-    (1, 1): [(0, 2), (1, 2)],
-    (1, 3): [(2, 2), (3, 2), (4, 2)],
-    (2, 2): [(0, 3), (1, 3), (4, 3)],
-    (2, 3): [(0, 4), (1, 4), (4, 4)],
+    (1, 2): [(0, 2), (1, 2)],
+    (2, 1): [(2, 2), (3, 2), (4, 2)],
+    (2, 3): [(0, 3), (1, 3)],
 }
 
 
 def back_kernel(
-    dp_size, hidden, joined_grad, residual_grad, q_in, k_in, v_in, probs, conv_pad, taps, tap_mask, query_pre, key_conv, depth_low,
-    conv_attn, units2, small2, query_w, key_w, value_w, point_w, conv_w, depth_w, kernel_w,
+    dp_size, hidden_far, joined_grad_far, residual_grad_far, q_in_far, k_in_far, v_in_far, probs_far, conv_pad_far, taps, tap_mask, query_pre_far, key_conv_far, depth_low_far,
+    conv_attn_far, units2, small2, query_w_far, key_w_far, value_w_far, point_w_far, conv_w_far, depth_w, kernel_w,
     grad_own, got_other, out, small_sum,
     dk_acc, dv_acc, k_t, dq_low, kvc, key_conv_low, dg_pad, cg_pad, x_pad, mask_cols, dw_acc, dq_t, kernel_acc, bias_acc, moved_taps, part,
     sums, grad_other, units, buffer, sent3, got3, extra_got,
     send, recv, send3, recv3, other_sem, extra_sem, kept, kept_sem,
+    hidden, joined_grad, residual_grad, q_in, k_in, v_in, probs, conv_pad, query_pre, key_conv, depth_low, conv_attn,
+    query_w, key_w, value_w, point_w, conv_w, load_sem, probs_sem,
 ):
+    order = (
+        (hidden_far, hidden), (k_in_far, k_in), (joined_grad_far, joined_grad), (q_in_far, q_in), (v_in_far, v_in),
+        (conv_pad_far, conv_pad), (conv_attn_far, conv_attn), (query_pre_far, query_pre), (key_conv_far, key_conv), (point_w_far, point_w),
+        (depth_low_far, depth_low), (key_w_far, key_w), (value_w_far, value_w), (conv_w_far, conv_w), (query_w_far, query_w),
+        (residual_grad_far, residual_grad),
+    )
+    loads = [pltpu.make_async_copy(away, near, load_sem.at[n]) for n, (away, near) in enumerate(order)]
+
+    def probs_load(i):
+        heads = pl.ds(i * HEADS, HEADS)
+        return pltpu.make_async_copy(probs_far.at[heads], probs.at[heads], probs_sem.at[i])
+
+    for load in loads[:5]:
+        load.start()
+    for i in range(3):
+        probs_load(i).start()
+    for load in loads[5:]:
+        load.start()
     reducer = Reducer(dp_size, (units2, units), kept, kept_sem, buffer, out, send, recv)
     nh, bits, extra = reducer.nh, reducer.bits, reducer.extra
     late = Doubler(reducer, small_sum, sent3, got3, send3, recv3)
@@ -575,6 +607,8 @@
             x_pad[c, place, :] = x[:, c * 128 : c * 128 + 128].astype(f32)
         return carry
 
+    for load in loads[:2]:
+        load.wait()
     lax.fori_loop(0, 4, prepare, 0)
     kernel_rows = mm(tap_permutation().astype(low_type), kernel_w[...]).astype(low_type)
     depth_weights = [depth_w[j : j + 1, :].astype(f32) for j in range(KERNEL)]
@@ -592,6 +626,7 @@
         ext = aligned(e * TILE, TILE)
         place = pl.ds(pl.multiple_of(e * TILE + PAD, 8), TILE)
         keys = aligned(lax.div(e, 2) * 512, 512)
+        probs_load(i).wait()
         d_ctx = joined_grad[rows, 0:WIDTH]
         d_ctx_t = jnp.transpose(d_ctx.astype(f32)).astype(low_type)
         for p in range(HEADS // 2):
@@ -661,7 +696,11 @@
         advance_at(i, 3)
         return carry
 
+    for load in loads[2:10]:
+        load.wait()
     lax.fori_loop(0, 3, own, 0)
+    for load in loads[10:]:
+        load.wait()
 
     def settle(e, carry):
         ext = aligned(e * TILE, TILE)
@@ -685,7 +724,7 @@
     lax.fori_loop(0, 4, settle, 0)
     own_tokens = pl.ds(pl.multiple_of(b * 768, 256), 768)
     pack(0, lambda lanes: mm_tn(hidden[own_tokens, lanes], dq_low[...]), token_grad(0))
-    run([(5, 0), (2, 3), (3, 3)])
+    run([(5, 0), (4, 3)])
     depth_total = jnp.sum(dw_acc[...], axis=1)
     depth_t = jnp.transpose(jnp.concatenate([depth_total, jnp.zeros((128 - KERNEL, D), f32)], axis=0))
     pack(
@@ -693,7 +732,7 @@
         lambda lanes: mm_tn(depth_low[:, lanes], key_conv_low[...]),
         lambda lanes: jnp.concatenate([depth_t[lanes], jnp.zeros((384, 256), f32)], axis=1),
     )
-    run([(7, 0)])
+    run([(7, 0), (2, 3), (3, 3), (0, 4), (1, 4)])
 
     def spans(e, carry):
         ext = aligned(e * TILE, TILE)
@@ -702,8 +741,8 @@
         sums[3] += fold_rows(dc.astype(f32))
         return carry
 
-    lax.fori_loop(0, 4, spans, 0)
-    run([(2, 4), (3, 4), (0, 5), (1, 5), (4, 5)])
+    lax.fori_loop(0, 4, spans, 0, unroll=2)
+    run([(4, 4), (2, 4), (3, 4)])
     small_sum[...] = jnp.zeros_like(small_sum)
     small_sum[0:72, :] = kernel_acc[...]
     for k in range(4):
@@ -728,7 +767,7 @@
         return part[...] + mm_nt(pieces[0], key_w[...]) + mm_nt(pieces[1], value_w[...]) + mm_nt(pieces[2], conv_w[...])
 
     grad_other[...] = input_part(3 * (1 - b)).astype(low_type)
-    run([(6, 1), (2, 5), (3, 5)])
+    run([(6, 1), (0, 5), (1, 5), (4, 5), (2, 5), (3, 5)])
     other_copy.start()
 
     def finish(i, carry):
@@ -764,7 +803,7 @@
     nh = bits - extra
     dma = pltpu.SemaphoreType.DMA
     return pl.pallas_call(
-        functools.partial(back_kernel, dp_size), out_shape=outs, in_specs=[VM] * 14 + [pl.BlockSpec(memory_space=pl.ANY)] + [VM] * (len(operands) - 15), out_specs=(VM,) * len(outs),
+        functools.partial(back_kernel, dp_size), out_shape=outs, in_specs=[ANY] * 8 + [VM] * 2 + [ANY] * 5 + [VM] + [ANY] * 5 + [VM] * 2, out_specs=(VM,) * len(outs),
         scratch_shapes=[
             pltpu.VMEM((1024, WIDTH), f32), pltpu.VMEM((1024, WIDTH), f32), pltpu.VMEM((WIDTH, 1024), low_type),
             pltpu.VMEM((768, WIDTH), low_type), pltpu.VMEM((1024, 3 * WIDTH), low_type), pltpu.VMEM((768, WIDTH), low_type),
@@ -778,6 +817,8 @@
             pltpu.VMEM((max(extra, 1), 384 if extra else 8, 384), f32),
             dma((8, nh)), dma((8, nh)), dma((bits,)), dma((bits,)), dma((2,)), dma((max(2 * extra, 2),)),
             pltpu.VMEM((5, 1 << (nh - 1), CHUNK, 384), low_type), dma((5,)),
+        ] + [pltpu.VMEM(operands[n].shape, operands[n].dtype) for n in (0, 1, 2, 3, 4, 5, 6, 7, 10, 11, 12, 13, 16, 17, 18, 19, 20)] + [
+            dma((16,)), dma((3,)),
         ],
         compiler_params=pltpu.CompilerParams(collective_id=0, has_side_effects=True, vmem_limit_bytes=67_000_000),
         name="mix_backward_reduce",

time: 150 us -> 138 us (0.920)
  Pallas kernels: 144 us -> 132 us
    pallas_call x1, Pallas kernels: 38.9 us -> 31.9 us  [ffn_call(): pl.pallas_call(ffn_kernel, out_shape=outs, in_specs=[VM] * len(operands),...]
    pallas_call x1, Pallas kernels: 77.6 us -> 72.8 us  [back_call(): pl.pallas_call(functools.partial(back_kernel, dp_size), out_shape=outs, i...]
where the time goes in v6:
time: 138 us; the launch traced here: 137 us
  Pallas kernels  132 us (96%)
  local copies, waits for them, and re-layouts  4.63 us (3%)
    pallas_call x1, Pallas kernels, back_call(): pl.pallas_call(functools.partial(back_kernel, dp_size), out_shape=outs, i...  72.8 us
    pallas_call x1, Pallas kernels, ffn_call(): pl.pallas_call(ffn_kernel, out_shape=outs, in_specs=[VM] * len(operands),...  31.9 us
    pallas_call x1, Pallas kernels, mix_call(): pl.pallas_call(mix_kernel, out_shape=outs, in_specs=[VM] * len(operands),...  25.2 us
    unnamed x8, local copies, waits for them, and re-layouts  4.63 us

profile of v6, /device:TPU:0, one launch (start us, length us, event | category | flops | bytes accessed | tf_op | source)
XLA Modules:
  0.0 137.3 jit_solution(13724851054879232411)
XLA Ops:
  0.7 25.2 %mix_forward.1 = (bf16[768,768]{1,0:T(8,128)(2,1)}, bf16[768,384]{1,0:T(8,128)(2,1)}, bf16[1024,384]{1,0:T(8,128)(2,1)}, bf16[1024,384]{1,0:T(8,128)(2,1)}, bf16...) custom-call(bf16[1536,768]{1,0:T(8,128)(2,1)} %hidden_far.1, ...), custom_call_target="tpu_custom_call" | custom-call | tf_op jit(solution)/shard_map/mix_forward/pallas_call | solution.py:253
  25.9 31.9 %ffn.1 = (bf16[768,768]{1,0:T(8,128)(2,1)}, f32[768,768]{1,0:T(8,128)}, bf16[768,768]{1,0:T(8,128)(2,1)}, bf16[32,240,384]{2,1,0:T(8,128)(2,1)}, f32[32,384]{1,0:T(8,128)}) custom-call(bf16[1536,768]{1,0:T(8,128)(2,1)} %hidden_far.1, bf16[768,768]{1,0:T(8,128)(2,1)} %get-tuple-element.68.joined, bf16[768,768]{1,0:T(8,128)(2,1)} %cotangent.1, ...), custom_call_target="tpu_custom_call" | custom-call | tf_op jit(solution)/shard_map/ffn/pallas_call | solution.py:396
  57.7 72.8 %mix_backward_reduce.1 = (f32[768,768]{1,0:T(8,128)}, bf16[256,768]{1,0:T(8,128)(2,1)}, f32[384,384]{1,0:T(8,128)}, f32[104,384]{1,0:T(8,128)}) custom-call(bf16[1536,768]{1,0:T(8,128)(2,1)} %hidden_far.1, bf16[768,768]{1,0:T(8,128)(2,1)} %get-tuple-element.70.joined_grad_far, f32[768,768]{1,0:T(8,128)} %get-tuple-element.71.residual_grad_far, ...), custom_call_target="tpu_custom_call" | custom-call | tf_op jit(solution)/shard_map/mix_backward_reduce/pallas_call | solution.py:805
  130.5 0.0 copy-start
  130.6 1.7 %copy-done = f32[768,768]{1,0:T(8,128)S(1)} copy-done((f32[768,768]{1,0:T(8,128)S(1)}, f32[768,768]{1,0:T(8,128)}, u32[]{:S(2)}) %copy-start) | copy-done | bytes 2359320
  132.2 0.0 copy-start.1
  132.2 1.1 copy-done.1
  133.3 0.0 copy-start.2
  133.3 1.0 copy-done.2
  134.3 0.0 copy-start.3
  134.3 0.9 copy-done.3
  135.2 2.0 %finish.1 = (f32[768,768]{1,0:T(8,128)}, f32[24,384]{1,0:T(8,128)}, f32[24,384]{1,0:T(8,128)}, f32[24,384]{1,0:T(8,128)}, f32[9,24]{1,0:T(8,128)}, /*index=5*/f3...) custom-call(f32[768,768]{1,0:T(8,128)S(1)} %copy-done, ...), custom_call_target="tpu_custom_call" | custom-call | tf_op jit(solution)/shard_map/finish/pallas_call | solution.py:870
Async XLA Ops:
  130.5 1.7 %copy-start = (f32[768,768]{1,0:T(8,128)S(1)}, f32[768,768]{1,0:T(8,128)}, u32[]{:S(2)}) copy-start(f32[768,768]{1,0:T(8,128)} %get-tuple-element.85.grad_own) | copy-start | bytes 7077892
  132.2 1.1 copy-start.1
  133.3 1.0 copy-start.2
  134.3 0.9 copy-start.3

commit v7 on v6

--- a/solution.py
+++ b/solution.py
@@ -772,11 +772,16 @@
 
     def finish(i, carry):
         rows = aligned(i * TILE, TILE)
+        @pl.when(i == 2)
+        def _():
+            late.step(2)
+            run([(c, 2) for c in (5, 7, 6)])
+
         grad_own[rows, :] = input_part(b + i) + mm_nt(dq_low[rows, :], query_w[...]) + residual_grad[rows, :]
         return carry
 
     lax.fori_loop(0, 3, finish, 0)
-    for stage in range(2, 6):
+    for stage in range(3, 6):
         late.step(stage)
         run([(c, stage) for c in (5, 7, 6)])
     for s in range(6, nh + 1):

time: 138 us -> 136 us (0.986)
  no operation moved by 1% of the time
where the time goes in v7:
time: 136 us
  Pallas kernels  131 us (96%)
  local copies, waits for them, and re-layouts  4.63 us (3%)
    pallas_call x1, Pallas kernels, back_call(): pl.pallas_call(functools.partial(back_kernel, dp_size), out_shape=outs, i...  71.7 us
    pallas_call x1, Pallas kernels, ffn_call(): pl.pallas_call(ffn_kernel, out_shape=outs, in_specs=[VM] * len(operands),...  31.9 us
    pallas_call x1, Pallas kernels, mix_call(): pl.pallas_call(mix_kernel, out_shape=outs, in_specs=[VM] * len(operands),...  25.2 us
    unnamed x8, local copies, waits for them, and re-layouts  4.63 us

profile of v7, /device:TPU:0, one launch (start us, length us, event | category | flops | bytes accessed | tf_op | source)
XLA Modules:
  0.0 136.2 jit_solution(5018343800809596827)
XLA Ops:
  0.7 25.2 %mix_forward.1 = (bf16[768,768]{1,0:T(8,128)(2,1)}, bf16[768,384]{1,0:T(8,128)(2,1)}, bf16[1024,384]{1,0:T(8,128)(2,1)}, bf16[1024,384]{1,0:T(8,128)(2,1)}, bf16...) custom-call(bf16[1536,768]{1,0:T(8,128)(2,1)} %hidden_far.1, ...), custom_call_target="tpu_custom_call" | custom-call | tf_op jit(solution)/shard_map/mix_forward/pallas_call | solution.py:253
  25.9 31.9 %ffn.1 = (bf16[768,768]{1,0:T(8,128)(2,1)}, f32[768,768]{1,0:T(8,128)}, bf16[768,768]{1,0:T(8,128)(2,1)}, bf16[32,240,384]{2,1,0:T(8,128)(2,1)}, f32[32,384]{1,0:T(8,128)}) custom-call(bf16[1536,768]{1,0:T(8,128)(2,1)} %hidden_far.1, bf16[768,768]{1,0:T(8,128)(2,1)} %get-tuple-element.68.joined, bf16[768,768]{1,0:T(8,128)(2,1)} %cotangent.1, ...), custom_call_target="tpu_custom_call" | custom-call | tf_op jit(solution)/shard_map/ffn/pallas_call | solution.py:396
  57.7 71.7 %mix_backward_reduce.1 = (f32[768,768]{1,0:T(8,128)}, bf16[256,768]{1,0:T(8,128)(2,1)}, f32[384,384]{1,0:T(8,128)}, f32[104,384]{1,0:T(8,128)}) custom-call(bf16[1536,768]{1,0:T(8,128)(2,1)} %hidden_far.1, bf16[768,768]{1,0:T(8,128)(2,1)} %get-tuple-element.70.joined_grad_far, f32[768,768]{1,0:T(8,128)} %get-tuple-element.71.residual_grad_far, ...), custom_call_target="tpu_custom_call" | custom-call | tf_op jit(solution)/shard_map/mix_backward_reduce/pallas_call | solution.py:810
  129.4 0.0 copy-start
  129.4 1.7 %copy-done = f32[768,768]{1,0:T(8,128)S(1)} copy-done((f32[768,768]{1,0:T(8,128)S(1)}, f32[768,768]{1,0:T(8,128)}, u32[]{:S(2)}) %copy-start) | copy-done | bytes 2359320
  131.1 0.0 copy-start.1
  131.1 1.1 copy-done.1
  132.2 0.0 copy-start.2
  132.2 1.0 copy-done.2
  133.2 0.0 copy-start.3
  133.2 0.9 copy-done.3
  134.1 2.0 %finish.1 = (f32[768,768]{1,0:T(8,128)}, f32[24,384]{1,0:T(8,128)}, f32[24,384]{1,0:T(8,128)}, f32[24,384]{1,0:T(8,128)}, f32[9,24]{1,0:T(8,128)}, /*index=5*/f3...) custom-call(f32[768,768]{1,0:T(8,128)S(1)} %copy-done, ...), custom_call_target="tpu_custom_call" | custom-call | tf_op jit(solution)/shard_map/finish/pallas_call | solution.py:875
Async XLA Ops:
  129.4 1.7 %copy-start = (f32[768,768]{1,0:T(8,128)S(1)}, f32[768,768]{1,0:T(8,128)}, u32[]{:S(2)}) copy-start(f32[768,768]{1,0:T(8,128)} %get-tuple-element.85.grad_own) | copy-start | bytes 7077892
  131.1 1.1 copy-start.1
  132.2 1.0 copy-start.2
  133.2 0.9 copy-start.3
